TPU v7x, 32 devices: a whole 2x2x4 slice. The times are simulated.
32 devices in a mesh: dp: 4 (over x, core), fsdp: 8 (over z, y).
Axes of the slice: x: 2, y: 2, z: 4, core: 2. Of those that a mesh axis runs over, the one named last changes fastest.
Arguments:
- tokens: bfloat16 [32768, 1024], P(('dp', 'fsdp')), may hold values from -6 to 6
- first_values: bfloat16 [32768, 1024], P(('dp', 'fsdp')), may hold values from -6 to 6
- cotangent: bfloat16 [32768, 1024], P(('dp', 'fsdp')), may hold values from -6 to 6
- lengths: int32 [64, 8], P(('dp', 'fsdp')), may hold values from 0 to 512, as said below
- w_query: bfloat16 [1024, 1024], P(('dp', 'fsdp')), may hold values from -0.1875 to 0.1875
- w_key: bfloat16 [1024, 1024], P(('dp', 'fsdp')), may hold values from -0.1875 to 0.1875
- w_value: bfloat16 [1024, 1024], P(('dp', 'fsdp')), may hold values from -0.1875 to 0.1875
- w_out: bfloat16 [1024, 1024], P(('dp', 'fsdp')), may hold values from -0.75 to 0.75
- w_gate: bfloat16 [1024, 2816], P(('dp', 'fsdp')), may hold values from -0.1875 to 0.1875
- w_up: bfloat16 [1024, 2816], P(('dp', 'fsdp')), may hold values from -0.1875 to 0.1875
- w_down: bfloat16 [2816, 1024], P(('dp', 'fsdp')), may hold values from -0.109375 to 0.109375
- gain_one: bfloat16 [1024], P(('dp', 'fsdp')), may hold values from 0.5 to 1.5
- gain_two: bfloat16 [1024], P(('dp', 'fsdp')), may hold values from 0.5 to 1.5
Outputs:
- out_tokens: bfloat16 [32768, 1024], P(('dp', 'fsdp'))
- grad_tokens: float32 [32768, 1024], P(('dp', 'fsdp'))
- grad_first_values: float32 [32768, 1024], P(('dp', 'fsdp'))
- grad_query: float32 [1024, 1024], P(('dp', 'fsdp'))
- grad_key: float32 [1024, 1024], P(('dp', 'fsdp'))
- grad_value: float32 [1024, 1024], P(('dp', 'fsdp'))
- grad_out: float32 [1024, 1024], P(('dp', 'fsdp'))
- grad_gate: float32 [1024, 2816], P(('dp', 'fsdp'))
- grad_up: float32 [1024, 2816], P(('dp', 'fsdp'))
- grad_down: float32 [2816, 1024], P(('dp', 'fsdp'))
- grad_gain_one: float32 [1024], P(('dp', 'fsdp'))
- grad_gain_two: float32 [1024], P(('dp', 'fsdp'))
Inputs may be any that keep to these rules, and one draw needn't show every extreme that they name: Row b lists the lengths of the sequences of bucket b, laid one after another from the bucket's first slot; 0 marks no sequence; a row adds up to at most 512, and the slots after its total are padding; bucket 0 holds one sequence of 512 tokens. Bucket b is micro-batch b % 2 of the device that holds its slots.
All inputs are finite; a program needn't handle non-finite values.
Results may differ from a plain program's by a relative error of at most 0.014.
Values may be sent and summed in bfloat16 or wider, within the bound.
No kernel may reach another device: no remote copies, remote signals or barrier semaphores. Data moves between devices by JAX's collectives and lax.ppermute only.
A program may use at most 256 MiB of HBM per device.

v0:
```python
import math

import jax
import jax.numpy as jnp
from jax import lax
from jax.sharding import PartitionSpec as P

HEADS = 16


EPSILON = 1e-06


def forward_dot(left, right):
    return jnp.dot(left, right, preferred_element_type=jnp.float32)


def contract_last(left, right):
    return lax.dot_general(
        left, right, (((1,), (1,)), ((), ())), preferred_element_type=jnp.float32
    )


def contract_first(left, right):
    return lax.dot_general(
        left, right, (((0,), (0,)), ((), ())), preferred_element_type=jnp.float32
    )


def bucket_layout(lengths_row, slot_count):
    seq_ends = jnp.cumsum(lengths_row)
    slot_places = jnp.arange(slot_count, dtype=jnp.int32)
    ended_mask = seq_ends[None, :] <= slot_places[:, None]
    segment = jnp.sum(ended_mask.astype(jnp.int32), axis=1)
    before_total = jnp.sum(jnp.where(ended_mask, lengths_row[None, :], 0), axis=1)
    return (segment, slot_places - before_total, slot_places < seq_ends[-1])


def rope_tables(position, head_size):
    half_size = head_size // 2
    frequency = jnp.exp(
        jnp.arange(half_size, dtype=jnp.float32) * (-2.0 * math.log(10000.0) / head_size)
    )
    angles = position.astype(jnp.float32)[:, None] * frequency[None, :]
    return (jnp.cos(angles), jnp.sin(angles))


def rotate(matrix, cosine, sine, head_count):
    row_count = matrix.shape[0]
    halves = matrix.reshape(row_count, head_count, 2, -1)
    first_half = halves[:, :, 0]
    second_half = halves[:, :, 1]
    cos_table = cosine[:, None, :]
    sin_table = sine[:, None, :]
    turned = jnp.stack(
        [
            first_half * cos_table - second_half * sin_table,
            second_half * cos_table + first_half * sin_table,
        ],
        axis=2,
    )
    return turned.reshape(row_count, -1)


def allowed_mask(segment, valid):
    slot_places = jnp.arange(segment.shape[0])
    earlier = slot_places[None, :] < slot_places[:, None]
    same_seq = segment[:, None] == segment[None, :]
    diagonal = slot_places[None, :] == slot_places[:, None]
    return diagonal | same_seq & earlier & valid[:, None]


def rms_scale(matrix):
    return lax.rsqrt(jnp.mean(matrix * matrix, axis=-1, keepdims=True) + EPSILON)


def masked_scores(query_heads, key_heads, allowed, score_scale):
    raw_scores = (
        jnp.einsum("qhd,khd->hqk", query_heads, key_heads, preferred_element_type=jnp.float32)
        * score_scale
    )
    return jnp.where(allowed[None], raw_scores, -1e30)


def shards(
    tokens,
    first_values,
    cotangent,
    lengths,
    w_query,
    w_key,
    w_value,
    w_out,
    w_gate,
    w_up,
    w_down,
    gain_one,
    gain_two,
):
    micro_count = lengths.shape[0]
    slot_count = tokens.shape[0] // micro_count
    model_width = tokens.shape[1]
    head_count = HEADS
    head_size = model_width // head_count
    group_heads = 4
    group_count = head_count // group_heads
    score_scale = head_size ** (-0.5)
    out_rows = []
    grad_token_rows = []
    grad_first_rows = []
    running = None
    for micro_index in range(micro_count):
        row_start = micro_index * slot_count
        inputs = tokens[row_start : row_start + slot_count].astype(jnp.float32)
        first_input = first_values[row_start : row_start + slot_count].astype(jnp.float32)
        segment, position, valid = bucket_layout(lengths[micro_index], slot_count)
        cosine, sine = rope_tables(position, head_size)
        allowed = allowed_mask(segment, valid)
        forward_set = (
            lax.all_gather(w_query, ("dp", "fsdp"), axis=0, tiled=True),
            lax.all_gather(w_key, ("dp", "fsdp"), axis=0, tiled=True),
            lax.all_gather(w_value, ("dp", "fsdp"), axis=0, tiled=True),
            lax.all_gather(w_out, ("dp", "fsdp"), axis=0, tiled=True),
            lax.all_gather(w_gate, ("dp", "fsdp"), axis=0, tiled=True),
            lax.all_gather(w_up, ("dp", "fsdp"), axis=0, tiled=True),
            lax.all_gather(w_down, ("dp", "fsdp"), axis=0, tiled=True),
            lax.all_gather(gain_one, ("dp", "fsdp"), axis=0, tiled=True),
            lax.all_gather(gain_two, ("dp", "fsdp"), axis=0, tiled=True),
        )
        query_w, key_w, value_w, out_w, gate_w, up_w, down_w, gain_first, gain_second = forward_set
        gain_first_f = gain_first.astype(jnp.float32)
        gain_second_f = gain_second.astype(jnp.float32)
        scale_one = rms_scale(inputs)
        normed = (inputs * scale_one * gain_first_f).astype(jnp.bfloat16)
        query_rot = rotate(forward_dot(normed, query_w), cosine, sine, head_count).astype(
            jnp.bfloat16
        )
        key_rot = rotate(forward_dot(normed, key_w), cosine, sine, head_count).astype(jnp.bfloat16)
        value_mix = (0.5 * forward_dot(normed, value_w) + 0.5 * first_input).astype(jnp.bfloat16)
        query_heads = query_rot.reshape(slot_count, head_count, head_size)
        key_heads = key_rot.reshape(slot_count, head_count, head_size)
        value_heads = value_mix.reshape(slot_count, head_count, head_size)
        context_parts = []
        log_masses = []
        for group_index in range(group_count):
            head_lo = group_index * group_heads
            head_hi = head_lo + group_heads
            scores = masked_scores(
                query_heads[:, head_lo:head_hi], key_heads[:, head_lo:head_hi], allowed, score_scale
            )
            top_score = jnp.max(scores, axis=-1, keepdims=True)
            exp_scores = jnp.exp(scores - top_score)
            total_mass = jnp.sum(exp_scores, axis=-1, keepdims=True)
            prob_low = (exp_scores / total_mass).astype(jnp.bfloat16)
            log_masses.append(top_score + jnp.log(total_mass))
            context_parts.append(
                jnp.einsum(
                    "hqk,khd->qhd",
                    prob_low,
                    value_heads[:, head_lo:head_hi],
                    preferred_element_type=jnp.float32,
                )
            )
        context = (
            jnp.concatenate(context_parts, axis=1)
            .reshape(slot_count, model_width)
            .astype(jnp.bfloat16)
        )
        hidden = inputs + forward_dot(context, out_w)
        scale_two = rms_scale(hidden)
        normed_two = (hidden * scale_two * gain_second_f).astype(jnp.bfloat16)
        gate_values = forward_dot(normed_two, gate_w)
        upward = forward_dot(normed_two, up_w)
        sigmoid_gate = jax.nn.sigmoid(gate_values)
        silu_gate = gate_values * sigmoid_gate
        product = (silu_gate * upward).astype(jnp.bfloat16)
        out_rows.append((hidden + forward_dot(product, down_w)).astype(jnp.bfloat16))
        backward_set = (
            lax.all_gather(w_query, ("dp", "fsdp"), axis=0, tiled=True),
            lax.all_gather(w_key, ("dp", "fsdp"), axis=0, tiled=True),
            lax.all_gather(w_value, ("dp", "fsdp"), axis=0, tiled=True),
            lax.all_gather(w_out, ("dp", "fsdp"), axis=0, tiled=True),
            lax.all_gather(w_gate, ("dp", "fsdp"), axis=0, tiled=True),
            lax.all_gather(w_up, ("dp", "fsdp"), axis=0, tiled=True),
            lax.all_gather(w_down, ("dp", "fsdp"), axis=0, tiled=True),
            lax.all_gather(gain_one, ("dp", "fsdp"), axis=0, tiled=True),
            lax.all_gather(gain_two, ("dp", "fsdp"), axis=0, tiled=True),
        )
        query_b, key_b, value_b, out_b, gate_b, up_b, down_b, gain_first_b, gain_second_b = (
            backward_set
        )
        gain_first_g = gain_first_b.astype(jnp.float32)
        gain_second_g = gain_second_b.astype(jnp.float32)
        grad_y = (
            cotangent[row_start : row_start + slot_count].astype(jnp.float32)
            * valid.astype(jnp.float32)[:, None]
        )
        grad_y_low = grad_y.astype(jnp.bfloat16)
        grad_product = contract_last(grad_y_low, down_b)
        grad_down_w = contract_first(product, grad_y_low)
        grad_upward = (grad_product * silu_gate).astype(jnp.bfloat16)
        grad_gate_low = (
            grad_product * upward * sigmoid_gate * (1.0 + gate_values * (1.0 - sigmoid_gate))
        ).astype(jnp.bfloat16)
        grad_gate_w = contract_first(normed_two, grad_gate_low)
        grad_up_w = contract_first(normed_two, grad_upward)
        grad_normed_two = contract_last(grad_gate_low, gate_b) + contract_last(grad_upward, up_b)
        grad_gain_second = jnp.sum(grad_normed_two * hidden * scale_two, axis=0)
        inner_two = grad_normed_two * gain_second_g
        grad_hidden = (
            grad_y
            + scale_two * inner_two
            - hidden * scale_two**3 * jnp.mean(inner_two * hidden, axis=-1, keepdims=True)
        )
        grad_hidden_low = grad_hidden.astype(jnp.bfloat16)
        grad_out_w = contract_first(context, grad_hidden_low)
        grad_context = contract_last(grad_hidden_low, out_b).astype(jnp.bfloat16)
        grad_context_heads = grad_context.reshape(slot_count, head_count, head_size)
        value_grad_parts = []
        query_grad_parts = []
        key_grad_parts = []
        for group_index in range(group_count):
            head_lo = group_index * group_heads
            head_hi = head_lo + group_heads
            query_part = query_heads[:, head_lo:head_hi]
            key_part = key_heads[:, head_lo:head_hi]
            value_part = value_heads[:, head_lo:head_hi]
            context_grad_part = grad_context_heads[:, head_lo:head_hi]
            scores_again = masked_scores(query_part, key_part, allowed, score_scale)
            prob_full = jnp.exp(scores_again - log_masses[group_index])
            prob_again = prob_full.astype(jnp.bfloat16)
            value_grad_parts.append(
                jnp.einsum(
                    "hqk,qhd->khd",
                    prob_again,
                    context_grad_part,
                    preferred_element_type=jnp.float32,
                )
            )
            grad_probs = jnp.einsum(
                "qhd,khd->hqk", context_grad_part, value_part, preferred_element_type=jnp.float32
            )
            grad_scores = prob_full * (
                grad_probs - jnp.sum(prob_full * grad_probs, axis=-1, keepdims=True)
            )
            grad_scores_low = grad_scores.astype(jnp.bfloat16)
            query_grad_parts.append(
                jnp.einsum(
                    "hqk,khd->qhd", grad_scores_low, key_part, preferred_element_type=jnp.float32
                )
                * score_scale
            )
            key_grad_parts.append(
                jnp.einsum(
                    "hqk,qhd->khd", grad_scores_low, query_part, preferred_element_type=jnp.float32
                )
                * score_scale
            )
        grad_value_heads = jnp.concatenate(value_grad_parts, axis=1)
        grad_query_rot = jnp.concatenate(query_grad_parts, axis=1)
        grad_key_rot = jnp.concatenate(key_grad_parts, axis=1)
        grad_query_low = rotate(
            grad_query_rot.reshape(slot_count, model_width), cosine, -sine, head_count
        ).astype(jnp.bfloat16)
        grad_key_low = rotate(
            grad_key_rot.reshape(slot_count, model_width), cosine, -sine, head_count
        ).astype(jnp.bfloat16)
        grad_value_full = grad_value_heads.reshape(slot_count, model_width)
        grad_first_rows.append(0.5 * grad_value_full)
        grad_value_low = (0.5 * grad_value_full).astype(jnp.bfloat16)
        grad_query_w = contract_first(normed, grad_query_low)
        grad_key_w = contract_first(normed, grad_key_low)
        grad_value_w = contract_first(normed, grad_value_low)
        grad_normed = (
            contract_last(grad_query_low, query_b)
            + contract_last(grad_key_low, key_b)
            + contract_last(grad_value_low, value_b)
        )
        grad_gain_first = jnp.sum(grad_normed * inputs * scale_one, axis=0)
        inner_one = grad_normed * gain_first_g
        grad_token_rows.append(
            grad_hidden
            + scale_one * inner_one
            - inputs * scale_one**3 * jnp.mean(inner_one * inputs, axis=-1, keepdims=True)
        )
        gradients = (
            grad_query_w,
            grad_key_w,
            grad_value_w,
            grad_out_w,
            grad_gate_w,
            grad_up_w,
            grad_down_w,
            grad_gain_first,
            grad_gain_second,
        )
        running = (
            gradients
            if running is None
            else tuple((older + newer for older, newer in zip(running, gradients)))
        )
    running = (
        lax.psum_scatter(running[0], ("dp", "fsdp"), scatter_dimension=0, tiled=True),
        lax.psum_scatter(running[1], ("dp", "fsdp"), scatter_dimension=0, tiled=True),
        lax.psum_scatter(running[2], ("dp", "fsdp"), scatter_dimension=0, tiled=True),
        lax.psum_scatter(running[3], ("dp", "fsdp"), scatter_dimension=0, tiled=True),
        lax.psum_scatter(running[4], ("dp", "fsdp"), scatter_dimension=0, tiled=True),
        lax.psum_scatter(running[5], ("dp", "fsdp"), scatter_dimension=0, tiled=True),
        lax.psum_scatter(running[6], ("dp", "fsdp"), scatter_dimension=0, tiled=True),
        lax.psum_scatter(running[7], ("dp", "fsdp"), scatter_dimension=0, tiled=True),
        lax.psum_scatter(running[8], ("dp", "fsdp"), scatter_dimension=0, tiled=True),
    )
    return (
        jnp.concatenate(out_rows, axis=0),
        jnp.concatenate(grad_token_rows, axis=0),
        jnp.concatenate(grad_first_rows, axis=0),
        running[0],
        running[1],
        running[2],
        running[3],
        running[4],
        running[5],
        running[6],
        running[7],
        running[8],
    )


def solution(mesh):
    return jax.shard_map(
        shards,
        mesh=mesh,
        in_specs=(
            P(("dp", "fsdp"), None),
            P(("dp", "fsdp"), None),
            P(("dp", "fsdp"), None),
            P(("dp", "fsdp"), None),
            P(("dp", "fsdp"), None),
            P(("dp", "fsdp"), None),
            P(("dp", "fsdp"), None),
            P(("dp", "fsdp"), None),
            P(("dp", "fsdp"), None),
            P(("dp", "fsdp"), None),
            P(("dp", "fsdp"), None),
            P(("dp", "fsdp")),
            P(("dp", "fsdp")),
        ),
        out_specs=(
            P(("dp", "fsdp"), None),
            P(("dp", "fsdp"), None),
            P(("dp", "fsdp"), None),
            P(("dp", "fsdp"), None),
            P(("dp", "fsdp"), None),
            P(("dp", "fsdp"), None),
            P(("dp", "fsdp"), None),
            P(("dp", "fsdp"), None),
            P(("dp", "fsdp"), None),
            P(("dp", "fsdp"), None),
            P(("dp", "fsdp")),
            P(("dp", "fsdp")),
        ),
        check_vma=False,
    )
```

profile of v0, /device:TPU:0, one launch (start us, length us, event | category | flops | bytes accessed | tf_op | source)
XLA Modules:
  0.0 1880.3 jit_solution(18313129562231017142)
XLA Ops:
  19.3 42.6 %all-reduce.5 = (bf16[1024]{0:T(1024)(128)(2,1)S(1)}, bf16[1024]{0:T(1024)(128)(2,1)S(1)}) all-reduce(bf16[1024]{0:T(1024)(128)(2,1)S(1)} %dynamic-update-slice, bf16[1024]{0:T(1024)(128)(2,1)S(1)} %dynamic-update-slice.1), channel_id=1, replica_groups=mesh['dp'=4,'fsdp'=8] {'dp','fsdp'}, use_global_device_ids=true, to_apply=%add | all-reduce | flops 2048 | bytes 8192
  74.8 54.0 %all-gather.12.cloned.1.call-done = bf16[1024,1024]{1,0:T(8,128)(2,1)} async-done(((bf16[32,1024]{1,0:T(8,128)(2,1)}), bf16[1024,1024]{1,0:T(8,128)(2,1)}) %all-gather.12.cloned.1.call-update) | async-done | bytes 2097168 | tf_op jit(solution)/shard_map/all_gather | solution.py:121
  146.9 40.1 %all-gather.8.cloned.1.call-done = bf16[1024,1024]{1,0:T(8,128)(2,1)} async-done(((bf16[32,1024]{1,0:T(8,128)(2,1)}), bf16[1024,1024]{1,0:T(8,128)(2,1)}) %all-gather.8.cloned.1.call-update) | async-done | bytes 2097168 | tf_op jit(solution)/shard_map/all_gather | solution.py:122
  233.6 11.7 all-gather.14.cloned.1.call-done
  251.8 62.5 %all-gather.16.cloned.1.call-done = bf16[1024,2816]{1,0:T(8,128)(2,1)} async-done(((bf16[32,2816]{1,0:T(8,128)(2,1)}), bf16[1024,2816]{1,0:T(8,128)(2,1)}) %all-gather.16.cloned.1.call-update) | async-done | bytes 5767184 | tf_op jit(solution)/shard_map/all_gather | solution.py:124
  314.2 7.5 fusion.201
  321.8 61.3 %all-gather.18.cloned.1.call-done = bf16[1024,2816]{1,0:T(8,128)(2,1)} async-done(((bf16[32,2816]{1,0:T(8,128)(2,1)}), bf16[1024,2816]{1,0:T(8,128)(2,1)}) %all-gather.18.cloned.1.call-update) | async-done | bytes 5767184 | tf_op jit(solution)/shard_map/all_gather | solution.py:125
  383.0 7.6 fusion.202
  390.6 61.4 %all-gather.20.cloned.1.call-done = bf16[2816,1024]{1,0:T(8,128)(2,1)} async-done(((bf16[88,1024]{1,0:T(8,128)(2,1)}), bf16[2816,1024]{1,0:T(8,128)(2,1)}) %all-gather.20.cloned.1.call-update) | async-done | bytes 5767184 | tf_op jit(solution)/shard_map/all_gather | solution.py:126
  452.0 11.3 multiply_convert_fusion.2
  463.3 6.5 fusion.205
  469.9 6.2 multiply_reduce_fusion.9
  476.2 5.0 fusion.204
  486.1 10.8 multiply_convert_fusion
  496.9 7.3 fusion.208
  504.3 6.4 multiply_reduce_fusion.8
  533.9 6.0 convolution_add_fusion.3
  618.1 5.6 fusion.212
  623.7 6.2 convolution_add_fusion.1
  630.0 5.6 fusion.211
  635.6 6.3 convolution_add_fusion.2
  642.6 5.6 fusion.140
  648.2 6.5 convolution_add_fusion
  674.6 40.0 %all-reduce.4 = (f32[1024]{0:T(1024)S(1)}, f32[1024]{0:T(1024)S(1)}) all-reduce(f32[1024]{0:T(1024)S(1)} %add.294, f32[1024]{0:T(1024)S(1)} %add.295), channel_id=9, replica_groups=mesh['dp'=4,'fsdp'=8] {'dp','fsdp'}, use_global_device_ids=true, to_apply=%region_47.48.clone | all-reduce | flops 2048 | bytes 16384
  715.7 7.4 add_convert_fusion.1
  723.2 5.8 add_convert_fusion
  740.9 89.3 %reduce-scatter.12.cloned.1.call-done = f32[32,1024]{1,0:T(8,128)} async-done(((f32[1024,1024]{1,0:T(8,128)}), f32[32,1024]{1,0:T(8,128)}) %reduce-scatter.12.cloned.1.call-update) | async-done | bytes 131088 | tf_op jit(solution)/shard_map/reduce_scatter | solution.py:305
  830.2 145.8 %reduce-scatter.10.cloned.1.call-done = f32[32,1024]{1,0:T(8,128)} async-done(((f32[1024,1024]{1,0:T(8,128)}), f32[32,1024]{1,0:T(8,128)}) %reduce-scatter.10.cloned.1.call-update) | async-done | bytes 131088 | tf_op jit(solution)/shard_map/reduce_scatter | solution.py:304
  976.0 145.4 %reduce-scatter.8.cloned.1.call-done = f32[32,1024]{1,0:T(8,128)} async-done(((f32[1024,1024]{1,0:T(8,128)}), f32[32,1024]{1,0:T(8,128)}) %reduce-scatter.8.cloned.1.call-update) | async-done | bytes 131088 | tf_op jit(solution)/shard_map/reduce_scatter | solution.py:303
  1121.4 249.3 %reduce-scatter.18.cloned.1.call-done = f32[32,2816]{1,0:T(8,128)} async-done(((f32[1024,2816]{1,0:T(8,128)}), f32[32,2816]{1,0:T(8,128)}) %reduce-scatter.18.cloned.1.call-update) | async-done | bytes 360464 | tf_op jit(solution)/shard_map/reduce_scatter | solution.py:308
  1370.7 251.9 %reduce-scatter.16.cloned.1.call-done = f32[32,2816]{1,0:T(8,128)} async-done(((f32[1024,2816]{1,0:T(8,128)}), f32[32,2816]{1,0:T(8,128)}) %reduce-scatter.16.cloned.1.call-update) | async-done | bytes 360464 | tf_op jit(solution)/shard_map/reduce_scatter | solution.py:307
  1622.6 251.0 %reduce-scatter.20.cloned.1.call-done = f32[88,1024]{1,0:T(8,128)} async-done(((f32[2816,1024]{1,0:T(8,128)}), f32[88,1024]{1,0:T(8,128)}) %reduce-scatter.20.cloned.1.call-update) | async-done | bytes 360464 | tf_op jit(solution)/shard_map/reduce_scatter | solution.py:309
  (499 shorter events, 234.5 us)
Async XLA Ops:
  7.2 63.3 %copy-start = (bf16[1024,1024]{1,0:T(8,128)(2,1)S(1)}, bf16[1024,1024]{1,0:T(8,128)(2,1)}, u32[]{:S(2)}) copy-start(bf16[1024,1024]{1,0:T(8,128)(2,1)} %param.13) | copy-start | bytes 6291460
  7.2 63.3 %all-gather.10.cloned.1.call-start = ((), (), s32[]{:S(2)}) async-start(), calls=%async_computation.8 | async-start | bytes 2162688 | tf_op jit(solution)/shard_map/all_gather | solution.py:120
  7.9 120.9 %all-gather.12.cloned.1.call-start = ((), (), s32[]{:S(2)}) async-start(), calls=%async_computation.9 | async-start | bytes 2162688 | tf_op jit(solution)/shard_map/all_gather | solution.py:121
  8.7 178.4 %all-gather.8.cloned.1.call-start = ((), (), s32[]{:S(2)}) async-start(), calls=%async_computation.7 | async-start | bytes 2162688 | tf_op jit(solution)/shard_map/all_gather | solution.py:122
  9.4 235.9 %all-gather.14.cloned.1.call-start = ((), (), s32[]{:S(2)}) async-start(), calls=%async_computation.10 | async-start | bytes 2162688 | tf_op jit(solution)/shard_map/all_gather | solution.py:123
  10.0 304.3 %all-gather.16.cloned.1.call-start = ((), (), s32[]{:S(2)}) async-start(), calls=%async_computation.11 | async-start | bytes 5947392 | tf_op jit(solution)/shard_map/all_gather | solution.py:124
  10.6 372.5 %all-gather.18.cloned.1.call-start = ((), (), s32[]{:S(2)}) async-start(), calls=%async_computation.12 | async-start | bytes 5947392 | tf_op jit(solution)/shard_map/all_gather | solution.py:125
  11.1 440.8 %all-gather.20.cloned.1.call-start = ((), (), s32[]{:S(2)}) async-start(), calls=%async_computation.13 | async-start | bytes 5947392 | tf_op jit(solution)/shard_map/all_gather | solution.py:126
  11.9 729.0 %reduce-scatter.14.cloned.1.call-start = ((), (), s32[]{:S(2)}) async-start(), calls=%async_computation.17 | async-start | bytes 4325376 | tf_op jit(solution)/shard_map/reduce_scatter | solution.py:306
  14.8 495.9 %copy-start.138 = (f32[512]{0:T(512)}, f32[512]{0:T(512)S(1)}, u32[]{:S(2)}) copy-start(f32[512]{0:T(512)S(1)} %fusion.173) | copy-start | bytes 6148
  61.9 152.1 %copy-start.99 = (f32[1024]{0:T(1024)}, f32[1024]{0:T(1024)S(1)}, u32[]{:S(2)}) copy-start(f32[1024]{0:T(1024)S(1)} %convert_element_type.247) | copy-start | bytes 12292
  64.5 122.5 %copy-start.108 = (f32[512]{0:T(512)}, f32[512]{0:T(512)S(1)}, u32[]{:S(2)}) copy-start(f32[512]{0:T(512)S(1)} %get-tuple-element.127) | copy-start | bytes 6148
  64.5 149.5 %copy-start.106 = (f32[512]{0:T(512)}, f32[512]{0:T(512)S(1)}, u32[]{:S(2)}) copy-start(f32[512]{0:T(512)S(1)} %get-tuple-element.76) | copy-start | bytes 6148
  66.2 65.7 %copy-start.89 = (f32[512,32]{0,1:T(8,128)}, f32[512,32]{0,1:T(8,128)S(1)}, u32[]{:S(2)}) copy-start(f32[512,32]{0,1:T(8,128)S(1)} %get-tuple-element.69) | copy-start | bytes 196612
  66.2 149.5 %copy-start.87 = (f32[512,32]{0,1:T(8,128)}, f32[512,32]{0,1:T(8,128)S(1)}, u32[]{:S(2)}) copy-start(f32[512,32]{0,1:T(8,128)S(1)} %get-tuple-element.86) | copy-start | bytes 196612
  132.8 10.6 copy-start.79
  193.1 23.6 %copy-start.59 = (bf16[512,1024]{0,1:T(8,128)(2,1)}, bf16[512,1024]{0,1:T(8,128)(2,1)S(1)}, u32[]{:S(2)}) copy-start(bf16[512,1024]{0,1:T(8,128)(2,1)S(1)} %copy.171) | copy-start | bytes 3145732
  220.6 24.7 %copy-start.36 = (bf16[512,16,64]{0,2,1:T(8,128)(2,1)}, bf16[512,16,64]{0,2,1:T(8,128)(2,1)S(1)}, u32[]{:S(2)}) copy-start(bf16[512,16,64]{0,2,1:T(8,128)(2,1)S(1)} %pad_maximum_fusion.9) | copy-start | bytes 3145732
  251.7 131.3 %copy-start.78 = (bf16[512,1024]{1,0:T(8,128)(2,1)}, bf16[512,1024]{1,0:T(8,128)(2,1)S(1)}, u32[]{:S(2)}) copy-start(bf16[512,1024]{1,0:T(8,128)(2,1)S(1)} %multiply_convert_fusion.16) | copy-start | bytes 3145732
  321.8 130.2 %copy-start.54 = (bf16[1024,1024]{1,0:T(8,128)(2,1)S(1)}, bf16[1024,1024]{1,0:T(8,128)(2,1)}, u32[]{:S(2)}) copy-start(bf16[1024,1024]{1,0:T(8,128)(2,1)} %param.15) | copy-start | bytes 6291460
  463.3 17.9 slice-start
  469.9 11.2 slice-start.1
  512.7 17.3 copy-start.34
  539.9 290.3 %reduce-scatter.12.cloned.1.call-start = ((), (), s32[]{:S(2)}) async-start(), calls=%async_computation.16 | async-start | bytes 4325376 | tf_op jit(solution)/shard_map/reduce_scatter | solution.py:305
  547.4 27.2 %copy-start.24 = (f32[512,16,64]{0,2,1:T(8,128)}, f32[512,16,64]{0,2,1:T(8,128)S(1)}, u32[]{:S(2)}) copy-start(f32[512,16,64]{0,2,1:T(8,128)S(1)} %maximum_multiply_fusion) | copy-start | bytes 6291460
  553.4 22.7 %copy-start.26 = (f32[512,16,64]{0,2,1:T(8,128)}, f32[512,16,64]{0,2,1:T(8,128)S(1)}, u32[]{:S(2)}) copy-start(f32[512,16,64]{0,2,1:T(8,128)S(1)} %maximum_multiply_fusion.1) | copy-start | bytes 6291460
  579.7 396.3 %reduce-scatter.10.cloned.1.call-start = ((), (), s32[]{:S(2)}) async-start(), calls=%async_computation.15 | async-start | bytes 4325376 | tf_op jit(solution)/shard_map/reduce_scatter | solution.py:304
  586.0 20.3 %copy-start.83 = (bf16[512,16,2,32]{0,3,2,1:T(8,128)(2,1)}, bf16[512,16,2,32]{0,3,2,1:T(8,128)(2,1)S(1)}, u32[]{:S(2)}) copy-start(bf16[512,16,2,32]{0,3,2,1:T(8,128)(2,1)S(1)} %pad_maximum_fusion.14) | copy-start | bytes 3145732
  611.2 510.2 %reduce-scatter.8.cloned.1.call-start = ((), (), s32[]{:S(2)}) async-start(), calls=%async_computation.14 | async-start | bytes 4325376 | tf_op jit(solution)/shard_map/reduce_scatter | solution.py:303
  617.8 752.9 %reduce-scatter.18.cloned.1.call-start = ((), (), s32[]{:S(2)}) async-start(), calls=%async_computation.19 | async-start | bytes 11894784 | tf_op jit(solution)/shard_map/reduce_scatter | solution.py:308
  629.9 992.7 %reduce-scatter.16.cloned.1.call-start = ((), (), s32[]{:S(2)}) async-start(), calls=%async_computation.18 | async-start | bytes 11894784 | tf_op jit(solution)/shard_map/reduce_scatter | solution.py:307
  641.9 1231.7 %reduce-scatter.20.cloned.1.call-start = ((), (), s32[]{:S(2)}) async-start(), calls=%async_computation.20 | async-start | bytes 11894784 | tf_op jit(solution)/shard_map/reduce_scatter | solution.py:309
  (135 other events, 429.3 us)
Sparse Core Ops, SparseCore 0:
  11.0 59.4 all-gather.9
  73.5 55.2 all-gather.11
  131.8 55.1 all-gather.7
  189.9 55.4 all-gather.13
  248.1 66.1 all-gather.15
  317.0 65.9 all-gather.17
  386.0 65.9 all-gather.19
  540.0 144.1 reduce-scatter.13
  687.1 143.0 reduce-scatter.11
  832.9 143.0 reduce-scatter.9
  978.9 142.4 reduce-scatter.7
  1124.2 246.5 reduce-scatter.17
  1373.6 248.9 reduce-scatter.15
  1625.4 248.1 reduce-scatter.19
where the time goes:
time: 1890 us; the launch traced here: 1880 us
  waiting for transfers between devices  1430 us (76%)
  matrix products  253 us (13%)
  blocking collectives  82.6 us (4%)
  local copies, waits for them, and re-layouts  47.9 us (3%)
  other arithmetic  47.5 us (3%)
    reduce_scatter x1, waiting for transfers between devices, shards(): lax.psum_scatter(running[4], ('dp', 'fsdp'), scatter_dimension=0, tiled=T...  252 us
    reduce_scatter x1, waiting for transfers between devices, shards(): lax.psum_scatter(running[6], ('dp', 'fsdp'), scatter_dimension=0, tiled=T...  251 us
    reduce_scatter x1, waiting for transfers between devices, shards(): lax.psum_scatter(running[5], ('dp', 'fsdp'), scatter_dimension=0, tiled=T...  249 us
    reduce_scatter x1, waiting for transfers between devices, shards(): lax.psum_scatter(running[1], ('dp', 'fsdp'), scatter_dimension=0, tiled=T...  146 us
    reduce_scatter x1, waiting for transfers between devices, shards(): lax.psum_scatter(running[0], ('dp', 'fsdp'), scatter_dimension=0, tiled=T...  145 us
    reduce_scatter x1, waiting for transfers between devices, shards(): lax.psum_scatter(running[2], ('dp', 'fsdp'), scatter_dimension=0, tiled=T...  89.3 us
    unnamed x2, blocking collectives  82.6 us
    dot_general x14, matrix products, contract_last(): lax.dot_general(left, right, (((1,), (1,)), ((), ())), preferred_element_...  65.3 us
  transfers between devices with their start and end apart: 14, of which 13 were waited for; matrix products, arithmetic and copies ran while one was open for 12% of the time, Pallas kernels for 0%

commit v1 on v0

v1 whole, which is shorter than its diff:
```python
import math
from functools import partial

import jax
import jax.numpy as jnp
from jax import lax
from jax.sharding import PartitionSpec as P

HEADS = 16


EPSILON = 1e-06


def forward_dot(left, right):
    return jnp.dot(left, right, preferred_element_type=jnp.float32)


def contract_last(left, right):
    return lax.dot_general(
        left, right, (((1,), (1,)), ((), ())), preferred_element_type=jnp.float32
    )


def contract_first(left, right):
    return lax.dot_general(
        left, right, (((0,), (0,)), ((), ())), preferred_element_type=jnp.float32
    )


def bucket_layout(lengths_row, slot_count):
    seq_ends = jnp.cumsum(lengths_row)
    slot_places = jnp.arange(slot_count, dtype=jnp.int32)
    ended_mask = seq_ends[None, :] <= slot_places[:, None]
    segment = jnp.sum(ended_mask.astype(jnp.int32), axis=1)
    before_total = jnp.sum(jnp.where(ended_mask, lengths_row[None, :], 0), axis=1)
    return (segment, slot_places - before_total, slot_places < seq_ends[-1])


def rope_tables(position, head_size):
    half_size = head_size // 2
    frequency = jnp.exp(
        jnp.arange(half_size, dtype=jnp.float32) * (-2.0 * math.log(10000.0) / head_size)
    )
    angles = position.astype(jnp.float32)[:, None] * frequency[None, :]
    return (jnp.cos(angles), jnp.sin(angles))


def rotate(matrix, cosine, sine, head_count):
    row_count = matrix.shape[0]
    halves = matrix.reshape(row_count, head_count, 2, -1)
    first_half = halves[:, :, 0]
    second_half = halves[:, :, 1]
    cos_table = cosine[:, None, :]
    sin_table = sine[:, None, :]
    turned = jnp.stack(
        [
            first_half * cos_table - second_half * sin_table,
            second_half * cos_table + first_half * sin_table,
        ],
        axis=2,
    )
    return turned.reshape(row_count, -1)


def allowed_mask(segment, valid):
    slot_places = jnp.arange(segment.shape[0])
    earlier = slot_places[None, :] < slot_places[:, None]
    same_seq = segment[:, None] == segment[None, :]
    diagonal = slot_places[None, :] == slot_places[:, None]
    return diagonal | same_seq & earlier & valid[:, None]


def rms_scale(matrix):
    return lax.rsqrt(jnp.mean(matrix * matrix, axis=-1, keepdims=True) + EPSILON)


def masked_scores(query_heads, key_heads, allowed, score_scale):
    raw_scores = (
        jnp.einsum("qhd,khd->hqk", query_heads, key_heads, preferred_element_type=jnp.float32)
        * score_scale
    )
    return jnp.where(allowed[None], raw_scores, -1e30)


AXES = ("dp", "fsdp")


def flip(value, bit, device_count):
    pairs = [(place, place ^ (1 << bit)) for place in range(device_count)]
    return lax.ppermute(value, AXES, pairs)


def stage_orders(dp_size, fsdp_size):
    bit_count = (dp_size * fsdp_size).bit_length() - 1
    core_bit = fsdp_size.bit_length() - 1
    high_bits = list(range(core_bit + 1, bit_count))
    rest = list(range(1, core_bit))
    return ([core_bit] + high_bits + [0] + rest, [core_bit, 0] + high_bits + rest)


def reduce_rows(partial_sum, order, place, device_count):
    bit_count = len(order)
    row_count, width = partial_sum.shape
    current = partial_sum.reshape((2,) * bit_count + (row_count // device_count, width))
    left = list(range(bit_count - 1, -1, -1))
    for step, bit in enumerate(order):
        axis = left.index(bit)
        mine = (place >> bit) & 1
        sent = lax.dynamic_index_in_dim(current, 1 - mine, axis, keepdims=False)
        kept = lax.dynamic_index_in_dim(current, mine, axis, keepdims=False)
        got = flip(sent.astype(jnp.bfloat16), bit, device_count)
        current = kept.astype(jnp.float32) + got.astype(jnp.float32)
        if step + 1 < bit_count:
            current = current.astype(jnp.bfloat16)
        left.remove(bit)
    return current


def shards(
    dp_size,
    fsdp_size,
    tokens,
    first_values,
    cotangent,
    lengths,
    w_query,
    w_key,
    w_value,
    w_out,
    w_gate,
    w_up,
    w_down,
    gain_one,
    gain_two,
):
    device_count = dp_size * fsdp_size
    place = lax.axis_index("dp") * fsdp_size + lax.axis_index("fsdp")
    order_a, order_b = stage_orders(dp_size, fsdp_size)
    micro_count = lengths.shape[0]
    token_count, model_width = tokens.shape
    slot_count = token_count // micro_count
    head_count = HEADS
    head_size = model_width // head_count
    hidden_width = w_gate.shape[1]
    group_heads = 4
    group_count = head_count // group_heads
    score_scale = head_size ** (-0.5)

    gains = jnp.pad(jnp.stack([gain_one, gain_two], axis=1), ((0, 0), (0, 126)))
    first_set = lax.all_gather(
        jnp.concatenate([w_query, w_key, w_value, gains], axis=1), AXES, axis=0, tiled=True
    )
    second_set = lax.all_gather(
        jnp.concatenate([w_out, w_gate, w_up], axis=1), AXES, axis=0, tiled=True
    )
    down_w = lax.all_gather(w_down, AXES, axis=0, tiled=True)
    query_w = first_set[:, :model_width]
    key_w = first_set[:, model_width : 2 * model_width]
    value_w = first_set[:, 2 * model_width : 3 * model_width]
    gain_first_f = first_set[:, 3 * model_width].astype(jnp.float32)[None, :]
    gain_second_f = first_set[:, 3 * model_width + 1].astype(jnp.float32)[None, :]
    out_w = second_set[:, :model_width]
    gate_w = second_set[:, model_width : model_width + hidden_width]
    up_w = second_set[:, model_width + hidden_width :]

    inputs = tokens.astype(jnp.float32)
    first_input = first_values.astype(jnp.float32)
    layouts = [bucket_layout(lengths[index], slot_count) for index in range(micro_count)]
    position = jnp.concatenate([layout[1] for layout in layouts])
    valid = jnp.concatenate([layout[2] for layout in layouts])
    cosine, sine = rope_tables(position, head_size)
    allowed = [allowed_mask(layout[0], layout[2]) for layout in layouts]
    scale_one = rms_scale(inputs)
    normed = (inputs * scale_one * gain_first_f).astype(jnp.bfloat16)
    query_rot = rotate(forward_dot(normed, query_w), cosine, sine, head_count).astype(jnp.bfloat16)
    key_rot = rotate(forward_dot(normed, key_w), cosine, sine, head_count).astype(jnp.bfloat16)
    value_mix = (0.5 * forward_dot(normed, value_w) + 0.5 * first_input).astype(jnp.bfloat16)
    shape = (micro_count, slot_count, head_count, head_size)
    query_heads = query_rot.reshape(shape)
    key_heads = key_rot.reshape(shape)
    value_heads = value_mix.reshape(shape)
    contexts = []
    log_masses = []
    for index in range(micro_count):
        context_parts = []
        for group_index in range(group_count):
            head_lo = group_index * group_heads
            head_hi = head_lo + group_heads
            scores = masked_scores(
                query_heads[index, :, head_lo:head_hi],
                key_heads[index, :, head_lo:head_hi],
                allowed[index],
                score_scale,
            )
            top_score = jnp.max(scores, axis=-1, keepdims=True)
            exp_scores = jnp.exp(scores - top_score)
            total_mass = jnp.sum(exp_scores, axis=-1, keepdims=True)
            prob_low = (exp_scores / total_mass).astype(jnp.bfloat16)
            log_masses.append(top_score + jnp.log(total_mass))
            context_parts.append(
                jnp.einsum(
                    "hqk,khd->qhd",
                    prob_low,
                    value_heads[index, :, head_lo:head_hi],
                    preferred_element_type=jnp.float32,
                )
            )
        contexts.append(jnp.concatenate(context_parts, axis=1).reshape(slot_count, model_width))
    context = jnp.concatenate(contexts, axis=0).astype(jnp.bfloat16)
    hidden = inputs + forward_dot(context, out_w)
    scale_two = rms_scale(hidden)
    normed_two = (hidden * scale_two * gain_second_f).astype(jnp.bfloat16)
    gate_values = forward_dot(normed_two, gate_w)
    upward = forward_dot(normed_two, up_w)
    sigmoid_gate = jax.nn.sigmoid(gate_values)
    silu_gate = gate_values * sigmoid_gate
    product = (silu_gate * upward).astype(jnp.bfloat16)
    out_tokens = (hidden + forward_dot(product, down_w)).astype(jnp.bfloat16)

    grad_y = cotangent.astype(jnp.float32) * valid.astype(jnp.float32)[:, None]
    grad_y_low = grad_y.astype(jnp.bfloat16)
    grad_down_w = contract_first(product, grad_y_low).astype(jnp.bfloat16)
    grad_down_sum = reduce_rows(grad_down_w, order_a, place, device_count)
    grad_product = contract_last(grad_y_low, down_w)
    grad_upward = (grad_product * silu_gate).astype(jnp.bfloat16)
    grad_gate_low = (
        grad_product * upward * sigmoid_gate * (1.0 + gate_values * (1.0 - sigmoid_gate))
    ).astype(jnp.bfloat16)
    grad_gate_w = contract_first(normed_two, grad_gate_low).astype(jnp.bfloat16)
    grad_gate_sum = reduce_rows(grad_gate_w, order_b, place, device_count)
    grad_up_w = contract_first(normed_two, grad_upward).astype(jnp.bfloat16)
    grad_up_sum = reduce_rows(grad_up_w, order_a, place, device_count)
    grad_normed_two = contract_last(grad_gate_low, gate_w) + contract_last(grad_upward, up_w)
    grad_gain_second = jnp.sum(grad_normed_two * hidden * scale_two, axis=0)
    inner_two = grad_normed_two * gain_second_f
    grad_hidden = (
        grad_y
        + scale_two * inner_two
        - hidden * scale_two**3 * jnp.mean(inner_two * hidden, axis=-1, keepdims=True)
    )
    grad_hidden_low = grad_hidden.astype(jnp.bfloat16)
    grad_out_w = contract_first(context, grad_hidden_low).astype(jnp.bfloat16)
    grad_out_sum = reduce_rows(grad_out_w, order_b, place, device_count)
    grad_context = contract_last(grad_hidden_low, out_w).astype(jnp.bfloat16)
    grad_context_heads = grad_context.reshape(shape)
    value_grads = []
    query_grads = []
    key_grads = []
    for index in range(micro_count):
        value_grad_parts = []
        query_grad_parts = []
        key_grad_parts = []
        for group_index in range(group_count):
            head_lo = group_index * group_heads
            head_hi = head_lo + group_heads
            query_part = query_heads[index, :, head_lo:head_hi]
            key_part = key_heads[index, :, head_lo:head_hi]
            value_part = value_heads[index, :, head_lo:head_hi]
            context_grad_part = grad_context_heads[index, :, head_lo:head_hi]
            scores_again = masked_scores(query_part, key_part, allowed[index], score_scale)
            prob_full = jnp.exp(scores_again - log_masses[index * group_count + group_index])
            prob_again = prob_full.astype(jnp.bfloat16)
            value_grad_parts.append(
                jnp.einsum(
                    "hqk,qhd->khd",
                    prob_again,
                    context_grad_part,
                    preferred_element_type=jnp.float32,
                )
            )
            grad_probs = jnp.einsum(
                "qhd,khd->hqk", context_grad_part, value_part, preferred_element_type=jnp.float32
            )
            grad_scores = prob_full * (
                grad_probs - jnp.sum(prob_full * grad_probs, axis=-1, keepdims=True)
            )
            grad_scores_low = grad_scores.astype(jnp.bfloat16)
            query_grad_parts.append(
                jnp.einsum(
                    "hqk,khd->qhd", grad_scores_low, key_part, preferred_element_type=jnp.float32
                )
                * score_scale
            )
            key_grad_parts.append(
                jnp.einsum(
                    "hqk,qhd->khd", grad_scores_low, query_part, preferred_element_type=jnp.float32
                )
                * score_scale
            )
        flat = (slot_count, model_width)
        value_grads.append(jnp.concatenate(value_grad_parts, axis=1).reshape(flat))
        query_grads.append(jnp.concatenate(query_grad_parts, axis=1).reshape(flat))
        key_grads.append(jnp.concatenate(key_grad_parts, axis=1).reshape(flat))
    grad_value_full = jnp.concatenate(value_grads, axis=0)
    grad_query_low = rotate(
        jnp.concatenate(query_grads, axis=0), cosine, -sine, head_count
    ).astype(jnp.bfloat16)
    grad_key_low = rotate(jnp.concatenate(key_grads, axis=0), cosine, -sine, head_count).astype(
        jnp.bfloat16
    )
    grad_first = 0.5 * grad_value_full
    grad_value_low = grad_first.astype(jnp.bfloat16)
    grad_query_w = contract_first(normed, grad_query_low).astype(jnp.bfloat16)
    grad_key_w = contract_first(normed, grad_key_low).astype(jnp.bfloat16)
    grad_value_w = contract_first(normed, grad_value_low).astype(jnp.bfloat16)
    grad_normed = (
        contract_last(grad_query_low, query_w)
        + contract_last(grad_key_low, key_w)
        + contract_last(grad_value_low, value_w)
    )
    grad_gain_first = jnp.sum(grad_normed * inputs * scale_one, axis=0)
    inner_one = grad_normed * gain_first_f
    grad_tokens = (
        grad_hidden
        + scale_one * inner_one
        - inputs * scale_one**3 * jnp.mean(inner_one * inputs, axis=-1, keepdims=True)
    )
    grad_query_sum = reduce_rows(grad_query_w, order_a, place, device_count)
    grad_key_sum = reduce_rows(grad_key_w, order_b, place, device_count)
    grad_value_sum = reduce_rows(grad_value_w, order_a, place, device_count)
    gain_columns = jnp.pad(
        jnp.stack([grad_gain_first, grad_gain_second], axis=1), ((0, 0), (0, 126))
    )
    grad_gains = reduce_rows(gain_columns, order_b, place, device_count)
    return (
        out_tokens,
        grad_tokens,
        grad_first,
        grad_query_sum,
        grad_key_sum,
        grad_value_sum,
        grad_out_sum,
        grad_gate_sum,
        grad_up_sum,
        grad_down_sum,
        grad_gains[:, 0],
        grad_gains[:, 1],
    )


def solution(mesh):
    rows = P(AXES, None)
    ends = P(AXES)
    return jax.shard_map(
        partial(shards, mesh.shape["dp"], mesh.shape["fsdp"]),
        mesh=mesh,
        in_specs=(rows,) * 11 + (ends,) * 2,
        out_specs=(rows,) * 10 + (ends,) * 2,
        check_vma=False,
    )
```

time: 1890 us -> 742 us (0.39)
  waiting for transfers between devices: 1430 us -> 256 us
  blocking collectives: 82.6 us -> 0 us
  local copies, waits for them, and re-layouts: 47.9 us -> 124 us
  starting transfers between devices: 0.94 us -> 35.1 us
  other arithmetic: 47.5 us -> 71.9 us
  matrix products: 253 us -> 229 us
    reduce_scatter x7 -> x0, waiting for transfers between devices: 1130 us -> none  [the longest x1 252 us: shards(): lax.psum_scatter(running[4], ('dp', 'fsdp'), scatter_dimension=0, tiled=T...]
    all_gather x7 -> x3, waiting for transfers between devices: 295 us -> 124 us  [the longest x1 60.6 us: shards(): lax.all_gather(jnp.concatenate([w_query, w_key, w_value, gains], axis=1),...]
    ppermute x0 -> x40, waiting for transfers between devices: none -> 131 us  [flip(): return lax.ppermute(value, AXES, pairs)]
    unnamed x2 -> x0, blocking collectives: 82.6 us -> none
    ppermute x0 -> x40, starting transfers between devices: none -> 35 us  [flip(): return lax.ppermute(value, AXES, pairs)]
    dynamic_slice x0 -> x14, local copies, waits for them, and re-layouts: none -> 27.2 us  [the longest x7 14.2 us: reduce_rows(): kept = lax.dynamic_index_in_dim(current, mine, axis, keepdims=False)]
    slice x0 -> x5, local copies, waits for them, and re-layouts: none -> 22.5 us  [the longest x1 6.08 us: shards(): query_heads[index, :, head_lo:head_hi]]
    dot_general x14 -> x7, matrix products: 59.7 us -> 41.6 us  [contract_first(): lax.dot_general(left, right, (((0,), (0,)), ((), ())), preferred_element_...]
  transfers between devices with their start and end apart: 14 -> 43, of which waited for: 13 -> 28; matrix products, arithmetic and copies ran while one was open for 12% -> 26% of each run, Pallas kernels for 0% -> 0%
where the time goes in v1:
time: 742 us; the launch traced here: 732 us
  waiting for transfers between devices  256 us (35%)
  matrix products  229 us (31%)
  local copies, waits for them, and re-layouts  124 us (17%)
  other arithmetic  71.9 us (10%)
  starting transfers between devices  35.1 us (5%)
  between operations  16.6 us (2%)
    ppermute x40, waiting for transfers between devices, flip(): return lax.ppermute(value, AXES, pairs)  131 us
    dot_general x7, matrix products, forward_dot(): return jnp.dot(left, right, preferred_element_type=jnp.float32)  62.6 us
    all_gather x1, waiting for transfers between devices, shards(): lax.all_gather(jnp.concatenate([w_query, w_key, w_value, gains], axis=1),...  60.6 us
    all_gather x1, waiting for transfers between devices, shards(): down_w = lax.all_gather(w_down, AXES, axis=0, tiled=True)  53.2 us
    dot_general x7, matrix products, contract_last(): lax.dot_general(left, right, (((1,), (1,)), ((), ())), preferred_element_...  49.1 us
    unnamed x304, local copies, waits for them, and re-layouts  47 us
    dot_general x7, matrix products, contract_first(): lax.dot_general(left, right, (((0,), (0,)), ((), ())), preferred_element_...  41.6 us
    ppermute x40, starting transfers between devices, flip(): return lax.ppermute(value, AXES, pairs)  35 us
  transfers between devices with their start and end apart: 43, of which 28 were waited for; matrix products, arithmetic and copies ran while one was open for 26% of the time, Pallas kernels for 0%

profile of v1, /device:TPU:0, one launch (start us, length us, event | category | flops | bytes accessed | tf_op | source)
XLA Modules:
  0.0 732.4 jit_solution(15424005569712097870)
XLA Ops:
  17.5 4.6 copy.324
  27.8 53.2 %all-gather.8.cloned.1.call-done = bf16[2816,1024]{1,0:T(8,128)(2,1)} async-done(((bf16[88,1024]{1,0:T(8,128)(2,1)}), bf16[2816,1024]{1,0:T(8,128)(2,1)}) %all-gather.8.cloned.1.call-update) | async-done | bytes 5767184 | tf_op jit(solution)/shard_map/all_gather | solution.py:157
  81.0 11.9 %fusion.94 = f32[1024,2816]{1,0:T(8,128)} fusion(bf16[2816,1024]{1,0:T(8,128)(2,1)} %all-gather.8.cloned.1.call-done, bf16[1024,1024]{0,1:T(8,128)(2,1)} %copy.324, f32[1024]{0:T(1024)S(1)} %add_convert_fusion.6), kind=kOutput, calls=%fused_computation.200 | convolution fusion | flops 5908725760 | bytes 19402752 | tf_op jit(solution)/shard_map/dot_general | solution.py:20
  92.9 60.6 %all-gather.4.cloned.1.call-done = bf16[1024,3200]{1,0:T(8,128)(2,1)} async-done(((bf16[32,3200]{1,0:T(8,128)(2,1)}), bf16[1024,3200]{1,0:T(8,128)(2,1)}) %all-gather.4.cloned.1.call-update) | async-done | bytes 6553616 | tf_op jit(solution)/shard_map/all_gather | solution.py:151
  154.9 6.2 multiply_convert_fusion.12
  161.1 6.4 reshape.631
  167.4 5.6 fusion.241
  209.5 6.1 fusion.243
  215.7 4.5 fusion.242
  244.6 10.4 %all-gather.6.cloned.1.call-done = bf16[1024,6656]{1,0:T(8,128)(2,1)} async-done(((bf16[32,6656]{1,0:T(8,128)(2,1)}), bf16[1024,6656]{1,0:T(8,128)(2,1)}) %all-gather.6.cloned.1.call-update) | async-done | bytes 13631504 | tf_op jit(solution)/shard_map/all_gather | solution.py:154
  255.0 4.5 multiply_reduce_fusion.10
  261.9 11.7 %fusion.6 = f32[1024,2816]{1,0:T(8,128)} fusion(bf16[1024,1024]{0,1:T(8,128)(2,1)S(1)} %multiply_convert_fusion.11, bf16[1024,6656]{1,0:T(8,128)(2,1)} %all-gather.6.cloned.1.call-done), kind=kOutput, calls=%fused_computation.22 | convolution fusion | flops 5905580032 | bytes 19398656 | tf_op jit(solution)/shard_map/dot_general | solution.py:16
  273.6 20.7 %multiply_convert_fusion.1 = (bf16[1024,2816]{1,0:T(8,128)(2,1)}, bf16[1024,2816]{1,0:T(8,128)(2,1)}, bf16[1024,2816]{1,0:T(8,128)(2,1)}) fusion(f32[1024,2816]{1,0:T(8,128)} %fusion.94, f32[1024,2816]{1,0:T(8,128)} %fusion.6, bf16[1024,1024]{0,1:T(8,128)(2,1)S(1)} %multiply_convert_fusion.11, bf16[1024,6656]{1,0:T(8,128)(2,1)} %all-gather.6.cloned.1.call-done), kind=kOutput, calls=%fused_computation.1 | convolution fusion | flops 5948833792 | bytes 48234496 | tf_op jit(solution)/shard_map/dot_general | solution.py:16
  294.2 10.7 %convolution_convert_fusion.1 = bf16[1024,2816]{1,0:T(8,128)(2,1)} fusion(bf16[1024,1024]{0,1:T(8,128)(2,1)S(1)} %multiply_convert_fusion.11, bf16[1024,2816]{1,0:T(8,128)(2,1)} %get-tuple-element.73), kind=kOutput, calls=%fused_computation.18 | convolution fusion | flops 5908463616 | bytes 13631488 | tf_op jit(solution)/shard_map/dot_general | solution.py:26
  305.0 7.9 %convolution_convert_fusion.2 = bf16[1024,2816]{1,0:T(8,128)(2,1)} fusion(bf16[1024,1024]{0,1:T(8,128)(2,1)S(1)} %multiply_convert_fusion.11, bf16[1024,2816]{1,0:T(8,128)(2,1)S(1)} %copy-done.126), kind=kOutput, calls=%fused_computation.19 | convolution fusion | flops 5908463616 | bytes 13631488 | tf_op jit(solution)/shard_map/dot_general | solution.py:26
  312.9 9.6 %fusion.4 = f32[1024,1024]{0,1:T(8,128)} fusion(bf16[1024,2816]{1,0:T(8,128)(2,1)} %get-tuple-element.73, bf16[1024,6656]{1,0:T(8,128)(2,1)S(1)} %bitcast.615), kind=kOutput, calls=%fused_computation.20 | convolution fusion | flops 5905580032 | bytes 15728640 | tf_op jit(solution)/shard_map/dot_general | solution.py:20
  322.6 12.4 %multiply_reduce_fusion = (f32[1024]{0:T(1024)}, f32[1024]{0:T(1024)S(1)}, f32[1024,1024]{0,1:T(8,128)S(1)}) fusion(f32[1024,1024]{0,1:T(8,128)S(1)} %copy-done.20, f32[1024]{0:T(1024)S(1)} %get-tuple-element.139, f32[1024]{0:T(1024)S(1)} %get-tuple-element.62, f32[1024,1024]{0,1:T(8,128)} %fusion.4, bf16[1024,2816]{1,0:T(8,128)(2,1)} %get-tuple-element.72, ...), kind=kOutput, calls=%fused_computation.41 | convolution fusion | flops 5912918016 | bytes 24133632 | tf_op jit(solution)/shard_map/dot_general | solution.py:20
  340.0 5.3 convolution_convert_fusion.7
  345.4 6.3 reshape.632
  351.7 5.6 fusion.240
  445.1 8.1 %convolution_convert_fusion = bf16[2816,1024]{1,0:T(8,128)(2,1)} fusion(bf16[1024,2816]{1,0:T(8,128)(2,1)S(1)} %bitcast.619, bf16[1024,1024]{0,1:T(8,128)(2,1)S(1)} %copy-done.27, f32[1024]{0:T(1024)S(1)} %copy-done.124), kind=kOutput, calls=%fused_computation.17 | convolution fusion | flops 5911609344 | bytes 13635584 | tf_op jit(solution)/shard_map/dot_general | solution.py:26
  482.9 5.1 fusion.19
  488.6 6.6 fusion.16
  495.2 11.0 %add_convert_fusion = bf16[1024,1024]{0,1:T(8,128)(2,1)} fusion(f32[1024,1024]{0,1:T(8,128)S(1)} %copy-done.21, bf16[1024,2816]{1,0:T(8,128)(2,1)} %get-tuple-element.74, bf16[2816,1024]{1,0:T(8,128)(2,1)} %all-gather.8.cloned.1.call-done), kind=kOutput, calls=%fused_computation.71 | convolution fusion | flops 5907677184 | bytes 17825792 | tf_op jit(solution)/shard_map/dot_general | solution.py:16
  539.7 5.6 copy.381
  553.8 11.1 %collective-permute-done.16 = bf16[2,2,2,32,1024]{4,3,1,2,0:T(8,128)(2,1)S(1)} collective-permute-done((bf16[2,2,2,32,1024]{4,3,1,2,0:T(8,128)(2,1)S(1)}, bf16[2,2,2,32,1024]{4,3,1,2,0:T(8,128)(2,1)S(1)}, u32[]{:S(2)}, u32[]{:S(2)}) %collective-permute-start.16) | collective-permute-done | bytes 524320 | tf_op jit(solution)/shard_map/ppermute | solution.py:91
  567.4 10.7 %collective-permute-done.6 = bf16[2,2,2,32,1024]{4,3,1,2,0:T(8,128)(2,1)S(1)} collective-permute-done((bf16[2,2,2,32,1024]{4,3,1,2,0:T(8,128)(2,1)S(1)}, bf16[2,2,2,32,1024]{4,3,1,2,0:T(8,128)(2,1)S(1)}, u32[]{:S(2)}, u32[]{:S(2)}) %collective-permute-start.6) | collective-permute-done | bytes 524320 | tf_op jit(solution)/shard_map/ppermute | solution.py:91
  629.6 27.3 %collective-permute-done.26 = bf16[2,2,2,32,2816]{4,3,0,1,2:T(8,128)(2,1)S(1)} collective-permute-done((bf16[2,2,2,32,2816]{4,3,0,1,2:T(8,128)(2,1)S(1)}, bf16[2,2,2,32,2816]{4,3,0,1,2:T(8,128)(2,1)S(1)}, u32[]{:S(2)}, u32[]{:S(2)}) %collective-permute-start.26) | collective-permute-done | bytes 1441824 | tf_op jit(solution)/shard_map/ppermute | solution.py:91
  660.6 25.9 %collective-permute-done.31 = bf16[2,2,2,88,1024]{4,3,0,1,2:T(8,128)(2,1)S(1)} collective-permute-done((bf16[2,2,2,88,1024]{4,3,0,1,2:T(8,128)(2,1)S(1)}, bf16[2,2,2,88,1024]{4,3,0,1,2:T(8,128)(2,1)S(1)}, u32[]{:S(2)}, u32[]{:S(2)}) %collective-permute-start.31) | collective-permute-done | bytes 1441824 | tf_op jit(solution)/shard_map/ppermute | solution.py:91
  688.2 6.0 collective-permute-done.22
  702.8 4.5 collective-permute-done.23
  716.9 5.8 collective-permute-done.24
  (602 shorter events, 323.8 us)
Async XLA Ops:
  7.2 73.8 %all-gather.8.cloned.1.call-start = ((), (), s32[]{:S(2)}) async-start(), calls=%async_computation.2 | async-start | bytes 5947392 | tf_op jit(solution)/shard_map/all_gather | solution.py:157
  7.9 145.6 %all-gather.4.cloned.1.call-start = ((), (), s32[]{:S(2)}) async-start(), calls=%async_computation | async-start | bytes 6758400 | tf_op jit(solution)/shard_map/all_gather | solution.py:151
  10.4 244.6 %all-gather.6.cloned.1.call-start = ((), (), s32[]{:S(2)}) async-start(), calls=%async_computation.1 | async-start | bytes 14057472 | tf_op jit(solution)/shard_map/all_gather | solution.py:154
  488.3 20.2 %collective-permute-start.35 = (bf16[2,2,2,2,32,128]{5,4,3,2,1,0:T(8,128)(2,1)S(1)}, bf16[2,2,2,2,32,128]{5,4,3,2,1,0:T(8,128)(2,1)S(1)}, u32[]{:S(2)}, u32[]{:S(2)}) collective-permute-start(bf16[2,2,2,2,32,128]{5,4,3,2,1,0:T(8,128)(2,1)S(1)} %fusion.223), channel_id=1, source_target_pairs={{0,8},{1,9},{2,10},{3,11},{4,12},{5,13},{6,14},{7,15},{8,0},{9,1},... | collective-permute-start | bytes 393224 | tf_op jit(solution)/shard_map/ppermute | solution.py:91
  512.3 34.0 %collective-permute-start.15 = (bf16[2,2,2,2,32,1024]{5,4,1,2,0,3:T(8,128)(2,1)}, bf16[2,2,2,2,32,1024]{5,4,1,2,0,3:T(8,128)(2,1)}, u32[]{:S(2)}, u32[]{:S(2)}) collective-permute-start(bf16[2,2,2,2,32,1024]{5,4,1,2,0,3:T(8,128)(2,1)} %bitcast.570), channel_id=1, source_target_pairs={{0,8},{1,9},{2,10},{3,11},{4,12},{5,13},{6,14},{7,15},{8,0},{9,1},... | collective-permute-start | bytes 3145736 | tf_op jit(solution)/shard_map/ppermute | solution.py:91
  516.9 18.1 %collective-permute-start.38 = (bf16[2,32,128]{2,1,0:T(8,128)(2,1)S(1)}, bf16[2,32,128]{2,1,0:T(8,128)(2,1)S(1)}, u32[]{:S(2)}, u32[]{:S(2)}) collective-permute-start(bf16[2,32,128]{2,1,0:T(8,128)(2,1)S(1)} %fusion.229), channel_id=1, source_target_pairs={{0,2},{1,3},{2,0},{3,1},{4,6},{5,7},{6,4},{7,5},{8,10},{9,11},{10,... | collective-permute-start | bytes 49160 | tf_op jit(solution)/shard_map/ppermute | solution.py:91
  526.0 22.7 %collective-permute-start.10 = (bf16[2,2,2,2,32,1024]{5,4,1,2,3,0:T(8,128)(2,1)}, bf16[2,2,2,2,32,1024]{5,4,1,2,3,0:T(8,128)(2,1)}, u32[]{:S(2)}, u32[]{:S(2)}) collective-permute-start(bf16[2,2,2,2,32,1024]{5,4,1,2,3,0:T(8,128)(2,1)} %bitcast.571), channel_id=1, source_target_pairs={{0,8},{1,9},{2,10},{3,11},{4,12},{5,13},{6,14},{7,15},{8,0},{9,1},... | collective-permute-start | bytes 3145736 | tf_op jit(solution)/shard_map/ppermute | solution.py:91
  534.5 85.1 %collective-permute-start.25 = (bf16[2,2,2,2,32,2816]{5,4,1,2,3,0:T(8,128)(2,1)}, bf16[2,2,2,2,32,2816]{5,4,1,2,3,0:T(8,128)(2,1)}, u32[]{:S(2)}, u32[]{:S(2)}) collective-permute-start(bf16[2,2,2,2,32,2816]{5,4,1,2,3,0:T(8,128)(2,1)} %bitcast.568), channel_id=1, source_target_pairs={{0,8},{1,9},{2,10},{3,11},{4,12},{5,13},{6,14},{7,15},{8,0},{9,1},... | collective-permute-start | bytes 8650760 | tf_op jit(solution)/shard_map/ppermute | solution.py:91
  535.0 87.9 %collective-permute-start.20 = (bf16[2,2,2,2,32,2816]{5,4,1,2,0,3:T(8,128)(2,1)}, bf16[2,2,2,2,32,2816]{5,4,1,2,0,3:T(8,128)(2,1)}, u32[]{:S(2)}, u32[]{:S(2)}) collective-permute-start(bf16[2,2,2,2,32,2816]{5,4,1,2,0,3:T(8,128)(2,1)} %bitcast.569), channel_id=1, source_target_pairs={{0,8},{1,9},{2,10},{3,11},{4,12},{5,13},{6,14},{7,15},{8,0},{9,1},... | collective-permute-start | bytes 8650760 | tf_op jit(solution)/shard_map/ppermute | solution.py:91
  535.0 10.3 %collective-permute-start.39 = (bf16[32,128]{1,0:T(8,128)(2,1)S(1)}, bf16[32,128]{1,0:T(8,128)(2,1)S(1)}, u32[]{:S(2)}, u32[]{:S(2)}) collective-permute-start(bf16[32,128]{1,0:T(8,128)(2,1)S(1)} %fusion.231), channel_id=1, source_target_pairs={{0,4},{1,5},{2,6},{3,7},{4,0},{5,1},{6,2},{7,3},{8,12},{9,13},{10,... | collective-permute-start | bytes 24584 | tf_op jit(solution)/shard_map/ppermute | solution.py:91
  548.7 78.0 %collective-permute-start.30 = (bf16[2,2,2,2,88,1024]{5,4,1,2,3,0:T(8,128)(2,1)S(1)}, bf16[2,2,2,2,88,1024]{5,4,1,2,3,0:T(8,128)(2,1)S(1)}, u32[]{:S(2)}, u32[]{:S(2)}) collective-permute-start(bf16[2,2,2,2,88,1024]{5,4,1,2,3,0:T(8,128)(2,1)S(1)} %bitcast.591), channel_id=1, source_target_pairs={{0,8},{1,9},{2,10},{3,11},{4,12},{5,13},{6,14},{7,15},{8,0},{9,1},... | collective-permute-start | bytes 8650760 | tf_op jit(solution)/shard_map/ppermute | solution.py:91
  550.7 14.2 %collective-permute-start.16 = (bf16[2,2,2,32,1024]{4,3,1,2,0:T(8,128)(2,1)S(1)}, bf16[2,2,2,32,1024]{4,3,1,2,0:T(8,128)(2,1)S(1)}, u32[]{:S(2)}, u32[]{:S(2)}) collective-permute-start(bf16[2,2,2,32,1024]{4,3,1,2,0:T(8,128)(2,1)S(1)} %dynamic-slice_bitcast_fusion.6), channel_id=1, source_target_pairs={{0,1},{1,0},{2,3},{3,2},{4,5},{5,4},{6,7},{7,6},{8,9},{9,8},{10,11... | collective-permute-start | bytes 1572872 | tf_op jit(solution)/shard_map/ppermute | solution.py:91
  552.6 13.9 %collective-permute-start.11 = (bf16[2,2,2,32,1024]{4,3,0,1,2:T(8,128)(2,1)S(1)}, bf16[2,2,2,32,1024]{4,3,0,1,2:T(8,128)(2,1)S(1)}, u32[]{:S(2)}, u32[]{:S(2)}) collective-permute-start(bf16[2,2,2,32,1024]{4,3,0,1,2:T(8,128)(2,1)S(1)} %dynamic-slice_bitcast_fusion.7), channel_id=1, source_target_pairs={{0,16},{1,17},{2,18},{3,19},{4,20},{5,21},{6,22},{7,23},{8,24},{9,... | collective-permute-start | bytes 1572872 | tf_op jit(solution)/shard_map/ppermute | solution.py:91
  564.9 13.3 %collective-permute-start.6 = (bf16[2,2,2,32,1024]{4,3,1,2,0:T(8,128)(2,1)S(1)}, bf16[2,2,2,32,1024]{4,3,1,2,0:T(8,128)(2,1)S(1)}, u32[]{:S(2)}, u32[]{:S(2)}) collective-permute-start(bf16[2,2,2,32,1024]{4,3,1,2,0:T(8,128)(2,1)S(1)} %dynamic-slice_bitcast_fusion.8), channel_id=1, source_target_pairs={{0,1},{1,0},{2,3},{3,2},{4,5},{5,4},{6,7},{7,6},{8,9},{9,8},{10,11... | collective-permute-start | bytes 1572872 | tf_op jit(solution)/shard_map/ppermute | solution.py:91
  566.5 13.4 %collective-permute-start.1 = (bf16[2,2,2,32,1024]{4,3,0,1,2:T(8,128)(2,1)S(1)}, bf16[2,2,2,32,1024]{4,3,0,1,2:T(8,128)(2,1)S(1)}, u32[]{:S(2)}, u32[]{:S(2)}) collective-permute-start(bf16[2,2,2,32,1024]{4,3,0,1,2:T(8,128)(2,1)S(1)} %dynamic-slice_bitcast_fusion.9), channel_id=1, source_target_pairs={{0,16},{1,17},{2,18},{3,19},{4,20},{5,21},{6,22},{7,23},{8,24},{9,... | collective-permute-start | bytes 1572872 | tf_op jit(solution)/shard_map/ppermute | solution.py:91
  578.1 7.1 collective-permute-start.17
  579.9 6.4 collective-permute-start.12
  586.3 6.8 collective-permute-start.2
  593.1 7.7 %collective-permute-start.13 = (bf16[2,32,1024]{2,1,0:T(8,128)(2,1)S(1)}, bf16[2,32,1024]{2,1,0:T(8,128)(2,1)S(1)}, u32[]{:S(2)}, u32[]{:S(2)}) collective-permute-start(bf16[2,32,1024]{2,1,0:T(8,128)(2,1)S(1)} %dynamic-slice_bitcast_fusion.21), channel_id=1, source_target_pairs={{0,2},{1,3},{2,0},{3,1},{4,6},{5,7},{6,4},{7,5},{8,10},{9,11},{10,... | collective-permute-start | bytes 393224 | tf_op jit(solution)/shard_map/ppermute | solution.py:91
  603.6 6.9 collective-permute-start.19
  622.4 34.5 %collective-permute-start.26 = (bf16[2,2,2,32,2816]{4,3,0,1,2:T(8,128)(2,1)S(1)}, bf16[2,2,2,32,2816]{4,3,0,1,2:T(8,128)(2,1)S(1)}, u32[]{:S(2)}, u32[]{:S(2)}) collective-permute-start(bf16[2,2,2,32,2816]{4,3,0,1,2:T(8,128)(2,1)S(1)} %dynamic-slice_bitcast_fusion.1), channel_id=1, source_target_pairs={{0,16},{1,17},{2,18},{3,19},{4,20},{5,21},{6,22},{7,23},{8,24},{9,... | collective-permute-start | bytes 4325384 | tf_op jit(solution)/shard_map/ppermute | solution.py:91
  625.6 32.8 %collective-permute-start.21 = (bf16[2,2,2,32,2816]{4,3,1,2,0:T(8,128)(2,1)S(1)}, bf16[2,2,2,32,2816]{4,3,1,2,0:T(8,128)(2,1)S(1)}, u32[]{:S(2)}, u32[]{:S(2)}) collective-permute-start(bf16[2,2,2,32,2816]{4,3,1,2,0:T(8,128)(2,1)S(1)} %dynamic-slice_bitcast_fusion.2), channel_id=1, source_target_pairs={{0,1},{1,0},{2,3},{3,2},{4,5},{5,4},{6,7},{7,6},{8,9},{9,8},{10,11... | collective-permute-start | bytes 4325384 | tf_op jit(solution)/shard_map/ppermute | solution.py:91
  628.3 58.1 %collective-permute-start.31 = (bf16[2,2,2,88,1024]{4,3,0,1,2:T(8,128)(2,1)S(1)}, bf16[2,2,2,88,1024]{4,3,0,1,2:T(8,128)(2,1)S(1)}, u32[]{:S(2)}, u32[]{:S(2)}) collective-permute-start(bf16[2,2,2,88,1024]{4,3,0,1,2:T(8,128)(2,1)S(1)} %dynamic-slice_bitcast_fusion), channel_id=1, source_target_pairs={{0,16},{1,17},{2,18},{3,19},{4,20},{5,21},{6,22},{7,23},{8,24},{9,... | collective-permute-start | bytes 4325384 | tf_op jit(solution)/shard_map/ppermute | solution.py:91
  657.3 30.5 %collective-permute-start.27 = (bf16[2,2,32,2816]{3,2,0,1:T(8,128)(2,1)S(1)}, bf16[2,2,32,2816]{3,2,0,1:T(8,128)(2,1)S(1)}, u32[]{:S(2)}, u32[]{:S(2)}) collective-permute-start(bf16[2,2,32,2816]{3,2,0,1:T(8,128)(2,1)S(1)} %dynamic-slice_bitcast_fusion.4), channel_id=1, source_target_pairs={{0,1},{1,0},{2,3},{3,2},{4,5},{5,4},{6,7},{7,6},{8,9},{9,8},{10,11... | collective-permute-start | bytes 2162696 | tf_op jit(solution)/shard_map/ppermute | solution.py:91
  658.9 35.3 %collective-permute-start.22 = (bf16[2,2,32,2816]{3,2,0,1:T(8,128)(2,1)S(1)}, bf16[2,2,32,2816]{3,2,0,1:T(8,128)(2,1)S(1)}, u32[]{:S(2)}, u32[]{:S(2)}) collective-permute-start(bf16[2,2,32,2816]{3,2,0,1:T(8,128)(2,1)S(1)} %dynamic-slice_bitcast_fusion.5), channel_id=1, source_target_pairs={{0,16},{1,17},{2,18},{3,19},{4,20},{5,21},{6,22},{7,23},{8,24},{9,... | collective-permute-start | bytes 2162696 | tf_op jit(solution)/shard_map/ppermute | solution.py:91
  687.2 11.4 %collective-permute-start.32 = (bf16[2,2,88,1024]{3,2,0,1:T(8,128)(2,1)S(1)}, bf16[2,2,88,1024]{3,2,0,1:T(8,128)(2,1)S(1)}, u32[]{:S(2)}, u32[]{:S(2)}) collective-permute-start(bf16[2,2,88,1024]{3,2,0,1:T(8,128)(2,1)S(1)} %dynamic-slice_bitcast_fusion.3), channel_id=1, source_target_pairs={{0,1},{1,0},{2,3},{3,2},{4,5},{5,4},{6,7},{7,6},{8,9},{9,8},{10,11... | collective-permute-start | bytes 2162696 | tf_op jit(solution)/shard_map/ppermute | solution.py:91
  688.1 14.5 %collective-permute-start.28 = (bf16[2,32,2816]{2,1,0:T(8,128)(2,1)S(1)}, bf16[2,32,2816]{2,1,0:T(8,128)(2,1)S(1)}, u32[]{:S(2)}, u32[]{:S(2)}) collective-permute-start(bf16[2,32,2816]{2,1,0:T(8,128)(2,1)S(1)} %dynamic-slice_bitcast_fusion.11), channel_id=1, source_target_pairs={{0,2},{1,3},{2,0},{3,1},{4,6},{5,7},{6,4},{7,5},{8,10},{9,11},{10,... | collective-permute-start | bytes 1081352 | tf_op jit(solution)/shard_map/ppermute | solution.py:91
  694.4 13.0 %collective-permute-start.23 = (bf16[2,32,2816]{2,1,0:T(8,128)(2,1)S(1)}, bf16[2,32,2816]{2,1,0:T(8,128)(2,1)S(1)}, u32[]{:S(2)}, u32[]{:S(2)}) collective-permute-start(bf16[2,32,2816]{2,1,0:T(8,128)(2,1)S(1)} %dynamic-slice_bitcast_fusion.12), channel_id=1, source_target_pairs={{0,2},{1,3},{2,0},{3,1},{4,6},{5,7},{6,4},{7,5},{8,10},{9,11},{10,... | collective-permute-start | bytes 1081352 | tf_op jit(solution)/shard_map/ppermute | solution.py:91
  698.8 16.2 %collective-permute-start.33 = (bf16[2,88,1024]{2,1,0:T(8,128)(2,1)S(1)}, bf16[2,88,1024]{2,1,0:T(8,128)(2,1)S(1)}, u32[]{:S(2)}, u32[]{:S(2)}) collective-permute-start(bf16[2,88,1024]{2,1,0:T(8,128)(2,1)S(1)} %dynamic-slice_bitcast_fusion.10), channel_id=1, source_target_pairs={{0,2},{1,3},{2,0},{3,1},{4,6},{5,7},{6,4},{7,5},{8,10},{9,11},{10,... | collective-permute-start | bytes 1081352 | tf_op jit(solution)/shard_map/ppermute | solution.py:91
  702.8 13.4 %collective-permute-start.29 = (bf16[32,2816]{1,0:T(8,128)(2,1)S(1)}, bf16[32,2816]{1,0:T(8,128)(2,1)S(1)}, u32[]{:S(2)}, u32[]{:S(2)}) collective-permute-start(bf16[32,2816]{1,0:T(8,128)(2,1)S(1)} %dynamic-slice_bitcast_fusion.18), channel_id=1, source_target_pairs={{0,4},{1,5},{2,6},{3,7},{4,0},{5,1},{6,2},{7,3},{8,12},{9,13},{10,... | collective-permute-start | bytes 540680 | tf_op jit(solution)/shard_map/ppermute | solution.py:91
  707.5 15.3 %collective-permute-start.24 = (bf16[32,2816]{1,0:T(8,128)(2,1)S(1)}, bf16[32,2816]{1,0:T(8,128)(2,1)S(1)}, u32[]{:S(2)}, u32[]{:S(2)}) collective-permute-start(bf16[32,2816]{1,0:T(8,128)(2,1)S(1)} %dynamic-slice_bitcast_fusion.19), channel_id=1, source_target_pairs={{0,4},{1,5},{2,6},{3,7},{4,0},{5,1},{6,2},{7,3},{8,12},{9,13},{10,... | collective-permute-start | bytes 540680 | tf_op jit(solution)/shard_map/ppermute | solution.py:91
  715.2 9.5 %collective-permute-start.34 = (bf16[88,1024]{1,0:T(8,128)(2,1)S(1)}, bf16[88,1024]{1,0:T(8,128)(2,1)S(1)}, u32[]{:S(2)}, u32[]{:S(2)}) collective-permute-start(bf16[88,1024]{1,0:T(8,128)(2,1)S(1)} %dynamic-slice_bitcast_fusion.17), channel_id=1, source_target_pairs={{0,4},{1,5},{2,6},{3,7},{4,0},{5,1},{6,2},{7,3},{8,12},{9,13},{10,... | collective-permute-start | bytes 540680 | tf_op jit(solution)/shard_map/ppermute | solution.py:91
  (152 other events, 1434.6 us)
Sparse Core Ops, SparseCore 0:
  10.9 70.0 all-gather.7
  84.5 68.9 all-gather.3
  156.4 98.4 all-gather.5

commit v2 on v1

--- a/solution.py
+++ b/solution.py
@@ -4,6 +4,8 @@
 import jax
 import jax.numpy as jnp
 from jax import lax
+from jax.experimental import pallas as pl
+from jax.experimental.pallas import tpu as pltpu
 from jax.sharding import PartitionSpec as P
 
 HEADS = 16
@@ -46,23 +48,6 @@
     return (jnp.cos(angles), jnp.sin(angles))
 
 
-def rotate(matrix, cosine, sine, head_count):
-    row_count = matrix.shape[0]
-    halves = matrix.reshape(row_count, head_count, 2, -1)
-    first_half = halves[:, :, 0]
-    second_half = halves[:, :, 1]
-    cos_table = cosine[:, None, :]
-    sin_table = sine[:, None, :]
-    turned = jnp.stack(
-        [
-            first_half * cos_table - second_half * sin_table,
-            second_half * cos_table + first_half * sin_table,
-        ],
-        axis=2,
-    )
-    return turned.reshape(row_count, -1)
-
-
 def allowed_mask(segment, valid):
     slot_places = jnp.arange(segment.shape[0])
     earlier = slot_places[None, :] < slot_places[:, None]
@@ -75,12 +60,261 @@
     return lax.rsqrt(jnp.mean(matrix * matrix, axis=-1, keepdims=True) + EPSILON)
 
 
-def masked_scores(query_heads, key_heads, allowed, score_scale):
-    raw_scores = (
-        jnp.einsum("qhd,khd->hqk", query_heads, key_heads, preferred_element_type=jnp.float32)
-        * score_scale
-    )
-    return jnp.where(allowed[None], raw_scores, -1e30)
+PAIR = 128
+
+
+def swap_halves(matrix, half_size):
+    lane = lax.broadcasted_iota(jnp.int32, matrix.shape, 1)
+    first = lane % (2 * half_size) < half_size
+    width = matrix.shape[1]
+    return jnp.where(
+        first, pltpu.roll(matrix, width - half_size, 1), pltpu.roll(matrix, half_size, 1)
+    )
+
+
+def head_part(matrix, head, head_size):
+    lane = lax.broadcasted_iota(jnp.int32, matrix.shape, 1)
+    return jnp.where(lane // head_size == head, matrix, jnp.zeros_like(matrix))
+
+
+def attend_kernel(
+    slot_count,
+    head_size,
+    x_ref,
+    scale_ref,
+    gain_ref,
+    wq_ref,
+    wk_ref,
+    wv_ref,
+    first_ref,
+    bias_ref,
+    cos_ref,
+    sin_ref,
+    normed_ref,
+    q_ref,
+    k_ref,
+    v_ref,
+    ctx_ref,
+    lse_ref,
+):
+    half_size = head_size // 2
+    score_scale = head_size ** (-0.5)
+    width = q_ref.shape[1]
+    bucket_count = bias_ref.shape[0]
+    query_rows = slot_count // 2
+
+    @pl.when(pl.program_id(0) == 0)
+    def _():
+        normed_ref[...] = (
+            x_ref[...].astype(jnp.float32) * scale_ref[...] * gain_ref[...]
+        ).astype(jnp.bfloat16)
+
+    normed = normed_ref[...]
+    cosine = cos_ref[...]
+    sine = sin_ref[...]
+    for raw_ref, w_ref in ((q_ref, wq_ref), (k_ref, wk_ref)):
+        raw = forward_dot(normed, w_ref[...])
+        for low in range(0, width, PAIR):
+            part = raw[:, low : low + PAIR]
+            raw_ref[:, low : low + PAIR] = (
+                part * cosine + swap_halves(part, half_size) * sine
+            ).astype(jnp.bfloat16)
+    v_ref[...] = (
+        0.5 * forward_dot(normed, wv_ref[...]) + 0.5 * first_ref[...].astype(jnp.float32)
+    ).astype(jnp.bfloat16)
+    for bucket in range(bucket_count):
+        base = bucket * slot_count
+        for low in range(0, width, PAIR):
+            keys = k_ref[base : base + slot_count, low : low + PAIR]
+            queries = q_ref[base : base + slot_count, low : low + PAIR] * score_scale
+            values_t = v_ref[base : base + slot_count, low : low + PAIR].T
+            for start in range(0, slot_count, query_rows):
+                end = start + query_rows
+                parts = []
+                for head in range(PAIR // head_size):
+                    key_head = head_part(keys[:end], head, head_size)
+                    scores = (
+                        contract_last(key_head, queries[start:end])
+                        + bias_ref[bucket, :end, start:end]
+                    )
+                    top = jnp.max(scores, axis=0, keepdims=True)
+                    weights = jnp.exp(scores - top)
+                    mass = jnp.sum(weights, axis=0, keepdims=True)
+                    row = (low // head_size) + head
+                    lse_ref[bucket, 0, row : row + 1, start:end] = top + jnp.log(mass)
+                    mixed = forward_dot(
+                        values_t[head * head_size : (head + 1) * head_size, :end],
+                        weights.astype(jnp.bfloat16),
+                    )
+                    parts.append(mixed * (1.0 / mass))
+                ctx_ref[base + start : base + end, low : low + PAIR] = (
+                    jnp.concatenate(parts, axis=0).T.astype(jnp.bfloat16)
+                )
+
+
+def attend(inputs, scale_one, gain, weights, first_values, bias, cosine, sine, head_size, width):
+    token_count, model_width = inputs.shape
+    bucket_count, slot_count = bias.shape[:2]
+    steps = model_width // width
+    whole = lambda step: (0, 0)
+    block = pl.BlockSpec((token_count, width), lambda step: (0, step))
+    heads = width // head_size
+    table = pl.BlockSpec((token_count, PAIR), whole)
+    low_shape = jax.ShapeDtypeStruct((token_count, model_width), jnp.bfloat16)
+    return pl.pallas_call(
+        partial(attend_kernel, slot_count, head_size),
+        grid=(steps,),
+        in_specs=[
+            pl.BlockSpec((token_count, model_width), whole),
+            pl.BlockSpec((token_count, 1), whole),
+            pl.BlockSpec((1, model_width), whole),
+            pl.BlockSpec((model_width, width), lambda step: (0, step)),
+            pl.BlockSpec((model_width, width), lambda step: (0, steps + step)),
+            pl.BlockSpec((model_width, width), lambda step: (0, 2 * steps + step)),
+            block,
+            pl.BlockSpec((bucket_count, slot_count, slot_count), lambda step: (0, 0, 0)),
+            table,
+            table,
+        ],
+        out_specs=[
+            pl.BlockSpec((token_count, model_width), whole),
+            block,
+            block,
+            block,
+            block,
+            pl.BlockSpec((bucket_count, 1, heads, slot_count), lambda step: (0, step, 0, 0)),
+        ],
+        out_shape=[low_shape] * 5
+        + [jax.ShapeDtypeStruct((bucket_count, steps, heads, slot_count), jnp.float32)],
+        compiler_params=pltpu.CompilerParams(vmem_limit_bytes=56 << 20),
+        name="attend",
+    )(inputs, scale_one, gain, weights, weights, weights, first_values, bias, cosine, sine)
+
+
+def attend_back_kernel(
+    slot_count,
+    head_size,
+    q_ref,
+    k_ref,
+    v_ref,
+    grad_ref,
+    lse_ref,
+    bias_ref,
+    cos_ref,
+    sin_ref,
+    grads_ref,
+    first_ref,
+    dk_ref,
+    dv_ref,
+):
+    half_size = head_size // 2
+    score_scale = head_size ** (-0.5)
+    width = q_ref.shape[1]
+    bucket_count = bias_ref.shape[0]
+    query_rows = slot_count // 2
+    head_count = PAIR // head_size
+    for bucket in range(bucket_count):
+        base = bucket * slot_count
+        cosine = cos_ref[base : base + slot_count]
+        sine = sin_ref[base : base + slot_count]
+        for low in range(0, width, PAIR):
+            keys = k_ref[base : base + slot_count, low : low + PAIR]
+            values = v_ref[base : base + slot_count, low : low + PAIR]
+            queries = q_ref[base : base + slot_count, low : low + PAIR] * score_scale
+            grads = grad_ref[base : base + slot_count, low : low + PAIR]
+            keys_t = keys.T
+            query_parts = []
+            for start in range(0, slot_count, query_rows):
+                end = start + query_rows
+                parts = []
+                for head in range(head_count):
+                    row = (low // head_size) + head
+                    scores = contract_last(
+                        head_part(keys[:end], head, head_size), queries[start:end]
+                    )
+                    probs = jnp.exp(
+                        scores
+                        + bias_ref[bucket, :end, start:end]
+                        - lse_ref[bucket, 0, row : row + 1, start:end]
+                    )
+                    grad_probs = contract_last(
+                        head_part(values[:end], head, head_size), grads[start:end]
+                    )
+                    weighted = probs * grad_probs
+                    grad_scores = (
+                        weighted - probs * jnp.sum(weighted, axis=0, keepdims=True)
+                    ).astype(jnp.bfloat16)
+                    dv = forward_dot(probs.astype(jnp.bfloat16), grads[start:end])
+                    dk = forward_dot(grad_scores, queries[start:end])
+                    if start == 0:
+                        dv_ref[head, :end] = dv
+                        dk_ref[head, :end] = dk
+                    else:
+                        dv_ref[head, :start] += dv[:start]
+                        dk_ref[head, :start] += dk[:start]
+                        dv_ref[head, start:end] = dv[start:]
+                        dk_ref[head, start:end] = dk[start:]
+                    parts.append(
+                        forward_dot(
+                            keys_t[head * head_size : (head + 1) * head_size, :end], grad_scores
+                        )
+                    )
+                query_parts.append((jnp.concatenate(parts, axis=0) * score_scale).T)
+            lane = lax.broadcasted_iota(jnp.int32, (slot_count, PAIR), 1)
+            dv = dv_ref[0]
+            dk = dk_ref[0]
+            for head in range(1, head_count):
+                here = lane // head_size == head
+                dv = jnp.where(here, dv_ref[head], dv)
+                dk = jnp.where(here, dk_ref[head], dk)
+            dq = jnp.concatenate(query_parts, axis=0)
+            rows = slice(base, base + slot_count)
+            for index, part in enumerate((dq, dk)):
+                grads_ref[index, rows, low : low + PAIR] = (
+                    part * cosine - swap_halves(part, half_size) * sine
+                ).astype(jnp.bfloat16)
+            first_ref[rows, low : low + PAIR] = 0.5 * dv
+            grads_ref[2, rows, low : low + PAIR] = (0.5 * dv).astype(jnp.bfloat16)
+
+
+def attend_back(
+    queries, keys, values, grads, lse, bias, cosine, sine, head_size, width, first_step, steps
+):
+    token_count = queries.shape[0]
+    bucket_count, slot_count = bias.shape[:2]
+    heads = width // head_size
+    block = pl.BlockSpec((token_count, width), lambda step: (0, first_step + step))
+    table = pl.BlockSpec((token_count, PAIR), lambda step: (0, 0))
+    return pl.pallas_call(
+        partial(attend_back_kernel, slot_count, head_size),
+        grid=(steps,),
+        in_specs=[
+            block,
+            block,
+            block,
+            block,
+            pl.BlockSpec(
+                (bucket_count, 1, heads, slot_count), lambda step: (0, first_step + step, 0, 0)
+            ),
+            pl.BlockSpec((bucket_count, slot_count, slot_count), lambda step: (0, 0, 0)),
+            table,
+            table,
+        ],
+        out_specs=[
+            pl.BlockSpec((3, token_count, width), lambda step: (0, 0, step)),
+            pl.BlockSpec((token_count, width), lambda step: (0, step)),
+        ],
+        out_shape=[
+            jax.ShapeDtypeStruct((3, token_count, steps * width), jnp.bfloat16),
+            jax.ShapeDtypeStruct((token_count, steps * width), jnp.float32),
+        ],
+        scratch_shapes=[
+            pltpu.VMEM((PAIR // head_size, slot_count, PAIR), jnp.float32),
+            pltpu.VMEM((PAIR // head_size, slot_count, PAIR), jnp.float32),
+        ],
+        compiler_params=pltpu.CompilerParams(vmem_limit_bytes=56 << 20),
+        name="attend_back",
+    )(queries, keys, values, grads, lse, bias, cosine, sine)
 
 
 AXES = ("dp", "fsdp")
@@ -143,9 +377,6 @@
     head_count = HEADS
     head_size = model_width // head_count
     hidden_width = w_gate.shape[1]
-    group_heads = 4
-    group_count = head_count // group_heads
-    score_scale = head_size ** (-0.5)
 
     gains = jnp.pad(jnp.stack([gain_one, gain_two], axis=1), ((0, 0), (0, 126)))
     first_set = lax.all_gather(
@@ -165,49 +396,32 @@
     up_w = second_set[:, model_width + hidden_width :]
 
     inputs = tokens.astype(jnp.float32)
-    first_input = first_values.astype(jnp.float32)
     layouts = [bucket_layout(lengths[index], slot_count) for index in range(micro_count)]
     position = jnp.concatenate([layout[1] for layout in layouts])
     valid = jnp.concatenate([layout[2] for layout in layouts])
     cosine, sine = rope_tables(position, head_size)
-    allowed = [allowed_mask(layout[0], layout[2]) for layout in layouts]
+    cosine = jnp.tile(cosine, (1, 2 * PAIR // head_size))
+    sine = jnp.tile(jnp.concatenate([-sine, sine], axis=1), (1, PAIR // head_size))
+    bias = jnp.stack(
+        [
+            jnp.where(allowed_mask(layout[0], layout[2]).T, 0.0, -1e30).astype(jnp.float32)
+            for layout in layouts
+        ]
+    )
     scale_one = rms_scale(inputs)
-    normed = (inputs * scale_one * gain_first_f).astype(jnp.bfloat16)
-    query_rot = rotate(forward_dot(normed, query_w), cosine, sine, head_count).astype(jnp.bfloat16)
-    key_rot = rotate(forward_dot(normed, key_w), cosine, sine, head_count).astype(jnp.bfloat16)
-    value_mix = (0.5 * forward_dot(normed, value_w) + 0.5 * first_input).astype(jnp.bfloat16)
-    shape = (micro_count, slot_count, head_count, head_size)
-    query_heads = query_rot.reshape(shape)
-    key_heads = key_rot.reshape(shape)
-    value_heads = value_mix.reshape(shape)
-    contexts = []
-    log_masses = []
-    for index in range(micro_count):
-        context_parts = []
-        for group_index in range(group_count):
-            head_lo = group_index * group_heads
-            head_hi = head_lo + group_heads
-            scores = masked_scores(
-                query_heads[index, :, head_lo:head_hi],
-                key_heads[index, :, head_lo:head_hi],
-                allowed[index],
-                score_scale,
-            )
-            top_score = jnp.max(scores, axis=-1, keepdims=True)
-            exp_scores = jnp.exp(scores - top_score)
-            total_mass = jnp.sum(exp_scores, axis=-1, keepdims=True)
-            prob_low = (exp_scores / total_mass).astype(jnp.bfloat16)
-            log_masses.append(top_score + jnp.log(total_mass))
-            context_parts.append(
-                jnp.einsum(
-                    "hqk,khd->qhd",
-                    prob_low,
-                    value_heads[index, :, head_lo:head_hi],
-                    preferred_element_type=jnp.float32,
-                )
-            )
-        contexts.append(jnp.concatenate(context_parts, axis=1).reshape(slot_count, model_width))
-    context = jnp.concatenate(contexts, axis=0).astype(jnp.bfloat16)
+    width = 4 * head_size
+    normed, query_rot, key_rot, value_mix, context, lse = attend(
+        tokens,
+        scale_one,
+        gain_first_f,
+        first_set,
+        first_values,
+        bias,
+        cosine,
+        sine,
+        head_size,
+        width,
+    )
     hidden = inputs + forward_dot(context, out_w)
     scale_two = rms_scale(hidden)
     normed_two = (hidden * scale_two * gain_second_f).astype(jnp.bfloat16)
@@ -243,64 +457,29 @@
     grad_out_w = contract_first(context, grad_hidden_low).astype(jnp.bfloat16)
     grad_out_sum = reduce_rows(grad_out_w, order_b, place, device_count)
     grad_context = contract_last(grad_hidden_low, out_w).astype(jnp.bfloat16)
-    grad_context_heads = grad_context.reshape(shape)
-    value_grads = []
-    query_grads = []
-    key_grads = []
-    for index in range(micro_count):
-        value_grad_parts = []
-        query_grad_parts = []
-        key_grad_parts = []
-        for group_index in range(group_count):
-            head_lo = group_index * group_heads
-            head_hi = head_lo + group_heads
-            query_part = query_heads[index, :, head_lo:head_hi]
-            key_part = key_heads[index, :, head_lo:head_hi]
-            value_part = value_heads[index, :, head_lo:head_hi]
-            context_grad_part = grad_context_heads[index, :, head_lo:head_hi]
-            scores_again = masked_scores(query_part, key_part, allowed[index], score_scale)
-            prob_full = jnp.exp(scores_again - log_masses[index * group_count + group_index])
-            prob_again = prob_full.astype(jnp.bfloat16)
-            value_grad_parts.append(
-                jnp.einsum(
-                    "hqk,qhd->khd",
-                    prob_again,
-                    context_grad_part,
-                    preferred_element_type=jnp.float32,
-                )
-            )
-            grad_probs = jnp.einsum(
-                "qhd,khd->hqk", context_grad_part, value_part, preferred_element_type=jnp.float32
-            )
-            grad_scores = prob_full * (
-                grad_probs - jnp.sum(prob_full * grad_probs, axis=-1, keepdims=True)
-            )
-            grad_scores_low = grad_scores.astype(jnp.bfloat16)
-            query_grad_parts.append(
-                jnp.einsum(
-                    "hqk,khd->qhd", grad_scores_low, key_part, preferred_element_type=jnp.float32
-                )
-                * score_scale
-            )
-            key_grad_parts.append(
-                jnp.einsum(
-                    "hqk,qhd->khd", grad_scores_low, query_part, preferred_element_type=jnp.float32
-                )
-                * score_scale
-            )
-        flat = (slot_count, model_width)
-        value_grads.append(jnp.concatenate(value_grad_parts, axis=1).reshape(flat))
-        query_grads.append(jnp.concatenate(query_grad_parts, axis=1).reshape(flat))
-        key_grads.append(jnp.concatenate(key_grad_parts, axis=1).reshape(flat))
-    grad_value_full = jnp.concatenate(value_grads, axis=0)
-    grad_query_low = rotate(
-        jnp.concatenate(query_grads, axis=0), cosine, -sine, head_count
-    ).astype(jnp.bfloat16)
-    grad_key_low = rotate(jnp.concatenate(key_grads, axis=0), cosine, -sine, head_count).astype(
-        jnp.bfloat16
-    )
-    grad_first = 0.5 * grad_value_full
-    grad_value_low = grad_first.astype(jnp.bfloat16)
+    steps = model_width // width
+    half_steps = steps // 2
+    halves = [
+        attend_back(
+            query_rot,
+            key_rot,
+            value_mix,
+            grad_context,
+            lse,
+            bias,
+            cosine,
+            sine,
+            head_size,
+            width,
+            half * half_steps,
+            half_steps,
+        )
+        for half in range(2)
+    ]
+    grad_first = jnp.concatenate([half[1] for half in halves], axis=1)
+    grad_query_low, grad_key_low, grad_value_low = [
+        jnp.concatenate([half[0][index] for half in halves], axis=1) for index in range(3)
+    ]
     grad_query_w = contract_first(normed, grad_query_low).astype(jnp.bfloat16)
     grad_key_w = contract_first(normed, grad_key_low).astype(jnp.bfloat16)
     grad_value_w = contract_first(normed, grad_value_low).astype(jnp.bfloat16)

time: 742 us -> 680 us (0.916)
  matrix products: 229 us -> 154 us
  Pallas kernels: 0 us -> 71.4 us
  local copies, waits for them, and re-layouts: 124 us -> 54.1 us
  waiting for transfers between devices: 256 us -> 308 us
  other arithmetic: 71.9 us -> 38.5 us
    dot_general x48 -> x0, matrix products: 75.3 us -> none  [the longest x8 30.5 us: shards(): jnp.einsum('hqk,qhd->khd', prob_again, context_grad_part, preferred_eleme...]
    pallas_call x0 -> x3, Pallas kernels: none -> 71.4 us  [the longest x1 37.2 us: attend(): pl.pallas_call(partial(attend_kernel, slot_count, head_size), grid=(steps...]
    all_gather x1, waiting for transfers between devices: 10.4 us -> 62.9 us  [shards(): lax.all_gather(jnp.concatenate([w_out, w_gate, w_up], axis=1), AXES, axis...]
    unnamed x304 -> x81, local copies, waits for them, and re-layouts: 47 us -> 24.2 us
    slice x4 -> x0, local copies, waits for them, and re-layouts: 21.8 us -> none  [the longest x1 6.08 us: shards(): query_heads[index, :, head_lo:head_hi]]
    reshape x4 -> x1, local copies, waits for them, and re-layouts: 16.5 us -> 0.76 us  [the longest x1 6.36 us: shards(): value_heads = value_mix.reshape(shape)]
    dot_general x7 -> x4, matrix products: 62.6 us -> 51.9 us  [forward_dot(): return jnp.dot(left, right, preferred_element_type=jnp.float32)]
    convert_element_type x8 -> x0, other arithmetic: 10.1 us -> none  [shards(): grad_scores_low = grad_scores.astype(jnp.bfloat16)]
  transfers between devices with their start and end apart: 43 -> 43, of which waited for: 28 -> 29; matrix products, arithmetic and copies ran while one was open for 26% -> 17% of each run, Pallas kernels for 0% -> 6%
where the time goes in v2:
time: 680 us; the launch traced here: 674 us
  waiting for transfers between devices  308 us (45%)
  matrix products  154 us (23%)
  Pallas kernels  71.4 us (11%)
  local copies, waits for them, and re-layouts  54.1 us (8%)
  other arithmetic  38.5 us (6%)
  starting transfers between devices  33.1 us (5%)
  between operations  15 us (2%)
    ppermute x40, waiting for transfers between devices, flip(): return lax.ppermute(value, AXES, pairs)  133 us
    all_gather x1, waiting for transfers between devices, shards(): lax.all_gather(jnp.concatenate([w_out, w_gate, w_up], axis=1), AXES, axis...  62.9 us
    all_gather x1, waiting for transfers between devices, shards(): lax.all_gather(jnp.concatenate([w_query, w_key, w_value, gains], axis=1),...  60.6 us
    dot_general x7, matrix products, contract_last(): lax.dot_general(left, right, (((1,), (1,)), ((), ())), preferred_element_...  57.1 us
    dot_general x4, matrix products, forward_dot(): return jnp.dot(left, right, preferred_element_type=jnp.float32)  51.9 us
    all_gather x1, waiting for transfers between devices, shards(): down_w = lax.all_gather(w_down, AXES, axis=0, tiled=True)  51.4 us
    dot_general x7, matrix products, contract_first(): lax.dot_general(left, right, (((0,), (0,)), ((), ())), preferred_element_...  45 us
    pallas_call x1, Pallas kernels, attend(): pl.pallas_call(partial(attend_kernel, slot_count, head_size), grid=(steps...  37.2 us
  transfers between devices with their start and end apart: 43, of which 29 were waited for; matrix products, arithmetic and copies ran while one was open for 17% of the time, Pallas kernels for 6%

profile of v2, /device:TPU:0, one launch (start us, length us, event | category | flops | bytes accessed | tf_op | source)
XLA Modules:
  0.0 674.4 jit_solution(3414959936885391462)
XLA Ops:
  22.3 4.0 copy.158
  29.6 51.4 %all-gather.8.cloned.1.call-done = bf16[2816,1024]{1,0:T(8,128)(2,1)} async-done(((bf16[88,1024]{1,0:T(8,128)(2,1)}), bf16[2816,1024]{1,0:T(8,128)(2,1)}) %all-gather.8.cloned.1.call-update) | async-done | bytes 5767184 | tf_op jit(solution)/shard_map/all_gather | solution.py:388
  81.0 11.9 %fusion.38 = f32[1024,2816]{1,0:T(8,128)} fusion(bf16[2816,1024]{1,0:T(8,128)(2,1)} %all-gather.8.cloned.1.call-done, bf16[1024,1024]{0,1:T(8,128)(2,1)} %copy.158, f32[1024]{0:T(1024)S(1)} %add_convert_fusion.2), kind=kOutput, calls=%fused_computation.81 | convolution fusion | flops 5908725760 | bytes 19402752 | tf_op jit(solution)/shard_map/dot_general | solution.py:22
  92.9 60.6 %all-gather.4.cloned.1.call-done.wq_ref.wk_ref.wv_ref = bf16[1024,3200]{1,0:T(8,128)(2,1)} async-done(((bf16[32,3200]{1,0:T(8,128)(2,1)}), bf16[1024,3200]{1,0:T(8,128)(2,1)}) %all-gather.4.cloned.1.call-update) | async-done | bytes 6553616 | tf_op jit(solution)/shard_map/all_gather | solution.py:382
  155.5 37.2 %attend.1 = (bf16[1024,1024]{1,0:T(8,128)(2,1)}, bf16[1024,1024]{1,0:T(8,128)(2,1)}, bf16[1024,1024]{1,0:T(8,128)(2,1)}, bf16[1024,1024]{1,0:T(8,128)(2,1)}, bf1...) custom-call(bf16[1024,1024]{1,0:T(8,128)(2,1)} %x_ref.1, f32[1024,1]{1,0:T(8,128)} %copy.154.scale_ref, ...), custom_call_target="tpu_custom_call" | custom-call | tf_op jit(solution)/shard_map/attend/pallas_call | solution.py:164
  192.7 62.9 %all-gather.6.cloned.1.call-done = bf16[1024,6656]{1,0:T(8,128)(2,1)} async-done(((bf16[32,6656]{1,0:T(8,128)(2,1)}), bf16[1024,6656]{1,0:T(8,128)(2,1)}) %all-gather.6.cloned.1.call-update) | async-done | bytes 13631504 | tf_op jit(solution)/shard_map/all_gather | solution.py:385
  255.7 4.8 multiply_reduce_fusion.2
  264.3 11.7 %fusion.6 = f32[1024,2816]{1,0:T(8,128)} fusion(bf16[1024,1024]{0,1:T(8,128)(2,1)S(1)} %multiply_convert_fusion.3, bf16[1024,6656]{1,0:T(8,128)(2,1)} %all-gather.6.cloned.1.call-done), kind=kOutput, calls=%fused_computation.21 | convolution fusion | flops 5905580032 | bytes 19398656 | tf_op jit(solution)/shard_map/dot_general | solution.py:18
  275.9 23.1 %multiply_convert_fusion.1 = (bf16[1024,2816]{1,0:T(8,128)(2,1)}, bf16[1024,2816]{1,0:T(8,128)(2,1)}, bf16[1024,2816]{1,0:T(8,128)(2,1)}) fusion(f32[1024,2816]{1,0:T(8,128)} %fusion.38, f32[1024,2816]{1,0:T(8,128)} %fusion.6, bf16[1024,1024]{0,1:T(8,128)(2,1)} %copy-done.18, bf16[1024,6656]{1,0:T(8,128)(2,1)} %all-gather.6.cloned.1.call-done), kind=kOutput, calls=%fused_computation.1 | convolution fusion | flops 5948833792 | bytes 48234496 | tf_op jit(solution)/shard_map/dot_general | solution.py:18
  299.1 19.8 %fusion.4 = f32[1024,1024]{0,1:T(8,128)S(1)} fusion(bf16[1024,2816]{1,0:T(8,128)(2,1)} %get-tuple-element.105, bf16[1024,6656]{1,0:T(8,128)(2,1)} %all-gather.6.cloned.1.call-done), kind=kOutput, calls=%fused_computation.19 | convolution fusion | flops 5905580032 | bytes 15728640 | tf_op jit(solution)/shard_map/dot_general | solution.py:22
  318.9 9.0 %multiply_reduce_fusion = (f32[1024]{0:T(1024)S(1)}, f32[1024]{0:T(1024)S(1)}, f32[1024,1024]{0,1:T(8,128)S(1)}) fusion(f32[1024,1024]{0,1:T(8,128)S(1)} %copy-done.1, f32[1024]{0:T(1024)S(1)} %get-tuple-element.133, f32[1024]{0:T(1024)S(1)} %get-tuple-element.94, f32[1024,1024]{0,1:T(8,128)S(1)} %fusion.4, bf16[1024,2816]{1,0:T(8,128)(2,1)S(1)} %copy-done.33, ...), kind=kOutput, calls=%fused_computation.34 | convolution fusion | flops 5912918016 | bytes 24133632 | tf_op jit(solution)/shard_map/dot_general | solution.py:22
  329.1 6.8 %convolution_convert_fusion.7.grad_ref = bf16[1024,1024]{1,0:T(8,128)(2,1)} fusion(bf16[1024,6656]{1,0:T(8,128)(2,1)} %all-gather.6.cloned.1.call-done, f32[1024,1024]{0,1:T(8,128)S(1)} %multiply_subtract_fusion), kind=kOutput, calls=%fused_computation.78 | convolution fusion | flops 2149580800 | bytes 8388608 | tf_op jit(solution)/shard_map/dot_general | solution.py:22
  335.9 16.9 %attend_back.2 = (bf16[3,1024,512]{2,1,0:T(8,128)(2,1)}, f32[1024,512]{1,0:T(8,128)}) custom-call(bf16[1024,1024]{1,0:T(8,128)(2,1)} %get-tuple-element.23.q_ref, bf16[1024,1024]{1,0:T(8,128)(2,1)} %get-tuple-element.24.k_ref, bf16[1024,1024]{1,0:T(8,128)(2,1)} %get-tuple-element.25.v_ref, bf16[1024,1024]{1,0:T(8,128)(2,1)} %convolution_convert_fusion.7.grad_ref, ...), custom_call_target="tpu_custom_call" | custom-call | tf_op jit(solution)/shard_map/attend_back/pallas_call | solution.py:288
  352.8 17.3 %attend_back.3 = (bf16[3,1024,512]{2,1,0:T(8,128)(2,1)}, f32[1024,512]{1,0:T(8,128)}) custom-call(bf16[1024,1024]{1,0:T(8,128)(2,1)} %get-tuple-element.23.q_ref, bf16[1024,1024]{1,0:T(8,128)(2,1)} %get-tuple-element.24.k_ref, bf16[1024,1024]{1,0:T(8,128)(2,1)} %get-tuple-element.25.v_ref, bf16[1024,1024]{1,0:T(8,128)(2,1)} %convolution_convert_fusion.7.grad_ref, ...), custom_call_target="tpu_custom_call" | custom-call | tf_op jit(solution)/shard_map/attend_back/pallas_call | solution.py:288
  370.2 11.0 %convolution_convert_fusion.1 = bf16[1024,2816]{1,0:T(8,128)(2,1)} fusion(bf16[1024,1024]{0,1:T(8,128)(2,1)} %copy-done.18, bf16[1024,2816]{1,0:T(8,128)(2,1)} %get-tuple-element.105), kind=kOutput, calls=%fused_computation.17 | convolution fusion | flops 5908463616 | bytes 13631488 | tf_op jit(solution)/shard_map/dot_general | solution.py:28
  381.1 10.9 %convolution_convert_fusion.2 = bf16[1024,2816]{1,0:T(8,128)(2,1)} fusion(bf16[1024,1024]{0,1:T(8,128)(2,1)S(1)} %copy-done.19, bf16[1024,2816]{1,0:T(8,128)(2,1)} %get-tuple-element.104), kind=kOutput, calls=%fused_computation.18 | convolution fusion | flops 5908463616 | bytes 13631488 | tf_op jit(solution)/shard_map/dot_general | solution.py:28
  411.0 4.9 fusion.17
  417.0 9.4 %convolution_convert_fusion = bf16[2816,1024]{1,0:T(8,128)(2,1)S(1)} fusion(bf16[1024,2816]{1,0:T(8,128)(2,1)} %get-tuple-element.106, bf16[1024,1024]{0,1:T(8,128)(2,1)} %copy.158, f32[1024]{0:T(1024)S(1)} %add_convert_fusion.2), kind=kOutput, calls=%fused_computation.16 | convolution fusion | flops 5911609344 | bytes 13635584 | tf_op jit(solution)/shard_map/dot_general | solution.py:28
  431.4 4.8 constant_dynamic-slice_fusion.7
  447.8 12.3 %add_convert_fusion = bf16[1024,1024]{0,1:T(8,128)(2,1)} fusion(f32[1024,1024]{0,1:T(8,128)S(1)} %copy-done.2, bf16[1024,2816]{1,0:T(8,128)(2,1)} %get-tuple-element.106, bf16[2816,1024]{1,0:T(8,128)(2,1)} %all-gather.8.cloned.1.call-done), kind=kOutput, calls=%fused_computation.40 | convolution fusion | flops 5907677184 | bytes 17825792 | tf_op jit(solution)/shard_map/dot_general | solution.py:18
  481.8 5.3 copy.184
  487.1 4.1 copy.183
  499.7 11.2 %collective-permute-done.16 = bf16[2,2,2,32,1024]{4,3,1,2,0:T(8,128)(2,1)S(1)} collective-permute-done((bf16[2,2,2,32,1024]{4,3,1,2,0:T(8,128)(2,1)S(1)}, bf16[2,2,2,32,1024]{4,3,1,2,0:T(8,128)(2,1)S(1)}, u32[]{:S(2)}, u32[]{:S(2)}) %collective-permute-start.16) | collective-permute-done | bytes 524320 | tf_op jit(solution)/shard_map/ppermute | solution.py:325
  513.4 10.7 %collective-permute-done.6 = bf16[2,2,2,32,1024]{4,3,1,2,0:T(8,128)(2,1)S(1)} collective-permute-done((bf16[2,2,2,32,1024]{4,3,1,2,0:T(8,128)(2,1)S(1)}, bf16[2,2,2,32,1024]{4,3,1,2,0:T(8,128)(2,1)S(1)}, u32[]{:S(2)}, u32[]{:S(2)}) %collective-permute-start.6) | collective-permute-done | bytes 524320 | tf_op jit(solution)/shard_map/ppermute | solution.py:325
  526.8 4.5 collective-permute-done.17
  533.4 4.3 collective-permute-done.7
  540.0 4.0 collective-permute-done.18
  574.7 28.2 %collective-permute-done.31 = bf16[2,2,2,88,1024]{4,3,0,1,2:T(8,128)(2,1)S(1)} collective-permute-done((bf16[2,2,2,88,1024]{4,3,0,1,2:T(8,128)(2,1)S(1)}, bf16[2,2,2,88,1024]{4,3,0,1,2:T(8,128)(2,1)S(1)}, u32[]{:S(2)}, u32[]{:S(2)}) %collective-permute-start.31) | collective-permute-done | bytes 1441824 | tf_op jit(solution)/shard_map/ppermute | solution.py:325
  604.1 24.9 %collective-permute-done.26 = bf16[2,2,2,32,2816]{4,3,0,1,2:T(8,128)(2,1)S(1)} collective-permute-done((bf16[2,2,2,32,2816]{4,3,0,1,2:T(8,128)(2,1)S(1)}, bf16[2,2,2,32,2816]{4,3,0,1,2:T(8,128)(2,1)S(1)}, u32[]{:S(2)}, u32[]{:S(2)}) %collective-permute-start.26) | collective-permute-done | bytes 1441824 | tf_op jit(solution)/shard_map/ppermute | solution.py:325
  632.9 7.9 %collective-permute-done.27 = bf16[2,2,32,2816]{3,2,0,1:T(8,128)(2,1)S(1)} collective-permute-done((bf16[2,2,32,2816]{3,2,0,1:T(8,128)(2,1)S(1)}, bf16[2,2,32,2816]{3,2,0,1:T(8,128)(2,1)S(1)}, u32[]{:S(2)}, u32[]{:S(2)}) %collective-permute-start.27) | collective-permute-done | bytes 720928 | tf_op jit(solution)/shard_map/ppermute | solution.py:325
  646.5 4.3 collective-permute-done.28
  653.1 6.3 collective-permute-done.23
  (289 shorter events, 152.8 us)
Async XLA Ops:
  7.2 73.9 %all-gather.8.cloned.1.call-start = ((), (), s32[]{:S(2)}) async-start(), calls=%async_computation.2 | async-start | bytes 5947392 | tf_op jit(solution)/shard_map/all_gather | solution.py:388
  7.9 145.6 %all-gather.4.cloned.1.call-start = ((), (), s32[]{:S(2)}) async-start(), calls=%async_computation | async-start | bytes 6758400 | tf_op jit(solution)/shard_map/all_gather | solution.py:382
  10.4 245.3 %all-gather.6.cloned.1.call-start = ((), (), s32[]{:S(2)}) async-start(), calls=%async_computation.1 | async-start | bytes 14057472 | tf_op jit(solution)/shard_map/all_gather | solution.py:385
  416.7 45.9 %collective-permute-start.35 = (bf16[2,2,2,2,32,128]{5,4,3,2,1,0:T(8,128)(2,1)S(1)}, bf16[2,2,2,2,32,128]{5,4,3,2,1,0:T(8,128)(2,1)S(1)}, u32[]{:S(2)}, u32[]{:S(2)}) collective-permute-start(bf16[2,2,2,2,32,128]{5,4,3,2,1,0:T(8,128)(2,1)S(1)} %fusion.73), channel_id=1, source_target_pairs={{0,8},{1,9},{2,10},{3,11},{4,12},{5,13},{6,14},{7,15},{8,0},{9,1},... | collective-permute-start | bytes 393224 | tf_op jit(solution)/shard_map/ppermute | solution.py:325
  431.2 133.7 %collective-permute-start.30 = (bf16[2,2,2,2,88,1024]{5,4,1,2,3,0:T(8,128)(2,1)}, bf16[2,2,2,2,88,1024]{5,4,1,2,3,0:T(8,128)(2,1)}, u32[]{:S(2)}, u32[]{:S(2)}) collective-permute-start(bf16[2,2,2,2,88,1024]{5,4,1,2,3,0:T(8,128)(2,1)} %bitcast.276), channel_id=1, source_target_pairs={{0,8},{1,9},{2,10},{3,11},{4,12},{5,13},{6,14},{7,15},{8,0},{9,1},... | collective-permute-start | bytes 8650760 | tf_op jit(solution)/shard_map/ppermute | solution.py:325
  438.0 130.6 %collective-permute-start.25 = (bf16[2,2,2,2,32,2816]{5,4,1,2,3,0:T(8,128)(2,1)}, bf16[2,2,2,2,32,2816]{5,4,1,2,3,0:T(8,128)(2,1)}, u32[]{:S(2)}, u32[]{:S(2)}) collective-permute-start(bf16[2,2,2,2,32,2816]{5,4,1,2,3,0:T(8,128)(2,1)} %bitcast.277), channel_id=1, source_target_pairs={{0,8},{1,9},{2,10},{3,11},{4,12},{5,13},{6,14},{7,15},{8,0},{9,1},... | collective-permute-start | bytes 8650760 | tf_op jit(solution)/shard_map/ppermute | solution.py:325
  441.0 51.0 %collective-permute-start.15 = (bf16[2,2,2,2,32,1024]{5,4,1,2,0,3:T(8,128)(2,1)}, bf16[2,2,2,2,32,1024]{5,4,1,2,0,3:T(8,128)(2,1)}, u32[]{:S(2)}, u32[]{:S(2)}) collective-permute-start(bf16[2,2,2,2,32,1024]{5,4,1,2,0,3:T(8,128)(2,1)} %bitcast.279), channel_id=1, source_target_pairs={{0,8},{1,9},{2,10},{3,11},{4,12},{5,13},{6,14},{7,15},{8,0},{9,1},... | collective-permute-start | bytes 3145736 | tf_op jit(solution)/shard_map/ppermute | solution.py:325
  443.4 51.2 %collective-permute-start.10 = (bf16[2,2,2,2,32,1024]{5,4,1,2,3,0:T(8,128)(2,1)}, bf16[2,2,2,2,32,1024]{5,4,1,2,3,0:T(8,128)(2,1)}, u32[]{:S(2)}, u32[]{:S(2)}) collective-permute-start(bf16[2,2,2,2,32,1024]{5,4,1,2,3,0:T(8,128)(2,1)} %bitcast.280), channel_id=1, source_target_pairs={{0,8},{1,9},{2,10},{3,11},{4,12},{5,13},{6,14},{7,15},{8,0},{9,1},... | collective-permute-start | bytes 3145736 | tf_op jit(solution)/shard_map/ppermute | solution.py:325
  474.8 16.4 %collective-permute-start.39 = (bf16[32,128]{1,0:T(8,128)(2,1)S(1)}, bf16[32,128]{1,0:T(8,128)(2,1)S(1)}, u32[]{:S(2)}, u32[]{:S(2)}) collective-permute-start(bf16[32,128]{1,0:T(8,128)(2,1)S(1)} %fusion.81), channel_id=1, source_target_pairs={{0,4},{1,5},{2,6},{3,7},{4,0},{5,1},{6,2},{7,3},{8,12},{9,13},{10,... | collective-permute-start | bytes 24584 | tf_op jit(solution)/shard_map/ppermute | solution.py:325
  492.0 6.5 collective-permute-start
  494.7 78.6 %collective-permute-start.20 = (bf16[2,2,2,2,32,2816]{5,4,1,2,0,3:T(8,128)(2,1)S(1)}, bf16[2,2,2,2,32,2816]{5,4,1,2,0,3:T(8,128)(2,1)S(1)}, u32[]{:S(2)}, u32[]{:S(2)}) collective-permute-start(bf16[2,2,2,2,32,2816]{5,4,1,2,0,3:T(8,128)(2,1)S(1)} %bitcast.290), channel_id=1, source_target_pairs={{0,8},{1,9},{2,10},{3,11},{4,12},{5,13},{6,14},{7,15},{8,0},{9,1},... | collective-permute-start | bytes 8650760 | tf_op jit(solution)/shard_map/ppermute | solution.py:325
  496.5 14.3 %collective-permute-start.16 = (bf16[2,2,2,32,1024]{4,3,1,2,0:T(8,128)(2,1)S(1)}, bf16[2,2,2,32,1024]{4,3,1,2,0:T(8,128)(2,1)S(1)}, u32[]{:S(2)}, u32[]{:S(2)}) collective-permute-start(bf16[2,2,2,32,1024]{4,3,1,2,0:T(8,128)(2,1)S(1)} %dynamic-slice_bitcast_fusion.6), channel_id=1, source_target_pairs={{0,1},{1,0},{2,3},{3,2},{4,5},{5,4},{6,7},{7,6},{8,9},{9,8},{10,11... | collective-permute-start | bytes 1572872 | tf_op jit(solution)/shard_map/ppermute | solution.py:325
  498.5 14.0 %collective-permute-start.11 = (bf16[2,2,2,32,1024]{4,3,0,1,2:T(8,128)(2,1)S(1)}, bf16[2,2,2,32,1024]{4,3,0,1,2:T(8,128)(2,1)S(1)}, u32[]{:S(2)}, u32[]{:S(2)}) collective-permute-start(bf16[2,2,2,32,1024]{4,3,0,1,2:T(8,128)(2,1)S(1)} %dynamic-slice_bitcast_fusion.7), channel_id=1, source_target_pairs={{0,16},{1,17},{2,18},{3,19},{4,20},{5,21},{6,22},{7,23},{8,24},{9,... | collective-permute-start | bytes 1572872 | tf_op jit(solution)/shard_map/ppermute | solution.py:325
  510.8 13.4 %collective-permute-start.6 = (bf16[2,2,2,32,1024]{4,3,1,2,0:T(8,128)(2,1)S(1)}, bf16[2,2,2,32,1024]{4,3,1,2,0:T(8,128)(2,1)S(1)}, u32[]{:S(2)}, u32[]{:S(2)}) collective-permute-start(bf16[2,2,2,32,1024]{4,3,1,2,0:T(8,128)(2,1)S(1)} %dynamic-slice_bitcast_fusion.8), channel_id=1, source_target_pairs={{0,1},{1,0},{2,3},{3,2},{4,5},{5,4},{6,7},{7,6},{8,9},{9,8},{10,11... | collective-permute-start | bytes 1572872 | tf_op jit(solution)/shard_map/ppermute | solution.py:325
  512.5 13.4 %collective-permute-start.1 = (bf16[2,2,2,32,1024]{4,3,0,1,2:T(8,128)(2,1)S(1)}, bf16[2,2,2,32,1024]{4,3,0,1,2:T(8,128)(2,1)S(1)}, u32[]{:S(2)}, u32[]{:S(2)}) collective-permute-start(bf16[2,2,2,32,1024]{4,3,0,1,2:T(8,128)(2,1)S(1)} %dynamic-slice_bitcast_fusion.9), channel_id=1, source_target_pairs={{0,16},{1,17},{2,18},{3,19},{4,20},{5,21},{6,22},{7,23},{8,24},{9,... | collective-permute-start | bytes 1572872 | tf_op jit(solution)/shard_map/ppermute | solution.py:325
  524.2 7.1 %collective-permute-start.17 = (bf16[2,2,32,1024]{3,2,0,1:T(8,128)(2,1)S(1)}, bf16[2,2,32,1024]{3,2,0,1:T(8,128)(2,1)S(1)}, u32[]{:S(2)}, u32[]{:S(2)}) collective-permute-start(bf16[2,2,32,1024]{3,2,0,1:T(8,128)(2,1)S(1)} %dynamic-slice_bitcast_fusion.13), channel_id=1, source_target_pairs={{0,16},{1,17},{2,18},{3,19},{4,20},{5,21},{6,22},{7,23},{8,24},{9,... | collective-permute-start | bytes 786440 | tf_op jit(solution)/shard_map/ppermute | solution.py:325
  525.9 6.6 collective-permute-start.12
  532.5 6.4 collective-permute-start.2
  539.0 7.8 %collective-permute-start.13 = (bf16[2,32,1024]{2,1,0:T(8,128)(2,1)S(1)}, bf16[2,32,1024]{2,1,0:T(8,128)(2,1)S(1)}, u32[]{:S(2)}, u32[]{:S(2)}) collective-permute-start(bf16[2,32,1024]{2,1,0:T(8,128)(2,1)S(1)} %dynamic-slice_bitcast_fusion.21), channel_id=1, source_target_pairs={{0,2},{1,3},{2,0},{3,1},{4,6},{5,7},{6,4},{7,5},{8,10},{9,11},{10,... | collective-permute-start | bytes 393224 | tf_op jit(solution)/shard_map/ppermute | solution.py:325
  549.7 7.0 %collective-permute-start.19 = (bf16[32,1024]{1,0:T(8,128)(2,1)S(1)}, bf16[32,1024]{1,0:T(8,128)(2,1)S(1)}, u32[]{:S(2)}, u32[]{:S(2)}) collective-permute-start(bf16[32,1024]{1,0:T(8,128)(2,1)S(1)} %dynamic-slice_bitcast_fusion.25), channel_id=1, source_target_pairs={{0,4},{1,5},{2,6},{3,7},{4,0},{5,1},{6,2},{7,3},{8,12},{9,13},{10,... | collective-permute-start | bytes 196616 | tf_op jit(solution)/shard_map/ppermute | solution.py:325
  568.4 34.5 %collective-permute-start.31 = (bf16[2,2,2,88,1024]{4,3,0,1,2:T(8,128)(2,1)S(1)}, bf16[2,2,2,88,1024]{4,3,0,1,2:T(8,128)(2,1)S(1)}, u32[]{:S(2)}, u32[]{:S(2)}) collective-permute-start(bf16[2,2,2,88,1024]{4,3,0,1,2:T(8,128)(2,1)S(1)} %dynamic-slice_bitcast_fusion), channel_id=1, source_target_pairs={{0,16},{1,17},{2,18},{3,19},{4,20},{5,21},{6,22},{7,23},{8,24},{9,... | collective-permute-start | bytes 4325384 | tf_op jit(solution)/shard_map/ppermute | solution.py:325
  571.3 57.7 %collective-permute-start.26 = (bf16[2,2,2,32,2816]{4,3,0,1,2:T(8,128)(2,1)S(1)}, bf16[2,2,2,32,2816]{4,3,0,1,2:T(8,128)(2,1)S(1)}, u32[]{:S(2)}, u32[]{:S(2)}) collective-permute-start(bf16[2,2,2,32,2816]{4,3,0,1,2:T(8,128)(2,1)S(1)} %dynamic-slice_bitcast_fusion.1), channel_id=1, source_target_pairs={{0,16},{1,17},{2,18},{3,19},{4,20},{5,21},{6,22},{7,23},{8,24},{9,... | collective-permute-start | bytes 4325384 | tf_op jit(solution)/shard_map/ppermute | solution.py:325
  574.2 56.5 %collective-permute-start.21 = (bf16[2,2,2,32,2816]{4,3,1,2,0:T(8,128)(2,1)S(1)}, bf16[2,2,2,32,2816]{4,3,1,2,0:T(8,128)(2,1)S(1)}, u32[]{:S(2)}, u32[]{:S(2)}) collective-permute-start(bf16[2,2,2,32,2816]{4,3,1,2,0:T(8,128)(2,1)S(1)} %dynamic-slice_bitcast_fusion.2), channel_id=1, source_target_pairs={{0,1},{1,0},{2,3},{3,2},{4,5},{5,4},{6,7},{7,6},{8,9},{9,8},{10,11... | collective-permute-start | bytes 4325384 | tf_op jit(solution)/shard_map/ppermute | solution.py:325
  603.6 27.6 %collective-permute-start.32 = (bf16[2,2,88,1024]{3,2,0,1:T(8,128)(2,1)S(1)}, bf16[2,2,88,1024]{3,2,0,1:T(8,128)(2,1)S(1)}, u32[]{:S(2)}, u32[]{:S(2)}) collective-permute-start(bf16[2,2,88,1024]{3,2,0,1:T(8,128)(2,1)S(1)} %dynamic-slice_bitcast_fusion.3), channel_id=1, source_target_pairs={{0,1},{1,0},{2,3},{3,2},{4,5},{5,4},{6,7},{7,6},{8,9},{9,8},{10,11... | collective-permute-start | bytes 2162696 | tf_op jit(solution)/shard_map/ppermute | solution.py:325
  629.4 11.4 %collective-permute-start.27 = (bf16[2,2,32,2816]{3,2,0,1:T(8,128)(2,1)S(1)}, bf16[2,2,32,2816]{3,2,0,1:T(8,128)(2,1)S(1)}, u32[]{:S(2)}, u32[]{:S(2)}) collective-permute-start(bf16[2,2,32,2816]{3,2,0,1:T(8,128)(2,1)S(1)} %dynamic-slice_bitcast_fusion.4), channel_id=1, source_target_pairs={{0,1},{1,0},{2,3},{3,2},{4,5},{5,4},{6,7},{7,6},{8,9},{9,8},{10,11... | collective-permute-start | bytes 2162696 | tf_op jit(solution)/shard_map/ppermute | solution.py:325
  631.1 11.4 %collective-permute-start.22 = (bf16[2,2,32,2816]{3,2,0,1:T(8,128)(2,1)S(1)}, bf16[2,2,32,2816]{3,2,0,1:T(8,128)(2,1)S(1)}, u32[]{:S(2)}, u32[]{:S(2)}) collective-permute-start(bf16[2,2,32,2816]{3,2,0,1:T(8,128)(2,1)S(1)} %dynamic-slice_bitcast_fusion.5), channel_id=1, source_target_pairs={{0,16},{1,17},{2,18},{3,19},{4,20},{5,21},{6,22},{7,23},{8,24},{9,... | collective-permute-start | bytes 2162696 | tf_op jit(solution)/shard_map/ppermute | solution.py:325
  631.5 14.2 %collective-permute-start.33 = (bf16[2,88,1024]{2,1,0:T(8,128)(2,1)S(1)}, bf16[2,88,1024]{2,1,0:T(8,128)(2,1)S(1)}, u32[]{:S(2)}, u32[]{:S(2)}) collective-permute-start(bf16[2,88,1024]{2,1,0:T(8,128)(2,1)S(1)} %dynamic-slice_bitcast_fusion.10), channel_id=1, source_target_pairs={{0,2},{1,3},{2,0},{3,1},{4,6},{5,7},{6,4},{7,5},{8,10},{9,11},{10,... | collective-permute-start | bytes 1081352 | tf_op jit(solution)/shard_map/ppermute | solution.py:325
  641.0 9.8 %collective-permute-start.28 = (bf16[2,32,2816]{2,1,0:T(8,128)(2,1)S(1)}, bf16[2,32,2816]{2,1,0:T(8,128)(2,1)S(1)}, u32[]{:S(2)}, u32[]{:S(2)}) collective-permute-start(bf16[2,32,2816]{2,1,0:T(8,128)(2,1)S(1)} %dynamic-slice_bitcast_fusion.11), channel_id=1, source_target_pairs={{0,2},{1,3},{2,0},{3,1},{4,6},{5,7},{6,4},{7,5},{8,10},{9,11},{10,... | collective-permute-start | bytes 1081352 | tf_op jit(solution)/shard_map/ppermute | solution.py:325
  642.7 16.7 %collective-permute-start.23 = (bf16[2,32,2816]{2,1,0:T(8,128)(2,1)S(1)}, bf16[2,32,2816]{2,1,0:T(8,128)(2,1)S(1)}, u32[]{:S(2)}, u32[]{:S(2)}) collective-permute-start(bf16[2,32,2816]{2,1,0:T(8,128)(2,1)S(1)} %dynamic-slice_bitcast_fusion.12), channel_id=1, source_target_pairs={{0,2},{1,3},{2,0},{3,1},{4,6},{5,7},{6,4},{7,5},{8,10},{9,11},{10,... | collective-permute-start | bytes 1081352 | tf_op jit(solution)/shard_map/ppermute | solution.py:325
  645.9 16.9 %collective-permute-start.34 = (bf16[88,1024]{1,0:T(8,128)(2,1)S(1)}, bf16[88,1024]{1,0:T(8,128)(2,1)S(1)}, u32[]{:S(2)}, u32[]{:S(2)}) collective-permute-start(bf16[88,1024]{1,0:T(8,128)(2,1)S(1)} %dynamic-slice_bitcast_fusion.17), channel_id=1, source_target_pairs={{0,4},{1,5},{2,6},{3,7},{4,0},{5,1},{6,2},{7,3},{8,12},{9,13},{10,... | collective-permute-start | bytes 540680 | tf_op jit(solution)/shard_map/ppermute | solution.py:325
  650.9 11.1 %collective-permute-start.29 = (bf16[32,2816]{1,0:T(8,128)(2,1)S(1)}, bf16[32,2816]{1,0:T(8,128)(2,1)S(1)}, u32[]{:S(2)}, u32[]{:S(2)}) collective-permute-start(bf16[32,2816]{1,0:T(8,128)(2,1)S(1)} %dynamic-slice_bitcast_fusion.18), channel_id=1, source_target_pairs={{0,4},{1,5},{2,6},{3,7},{4,0},{5,1},{6,2},{7,3},{8,12},{9,13},{10,... | collective-permute-start | bytes 540680 | tf_op jit(solution)/shard_map/ppermute | solution.py:325
  659.5 7.4 %collective-permute-start.24 = (bf16[32,2816]{1,0:T(8,128)(2,1)S(1)}, bf16[32,2816]{1,0:T(8,128)(2,1)S(1)}, u32[]{:S(2)}, u32[]{:S(2)}) collective-permute-start(bf16[32,2816]{1,0:T(8,128)(2,1)S(1)} %dynamic-slice_bitcast_fusion.19), channel_id=1, source_target_pairs={{0,4},{1,5},{2,6},{3,7},{4,0},{5,1},{6,2},{7,3},{8,12},{9,13},{10,... | collective-permute-start | bytes 540680 | tf_op jit(solution)/shard_map/ppermute | solution.py:325
  (49 other events, 422.0 us)
Sparse Core Ops, SparseCore 0:
  10.9 70.0 all-gather.7
  84.5 68.9 all-gather.3
  157.0 98.5 all-gather.5

commit v3 on v2

--- a/solution.py
+++ b/solution.py
@@ -80,9 +80,7 @@
 def attend_kernel(
     slot_count,
     head_size,
-    x_ref,
-    scale_ref,
-    gain_ref,
+    normed_ref,
     wq_ref,
     wk_ref,
     wv_ref,
@@ -90,7 +88,6 @@
     bias_ref,
     cos_ref,
     sin_ref,
-    normed_ref,
     q_ref,
     k_ref,
     v_ref,
@@ -102,13 +99,6 @@
     width = q_ref.shape[1]
     bucket_count = bias_ref.shape[0]
     query_rows = slot_count // 2
-
-    @pl.when(pl.program_id(0) == 0)
-    def _():
-        normed_ref[...] = (
-            x_ref[...].astype(jnp.float32) * scale_ref[...] * gain_ref[...]
-        ).astype(jnp.bfloat16)
-
     normed = normed_ref[...]
     cosine = cos_ref[...]
     sine = sin_ref[...]
@@ -152,22 +142,20 @@
                 )
 
 
-def attend(inputs, scale_one, gain, weights, first_values, bias, cosine, sine, head_size, width):
-    token_count, model_width = inputs.shape
+def attend(normed, weights, first_values, bias, cosine, sine, head_size, width):
+    token_count, model_width = normed.shape
     bucket_count, slot_count = bias.shape[:2]
     steps = model_width // width
     whole = lambda step: (0, 0)
     block = pl.BlockSpec((token_count, width), lambda step: (0, step))
     heads = width // head_size
     table = pl.BlockSpec((token_count, PAIR), whole)
-    low_shape = jax.ShapeDtypeStruct((token_count, model_width), jnp.bfloat16)
+    low_shape = jax.ShapeDtypeStruct((token_count, steps * width), jnp.bfloat16)
     return pl.pallas_call(
         partial(attend_kernel, slot_count, head_size),
         grid=(steps,),
         in_specs=[
             pl.BlockSpec((token_count, model_width), whole),
-            pl.BlockSpec((token_count, 1), whole),
-            pl.BlockSpec((1, model_width), whole),
             pl.BlockSpec((model_width, width), lambda step: (0, step)),
             pl.BlockSpec((model_width, width), lambda step: (0, steps + step)),
             pl.BlockSpec((model_width, width), lambda step: (0, 2 * steps + step)),
@@ -177,18 +165,17 @@
             table,
         ],
         out_specs=[
-            pl.BlockSpec((token_count, model_width), whole),
             block,
             block,
             block,
             block,
             pl.BlockSpec((bucket_count, 1, heads, slot_count), lambda step: (0, step, 0, 0)),
         ],
-        out_shape=[low_shape] * 5
+        out_shape=[low_shape] * 4
         + [jax.ShapeDtypeStruct((bucket_count, steps, heads, slot_count), jnp.float32)],
         compiler_params=pltpu.CompilerParams(vmem_limit_bytes=56 << 20),
         name="attend",
-    )(inputs, scale_one, gain, weights, weights, weights, first_values, bias, cosine, sine)
+    )(normed, weights, weights, weights, first_values, bias, cosine, sine)
 
 
 def attend_back_kernel(
@@ -202,11 +189,9 @@
     bias_ref,
     cos_ref,
     sin_ref,
-    grads_ref,
-    first_ref,
-    dk_ref,
-    dv_ref,
+    *rest,
 ):
+    grads_ref, first_ref, dk_ref, dv_ref = rest[-4:]
     half_size = head_size // 2
     score_scale = head_size ** (-0.5)
     width = q_ref.shape[1]
@@ -278,13 +263,14 @@
 
 
 def attend_back(
-    queries, keys, values, grads, lse, bias, cosine, sine, head_size, width, first_step, steps
+    queries, keys, values, grads, lse, bias, cosine, sine, head_size, width, first_step, steps, first
 ):
-    token_count = queries.shape[0]
+    token_count, model_width = queries.shape
     bucket_count, slot_count = bias.shape[:2]
     heads = width // head_size
     block = pl.BlockSpec((token_count, width), lambda step: (0, first_step + step))
     table = pl.BlockSpec((token_count, PAIR), lambda step: (0, 0))
+    shared = [] if first is None else [first]
     return pl.pallas_call(
         partial(attend_back_kernel, slot_count, head_size),
         grid=(steps,),
@@ -299,56 +285,145 @@
             pl.BlockSpec((bucket_count, slot_count, slot_count), lambda step: (0, 0, 0)),
             table,
             table,
-        ],
+        ]
+        + [pl.BlockSpec(memory_space=pl.ANY)] * len(shared),
         out_specs=[
             pl.BlockSpec((3, token_count, width), lambda step: (0, 0, step)),
-            pl.BlockSpec((token_count, width), lambda step: (0, step)),
+            block,
         ],
         out_shape=[
             jax.ShapeDtypeStruct((3, token_count, steps * width), jnp.bfloat16),
-            jax.ShapeDtypeStruct((token_count, steps * width), jnp.float32),
+            jax.ShapeDtypeStruct((token_count, model_width), jnp.float32),
         ],
         scratch_shapes=[
             pltpu.VMEM((PAIR // head_size, slot_count, PAIR), jnp.float32),
             pltpu.VMEM((PAIR // head_size, slot_count, PAIR), jnp.float32),
         ],
+        input_output_aliases={8: 1} if shared else {},
         compiler_params=pltpu.CompilerParams(vmem_limit_bytes=56 << 20),
         name="attend_back",
-    )(queries, keys, values, grads, lse, bias, cosine, sine)
+    )(queries, keys, values, grads, lse, bias, cosine, sine, *shared)
 
 
 AXES = ("dp", "fsdp")
 
 
-def flip(value, bit, device_count):
-    pairs = [(place, place ^ (1 << bit)) for place in range(device_count)]
+def flip(value, mask, device_count):
+    pairs = [(place, place ^ mask) for place in range(device_count)]
     return lax.ppermute(value, AXES, pairs)
 
 
-def stage_orders(dp_size, fsdp_size):
+def masks_of(bits):
+    masks = [0]
+    for bit in bits:
+        masks += [mask | 1 << bit for mask in masks]
+    return masks
+
+
+class Exchange:
+    def __init__(self, partial_sum, steps, place, device_count):
+        self.current = partial_sum
+        self.steps = [list(step) for step in steps]
+        self.left = sorted([bit for step in steps for bit in step], reverse=True)
+        self.place = place
+        self.device_count = device_count
+        self.got = None
+
+    def part(self, mask):
+        value = self.current
+        left = list(self.left)
+        for bit in self.steps[0]:
+            lead, row_count, width = value.shape
+            high = 1 << left.index(bit)
+            view = value.reshape(lead, high, 2, row_count // (2 * high), width)
+            chosen = ((self.place ^ mask) >> bit) & 1
+            value = lax.dynamic_index_in_dim(view, chosen, 2, keepdims=False)
+            value = value.reshape(lead, row_count // 2, width)
+            left.remove(bit)
+        return value
+
+    def outgoing(self):
+        masks = masks_of(self.steps[0])
+        self.kept = self.part(0)
+        return [self.part(mask) for mask in masks[1:]]
+
+    def launch(self, sent):
+        masks = masks_of(self.steps[0])[1:]
+        self.got = [flip(value, mask, self.device_count) for value, mask in zip(sent, masks)]
+
+    def settle(self, got):
+        total = self.kept.astype(jnp.float32)
+        for value in got:
+            total = total + value.astype(jnp.float32)
+        for bit in self.steps.pop(0):
+            self.left.remove(bit)
+        self.current = total.astype(jnp.bfloat16) if self.steps else total
+
+
+class Gather:
+    def __init__(self, rows, steps, place, device_count):
+        self.current = rows
+        self.steps = [list(step) for step in steps]
+        self.have = []
+        self.place = place
+        self.device_count = device_count
+        self.got = None
+
+    def outgoing(self):
+        return [self.current]
+
+    def launch(self, sent):
+        masks = masks_of(self.steps[0])[1:]
+        self.got = [flip(sent[0], mask, self.device_count) for mask in masks]
+
+    def settle(self, got):
+        pieces = [self.current] + list(got)
+        for bit in self.steps.pop(0):
+            row_count, width = pieces[0].shape
+            high = 1 << len([other for other in self.have if other > bit])
+            shape = (high, 1, row_count // high, width)
+            side = lax.broadcasted_iota(jnp.int32, (1, 2, 1, 1), 1)
+            mine = side == ((self.place >> bit) & 1)
+            pieces = [
+                jnp.where(mine, near.reshape(shape), far.reshape(shape)).reshape(
+                    2 * row_count, width
+                )
+                for near, far in zip(pieces[0::2], pieces[1::2])
+            ]
+            self.have.append(bit)
+        self.current = pieces[0]
+
+
+def tick(chain, settled, launched):
+    settled = [item for item in settled if item.got is not None]
+    if settled:
+        chain, gots = lax.optimization_barrier((chain, [item.got for item in settled]))
+        for item, got in zip(settled, gots):
+            item.settle(got)
+            item.got = None
+    launched = [item for item in launched if item.steps and item.got is None]
+    if launched:
+        chain, sents = lax.optimization_barrier((chain, [item.outgoing() for item in launched]))
+        for item, sent in zip(launched, sents):
+            item.launch(sent)
+    return chain
+
+
+def step_plans(dp_size, fsdp_size):
     bit_count = (dp_size * fsdp_size).bit_length() - 1
     core_bit = fsdp_size.bit_length() - 1
-    high_bits = list(range(core_bit + 1, bit_count))
+    high = list(range(core_bit + 1, bit_count))
     rest = list(range(1, core_bit))
-    return ([core_bit] + high_bits + [0] + rest, [core_bit, 0] + high_bits + rest)
-
-
-def reduce_rows(partial_sum, order, place, device_count):
-    bit_count = len(order)
-    row_count, width = partial_sum.shape
-    current = partial_sum.reshape((2,) * bit_count + (row_count // device_count, width))
-    left = list(range(bit_count - 1, -1, -1))
-    for step, bit in enumerate(order):
-        axis = left.index(bit)
-        mine = (place >> bit) & 1
-        sent = lax.dynamic_index_in_dim(current, 1 - mine, axis, keepdims=False)
-        kept = lax.dynamic_index_in_dim(current, mine, axis, keepdims=False)
-        got = flip(sent.astype(jnp.bfloat16), bit, device_count)
-        current = kept.astype(jnp.float32) + got.astype(jnp.float32)
-        if step + 1 < bit_count:
-            current = current.astype(jnp.bfloat16)
-        left.remove(bit)
-    return current
+    pairs = [rest[index : index + 2] for index in range(0, len(rest), 2)]
+    core = [core_bit]
+    return {
+        "high_first": [core, high, [0]] + pairs,
+        "low_first": [core, [0], high] + pairs,
+        "short": [core, high + [0]] + pairs,
+        "gather": pairs[::-1] + [[0] + high, core],
+        "gather_low_first": pairs[::-1] + [[0], high, core],
+        "gather_high_first": pairs[::-1] + [high, [0], core],
+    }
 
 
 def shards(
@@ -370,30 +445,28 @@
 ):
     device_count = dp_size * fsdp_size
     place = lax.axis_index("dp") * fsdp_size + lax.axis_index("fsdp")
-    order_a, order_b = stage_orders(dp_size, fsdp_size)
+    plans = step_plans(dp_size, fsdp_size)
     micro_count = lengths.shape[0]
     token_count, model_width = tokens.shape
     slot_count = token_count // micro_count
-    head_count = HEADS
-    head_size = model_width // head_count
+    head_size = model_width // HEADS
     hidden_width = w_gate.shape[1]
-
-    gains = jnp.pad(jnp.stack([gain_one, gain_two], axis=1), ((0, 0), (0, 126)))
+    width = 4 * head_size
+    half_width = model_width // 2
+    half_steps = half_width // width
+    exchange = partial(Exchange, place=place, device_count=device_count)
+
+    gain_columns = jnp.pad(jnp.stack([gain_one, gain_two], axis=1), ((0, 0), (0, 126)))
+    gather = partial(Gather, place=place, device_count=device_count)
+    projections = (w_query, w_key, w_value)
     first_set = lax.all_gather(
-        jnp.concatenate([w_query, w_key, w_value, gains], axis=1), AXES, axis=0, tiled=True
+        jnp.concatenate([*projections, gain_columns], axis=1), AXES, axis=0, tiled=True
     )
     second_set = lax.all_gather(
-        jnp.concatenate([w_out, w_gate, w_up], axis=1), AXES, axis=0, tiled=True
-    )
-    down_w = lax.all_gather(w_down, AXES, axis=0, tiled=True)
-    query_w = first_set[:, :model_width]
-    key_w = first_set[:, model_width : 2 * model_width]
-    value_w = first_set[:, 2 * model_width : 3 * model_width]
-    gain_first_f = first_set[:, 3 * model_width].astype(jnp.float32)[None, :]
-    gain_second_f = first_set[:, 3 * model_width + 1].astype(jnp.float32)[None, :]
-    out_w = second_set[:, :model_width]
-    gate_w = second_set[:, model_width : model_width + hidden_width]
-    up_w = second_set[:, model_width + hidden_width :]
+        jnp.concatenate([w_gate, w_up], axis=1), AXES, axis=0, tiled=True
+    )
+    out_rows = gather(w_out, plans["gather"])
+    down_rows = gather(w_down, plans["gather"])
 
     inputs = tokens.astype(jnp.float32)
     layouts = [bucket_layout(lengths[index], slot_count) for index in range(micro_count)]
@@ -409,44 +482,53 @@
         ]
     )
     scale_one = rms_scale(inputs)
-    width = 4 * head_size
-    normed, query_rot, key_rot, value_mix, context, lse = attend(
-        tokens,
-        scale_one,
-        gain_first_f,
-        first_set,
-        first_values,
-        bias,
-        cosine,
-        sine,
-        head_size,
-        width,
-    )
+
+    scale_one = tick(scale_one, [], [out_rows, down_rows])
+    scale_one = tick(scale_one, [out_rows, down_rows], [out_rows, down_rows])
+    gain_first_f = first_set[:, 3 * model_width].astype(jnp.float32)[None, :]
+    gain_second_f = first_set[:, 3 * model_width + 1].astype(jnp.float32)[None, :]
+    normed = (inputs * scale_one * gain_first_f).astype(jnp.bfloat16)
+    query_rot, key_rot, value_mix, context, lse = attend(
+        normed, first_set, first_values, bias, cosine, sine, head_size, width
+    )
+    context = tick(context, [out_rows, down_rows], [out_rows, down_rows])
+    while out_rows.steps:
+        context = tick(context, [out_rows], [out_rows])
+    out_w = out_rows.current
     hidden = inputs + forward_dot(context, out_w)
     scale_two = rms_scale(hidden)
     normed_two = (hidden * scale_two * gain_second_f).astype(jnp.bfloat16)
+    gate_w = second_set[:, :hidden_width]
+    up_w = second_set[:, hidden_width:]
+    while down_rows.steps:
+        normed_two = tick(normed_two, [down_rows], [down_rows])
+    down_w = down_rows.current
     gate_values = forward_dot(normed_two, gate_w)
     upward = forward_dot(normed_two, up_w)
     sigmoid_gate = jax.nn.sigmoid(gate_values)
     silu_gate = gate_values * sigmoid_gate
     product = (silu_gate * upward).astype(jnp.bfloat16)
-    out_tokens = (hidden + forward_dot(product, down_w)).astype(jnp.bfloat16)
-
     grad_y = cotangent.astype(jnp.float32) * valid.astype(jnp.float32)[:, None]
     grad_y_low = grad_y.astype(jnp.bfloat16)
-    grad_down_w = contract_first(product, grad_y_low).astype(jnp.bfloat16)
-    grad_down_sum = reduce_rows(grad_down_w, order_a, place, device_count)
+    down = exchange(
+        contract_first(product, grad_y_low).astype(jnp.bfloat16)[None], plans["high_first"]
+    )
+    grad_y_low = tick(grad_y_low, [], [down])
     grad_product = contract_last(grad_y_low, down_w)
     grad_upward = (grad_product * silu_gate).astype(jnp.bfloat16)
     grad_gate_low = (
         grad_product * upward * sigmoid_gate * (1.0 + gate_values * (1.0 - sigmoid_gate))
     ).astype(jnp.bfloat16)
-    grad_gate_w = contract_first(normed_two, grad_gate_low).astype(jnp.bfloat16)
-    grad_gate_sum = reduce_rows(grad_gate_w, order_b, place, device_count)
-    grad_up_w = contract_first(normed_two, grad_upward).astype(jnp.bfloat16)
-    grad_up_sum = reduce_rows(grad_up_w, order_a, place, device_count)
+    grad_upward, grad_gate_low = tick((grad_upward, grad_gate_low), [down], [down])
+    gate = exchange(
+        contract_first(normed_two, grad_gate_low).astype(jnp.bfloat16)[None], plans["low_first"]
+    )
+    up = exchange(
+        contract_first(normed_two, grad_upward).astype(jnp.bfloat16)[None], plans["high_first"]
+    )
+    grad_upward, grad_gate_low = tick((grad_upward, grad_gate_low), [], [gate, up])
     grad_normed_two = contract_last(grad_gate_low, gate_w) + contract_last(grad_upward, up_w)
-    grad_gain_second = jnp.sum(grad_normed_two * hidden * scale_two, axis=0)
+    grad_normed_two = tick(grad_normed_two, [gate, up], [gate, up])
     inner_two = grad_normed_two * gain_second_f
     grad_hidden = (
         grad_y
@@ -454,13 +536,17 @@
         - hidden * scale_two**3 * jnp.mean(inner_two * hidden, axis=-1, keepdims=True)
     )
     grad_hidden_low = grad_hidden.astype(jnp.bfloat16)
-    grad_out_w = contract_first(context, grad_hidden_low).astype(jnp.bfloat16)
-    grad_out_sum = reduce_rows(grad_out_w, order_b, place, device_count)
     grad_context = contract_last(grad_hidden_low, out_w).astype(jnp.bfloat16)
-    steps = model_width // width
-    half_steps = steps // 2
-    halves = [
-        attend_back(
+    grad_out_w = jnp.stack(
+        [
+            contract_first(context, grad_hidden_low[:, low : low + half_width])
+            for low in (0, half_width)
+        ]
+    ).astype(jnp.bfloat16)
+    grad_context, grad_out_w = tick((grad_context, grad_out_w), [down], [down])
+
+    def attend_back_half(half, grad_context, first):
+        return attend_back(
             query_rot,
             key_rot,
             value_mix,
@@ -473,48 +559,78 @@
             width,
             half * half_steps,
             half_steps,
+            first,
         )
-        for half in range(2)
-    ]
-    grad_first = jnp.concatenate([half[1] for half in halves], axis=1)
-    grad_query_low, grad_key_low, grad_value_low = [
-        jnp.concatenate([half[0][index] for half in halves], axis=1) for index in range(3)
-    ]
-    grad_query_w = contract_first(normed, grad_query_low).astype(jnp.bfloat16)
-    grad_key_w = contract_first(normed, grad_key_low).astype(jnp.bfloat16)
-    grad_value_w = contract_first(normed, grad_value_low).astype(jnp.bfloat16)
-    grad_normed = (
-        contract_last(grad_query_low, query_w)
-        + contract_last(grad_key_low, key_w)
-        + contract_last(grad_value_low, value_w)
-    )
-    grad_gain_first = jnp.sum(grad_normed * inputs * scale_one, axis=0)
+
+    def weight_parts(low):
+        return [contract_first(normed, low[index]).astype(jnp.bfloat16) for index in range(3)]
+
+    low_one, first_part = attend_back_half(0, grad_context, None)
+    low_one, grad_context = tick((low_one, grad_context), [gate, up], [gate, up])
+    one = exchange(
+        jnp.concatenate([jnp.stack(weight_parts(low_one)), grad_out_w]), plans["short"]
+    )
+    grad_context, product = tick((grad_context, product), [], [one])
+    out_tokens = (hidden + forward_dot(product, down_w)).astype(jnp.bfloat16)
+    grad_context, out_tokens = tick((grad_context, out_tokens), [one, down], [one, down])
+    low_two, grad_first = attend_back_half(1, grad_context, first_part)
+    two = exchange(jnp.stack(weight_parts(low_two)), plans["short"])
+    low_one, low_two = tick((low_one, low_two), [], [two])
+
+    def normed_part(low, half):
+        return sum(
+            contract_last(low[index], first_set[:, start : start + half_width])
+            for index in range(3)
+            for start in [index * model_width + half * half_width]
+        )
+
+    part_one = normed_part(low_one, 0)
+    part_one, low_two = tick((part_one, low_two), [two, gate, up, down], [two, gate, up, down])
+    grad_normed = part_one + normed_part(low_two, 1)
+    grad_normed = tick(grad_normed, [one], [one])
     inner_one = grad_normed * gain_first_f
     grad_tokens = (
         grad_hidden
         + scale_one * inner_one
         - inputs * scale_one**3 * jnp.mean(inner_one * inputs, axis=-1, keepdims=True)
     )
-    grad_query_sum = reduce_rows(grad_query_w, order_a, place, device_count)
-    grad_key_sum = reduce_rows(grad_key_w, order_b, place, device_count)
-    grad_value_sum = reduce_rows(grad_value_w, order_a, place, device_count)
-    gain_columns = jnp.pad(
-        jnp.stack([grad_gain_first, grad_gain_second], axis=1), ((0, 0), (0, 126))
-    )
-    grad_gains = reduce_rows(gain_columns, order_b, place, device_count)
+    grad_tokens = tick(grad_tokens, [two], [two])
+    pending = [gate, up, down, one, two]
+    while True:
+        pending = [item for item in pending if item.steps]
+        if not pending:
+            break
+        for item in pending:
+            if item.got is not None:
+                item.settle(item.got)
+            if item.steps:
+                item.launch(item.outgoing())
+    projection_sums = [
+        jnp.concatenate([one.current[index], two.current[index]], axis=1) for index in range(3)
+    ]
+    grad_out_sum = jnp.concatenate([one.current[3], one.current[4]], axis=1)
+    grad_gate_sum = gate.current[0]
+    grad_up_sum = up.current[0]
+    grad_down_sum = down.current[0]
+
+    def gain_grad(gain, sums, weights):
+        total = sum(
+            jnp.sum(grads * weight.astype(jnp.float32), axis=1)
+            for grads, weight in zip(sums, weights)
+        )
+        return total / gain.astype(jnp.float32)
+
     return (
         out_tokens,
         grad_tokens,
         grad_first,
-        grad_query_sum,
-        grad_key_sum,
-        grad_value_sum,
+        *projection_sums,
         grad_out_sum,
         grad_gate_sum,
         grad_up_sum,
         grad_down_sum,
-        grad_gains[:, 0],
-        grad_gains[:, 1],
+        gain_grad(gain_one, projection_sums, projections),
+        gain_grad(gain_two, (grad_gate_sum, grad_up_sum), (w_gate, w_up)),
     )
 
 

time: 680 us -> 529 us (0.78)
  waiting for transfers between devices: 308 us -> 141 us
  other arithmetic: 38.5 us -> 69.9 us
  starting transfers between devices: 33.1 us -> 64.2 us
  matrix products: 154 us -> 127 us
  local copies, waits for them, and re-layouts: 54.1 us -> 35.3 us
    all_gather x3 -> x2, waiting for transfers between devices: 175 us -> 76.5 us  [the longest x1 54.3 us: shards(): lax.all_gather(jnp.concatenate([*projections, gain_columns], axis=1), AXE...]
    ppermute x40 -> x46, waiting for transfers between devices: 133 us -> 64.9 us  [flip(): return lax.ppermute(value, AXES, pairs)]
    ppermute x40 -> x46, starting transfers between devices: 33 us -> 64.2 us  [flip(): return lax.ppermute(value, AXES, pairs)]
    select_n x0 -> x14, other arithmetic: none -> 18.4 us  [settle(): jnp.where(mine, near.reshape(shape), far.reshape(shape))]
    unnamed x81 -> x168, local copies, waits for them, and re-layouts: 24.2 us -> 9.16 us
    dot_general x4, matrix products: 51.9 us -> 38.9 us  [forward_dot(): return jnp.dot(left, right, preferred_element_type=jnp.float32)]
    dot_general x7 -> x11, matrix products: 45 us -> 34.6 us  [contract_first(): lax.dot_general(left, right, (((0,), (0,)), ((), ())), preferred_element_...]
    convert_element_type x32 -> x16, other arithmetic: 14.9 us -> 25.1 us  [the longest x13 16.2 us: settle(): self.current = total.astype(jnp.bfloat16) if self.steps else total]
  transfers between devices with their start and end apart: 43 -> 48, of which waited for: 29 -> 15; matrix products, arithmetic and copies ran while one was open for 17% -> 26% of each run, Pallas kernels for 6% -> 10%
where the time goes in v3:
time: 529 us; the launch traced here: 524 us
  waiting for transfers between devices  141 us (27%)
  matrix products  127 us (24%)
  Pallas kernels  70.5 us (13%)
  other arithmetic  69.9 us (13%)
  starting transfers between devices  64.2 us (12%)
  local copies, waits for them, and re-layouts  35.3 us (7%)
  between operations  15.7 us (3%)
    ppermute x46, waiting for transfers between devices, flip(): return lax.ppermute(value, AXES, pairs)  64.9 us
    ppermute x46, starting transfers between devices, flip(): return lax.ppermute(value, AXES, pairs)  64.2 us
    all_gather x1, waiting for transfers between devices, shards(): lax.all_gather(jnp.concatenate([*projections, gain_columns], axis=1), AXE...  54.3 us
    dot_general x10, matrix products, contract_last(): lax.dot_general(left, right, (((1,), (1,)), ((), ())), preferred_element_...  53.6 us
    dot_general x4, matrix products, forward_dot(): return jnp.dot(left, right, preferred_element_type=jnp.float32)  38.9 us
    pallas_call x1, Pallas kernels, attend(): pl.pallas_call(partial(attend_kernel, slot_count, head_size), grid=(steps...  36.1 us
    dot_general x11, matrix products, contract_first(): lax.dot_general(left, right, (((0,), (0,)), ((), ())), preferred_element_...  34.6 us
    pallas_call x2, Pallas kernels, attend_back(): pl.pallas_call(partial(attend_back_kernel, slot_count, head_size), grid=(...  34.4 us
  transfers between devices with their start and end apart: 48, of which 15 were waited for; matrix products, arithmetic and copies ran while one was open for 26% of the time, Pallas kernels for 10%

profile of v3, /device:TPU:0, one launch (start us, length us, event | category | flops | bytes accessed | tf_op | source)
XLA Modules:
  0.0 524.2 jit_solution(10374402778736233110)
XLA Ops:
  13.7 3.1 collective-permute-start.3
  20.3 3.5 collective-permute-start.1
  36.6 8.0 %collective-permute-done.1 = bf16[32,1024]{1,0:T(8,128)(2,1)S(1)} collective-permute-done((bf16[32,1024]{1,0:T(8,128)(2,1)S(1)}, bf16[32,1024]{1,0:T(8,128)(2,1)S(1)}, u32[]{:S(2)}, u32[]{:S(2)}) %collective-permute-start.1) | collective-permute-done | bytes 65568 | tf_op jit(solution)/shard_map/ppermute | solution.py:313
  55.9 54.3 %all-gather.3.cloned.1.call-done.wq_ref.wk_ref.wv_ref = bf16[1024,3200]{1,0:T(8,128)(2,1)} async-done(((bf16[32,3200]{1,0:T(8,128)(2,1)}), bf16[1024,3200]{1,0:T(8,128)(2,1)}) %all-gather.3.cloned.1.call-update) | async-done | bytes 6553616 | tf_op jit(solution)/shard_map/all_gather | solution.py:462
  115.0 36.1 %attend.1 = (bf16[1024,1024]{1,0:T(8,128)(2,1)}, bf16[1024,1024]{1,0:T(8,128)(2,1)}, bf16[1024,1024]{1,0:T(8,128)(2,1)}, bf16[1024,1024]{1,0:T(8,128)(2,1)}, f32[2,4,4,512]{3,2,1,0:T(4,128)}) custom-call(bf16[1024,1024]{1,0:T(8,128)(2,1)} %fusion.15.normed_ref, bf16[1024,3200]{1,0:T(8,128)(2,1)} %all-gather.3.cloned.1.call-done.wq_ref.wk_ref.wv_ref, ...), custom_call_target="tpu_custom_call" | custom-call | tf_op jit(solution)/shard_map/attend/pallas_call | solution.py:154
  163.3 3.8 fusion.19
  174.5 6.0 %bitcast_select_fusion = bf16[2816,1024]{1,0:T(8,128)(2,1)} fusion(pred[2816]{0:T(1024)(128)(4,1)S(1)} %copy-done.65, bf16[2,704,1024]{2,1,0:T(8,128)(2,1)} %bitcast.54, bf16[2,704,1024]{2,1,0:T(8,128)(2,1)S(1)} %broadcast_select_fusion), kind=kLoop, calls=%fused_computation.16 | loop fusion | flops 2883584 | bytes 11537152 | tf_op jit(solution)/shard_map/jit(_where)/select_n | solution.py:388
  180.5 22.2 %all-gather.5.cloned.1.call-done = bf16[1024,5632]{1,0:T(8,128)(2,1)} async-done(((bf16[32,5632]{1,0:T(8,128)(2,1)}), bf16[1024,5632]{1,0:T(8,128)(2,1)}) %all-gather.5.cloned.1.call-update) | async-done | bytes 11534352 | tf_op jit(solution)/shard_map/all_gather | solution.py:465
  202.7 11.5 %fusion.11 = f32[1024,2816]{1,0:T(8,128)} fusion(bf16[1024,1024]{1,0:T(8,128)(2,1)S(1)} %multiply_convert_fusion.3, bf16[1024,5632]{1,0:T(8,128)(2,1)} %all-gather.5.cloned.1.call-done), kind=kOutput, calls=%fused_computation.29 | convolution fusion | flops 5905580032 | bytes 19398656 | tf_op jit(solution)/shard_map/dot_general | solution.py:18
  214.3 13.4 %multiply_convert_fusion.2 = (bf16[1024,2816]{1,0:T(8,128)(2,1)S(1)}, f32[1024,2816]{1,0:T(8,128)}) fusion(f32[1024,2816]{1,0:T(8,128)} %fusion.11, bf16[1024,1024]{1,0:T(8,128)(2,1)S(1)} %multiply_convert_fusion.3, bf16[1024,5632]{1,0:T(8,128)(2,1)} %all-gather.5.cloned.1.call-done), kind=kOutput, calls=%fused_computation.2 | convolution fusion | flops 5922881536 | bytes 36700160 | tf_op jit(solution)/shard_map/dot_general | solution.py:18
  227.7 6.5 %convolution_convert_fusion.2 = bf16[2816,1024]{1,0:T(8,128)(2,1)S(1)} fusion(bf16[1024,2816]{1,0:T(8,128)(2,1)S(1)} %get-tuple-element.196, bf16[1024,1024]{1,0:T(8,128)(2,1)S(1)} %copy-done.20), kind=kOutput, calls=%fused_computation.19 | convolution fusion | flops 5908463616 | bytes 13631488 | tf_op jit(solution)/shard_map/dot_general | solution.py:28
  237.1 20.3 %multiply_convert_fusion = (bf16[1024,2816]{1,0:T(8,128)(2,1)}, bf16[1024,2816]{1,0:T(8,128)(2,1)}) fusion(f32[1024,2816]{1,0:T(8,128)} %fusion.11, f32[1024,2816]{1,0:T(8,128)} %get-tuple-element.341, bf16[1024,1024]{1,0:T(8,128)(2,1)} %fusion.19, bf16[2816,1024]{1,0:T(8,128)(2,1)} %bitcast_select_fusion), kind=kOutput, calls=%fused_computation | convolution fusion | flops 5943066624 | bytes 42467328 | tf_op jit(solution)/shard_map/dot_general | solution.py:22
  257.5 3.4 fusion.3
  261.6 6.9 %convolution_convert_fusion = bf16[1024,2816]{1,0:T(8,128)(2,1)S(1)} fusion(bf16[1024,1024]{1,0:T(8,128)(2,1)S(1)} %copy-done.22, bf16[1024,2816]{1,0:T(8,128)(2,1)S(1)} %copy-done.80), kind=kOutput, calls=%fused_computation.17 | convolution fusion | flops 5908463616 | bytes 13631488 | tf_op jit(solution)/shard_map/dot_general | solution.py:28
  268.9 9.6 %convolution_convert_fusion.1 = bf16[1024,2816]{1,0:T(8,128)(2,1)S(1)} fusion(bf16[1024,1024]{1,0:T(8,128)(2,1)S(1)} %copy-done.22, bf16[1024,2816]{1,0:T(8,128)(2,1)} %get-tuple-element.171), kind=kOutput, calls=%fused_computation.18 | convolution fusion | flops 5908463616 | bytes 13631488 | tf_op jit(solution)/shard_map/dot_general | solution.py:28
  280.8 11.2 %fusion.5 = f32[1024,1024]{1,0:T(8,128)} fusion(bf16[1024,2816]{1,0:T(8,128)(2,1)} %get-tuple-element.172, bf16[1024,5632]{1,0:T(8,128)(2,1)} %all-gather.5.cloned.1.call-done), kind=kOutput, calls=%fused_computation.23 | convolution fusion | flops 5905580032 | bytes 15728640 | tf_op jit(solution)/shard_map/dot_general | solution.py:22
  292.0 10.5 %fusion.24 = f32[1024,1024]{1,0:T(8,128)S(1)} fusion(f32[1024,1024]{1,0:T(8,128)} %fusion.5, bf16[1024,2816]{1,0:T(8,128)(2,1)} %get-tuple-element.171, bf16[1024,5632]{1,0:T(8,128)(2,1)} %all-gather.5.cloned.1.call-done), kind=kOutput, calls=%fused_computation.60 | convolution fusion | flops 5906628608 | bytes 19922944 | tf_op jit(solution)/shard_map/dot_general | solution.py:22
  311.0 3.2 fusion.100
  318.4 3.7 convolution_convert_fusion.3.grad_ref
  325.3 17.3 %attend_back.2 = (bf16[3,1024,512]{2,1,0:T(8,128)(2,1)}, f32[1024,1024]{1,0:T(8,128)}) custom-call(bf16[1024,1024]{1,0:T(8,128)(2,1)} %get-tuple-element.144.q_ref, bf16[1024,1024]{1,0:T(8,128)(2,1)} %get-tuple-element.145.k_ref, bf16[1024,1024]{1,0:T(8,128)(2,1)} %get-tuple-element.146.v_ref, bf16[1024,1024]{1,0:T(8,128)(2,1)} %convolution_convert_fusion.3.grad_ref, ...), custom_call_target="tpu_custom_call" | custom-call | tf_op jit(solution)/shard_map/attend_back/pallas_call | solution.py:274
  358.1 11.4 %add_convert_fusion = bf16[1024,1024]{1,0:T(8,128)(2,1)} fusion(f32[1024,1024]{1,0:T(8,128)} %copy-done, bf16[1024,2816]{1,0:T(8,128)(2,1)} %copy-done.81, bf16[2816,1024]{1,0:T(8,128)(2,1)} %bitcast_select_fusion), kind=kOutput, calls=%fused_computation.39 | convolution fusion | flops 5907677184 | bytes 17825792 | tf_op jit(solution)/shard_map/dot_general | solution.py:18
  369.5 5.9 %collective-permute-done.21 = bf16[1,352,1024]{2,1,0:T(8,128)(2,1)S(1)} collective-permute-done((bf16[1,352,1024]{2,1,0:T(8,128)(2,1)}, bf16[1,352,1024]{2,1,0:T(8,128)(2,1)S(1)}, u32[]{:S(2)}, u32[]{:S(2)}) %collective-permute-start.21) | collective-permute-done | bytes 720928 | tf_op jit(solution)/shard_map/ppermute | solution.py:313
  382.4 17.1 %attend_back.3 = (bf16[3,1024,512]{2,1,0:T(8,128)(2,1)}, f32[1024,1024]{1,0:T(8,128)}) custom-call(bf16[1024,1024]{1,0:T(8,128)(2,1)} %get-tuple-element.144.q_ref, bf16[1024,1024]{1,0:T(8,128)(2,1)} %get-tuple-element.145.k_ref, bf16[1024,1024]{1,0:T(8,128)(2,1)} %get-tuple-element.146.v_ref, ...), custom_call_target="tpu_custom_call", output_to_operand_aliasing={{1}: (8, {})} | custom-call | tf_op jit(solution)/shard_map/attend_back/pallas_call | solution.py:274
  413.7 10.9 %collective-permute-done.23 = bf16[1,128,2816]{2,1,0:T(8,128)(2,1)S(1)} collective-permute-done((bf16[1,128,2816]{2,1,0:T(8,128)(2,1)S(1)}, bf16[1,128,2816]{2,1,0:T(8,128)(2,1)S(1)}, u32[]{:S(2)}, u32[]{:S(2)}) %collective-permute-start.23) | collective-permute-done | bytes 720928 | tf_op jit(solution)/shard_map/ppermute | solution.py:313
  435.3 3.4 collective-permute-start.43
  446.9 12.1 %collective-permute-done.30 = bf16[5,128,512]{2,1,0:T(8,128)(2,1)} collective-permute-done((bf16[5,128,512]{2,1,0:T(8,128)(2,1)}, bf16[5,128,512]{2,1,0:T(8,128)(2,1)}, u32[]{:S(2)}, u32[]{:S(2)}) %collective-permute-start.30) | collective-permute-done | bytes 655392 | tf_op jit(solution)/shard_map/ppermute | solution.py:313
  471.6 7.0 %collective-permute-done.35 = bf16[5,32,512]{2,1,0:T(8,128)(2,1)S(1)} collective-permute-done((bf16[5,32,512]{2,1,0:T(8,128)(2,1)S(1)}, bf16[5,32,512]{2,1,0:T(8,128)(2,1)S(1)}, u32[]{:S(2)}, u32[]{:S(2)}) %collective-permute-start.35) | collective-permute-done | bytes 163872 | tf_op jit(solution)/shard_map/ppermute | solution.py:313
  478.6 4.4 collective-permute-start.41
  490.4 7.1 %collective-permute-done.41 = bf16[1,32,2816]{2,1,0:T(8,128)(2,1)S(1)} collective-permute-done((bf16[1,32,2816]{2,1,0:T(8,128)(2,1)S(1)}, bf16[1,32,2816]{2,1,0:T(8,128)(2,1)S(1)}, u32[]{:S(2)}, u32[]{:S(2)}) %collective-permute-start.41) | collective-permute-done | bytes 180256 | tf_op jit(solution)/shard_map/ppermute | solution.py:313
  498.5 3.4 collective-permute-done.32
  502.2 4.3 collective-permute-start.37
  509.5 4.6 collective-permute-done.38
  (402 shorter events, 162.1 us)
Async XLA Ops:
  7.2 103.0 %all-gather.3.cloned.1.call-start = ((), (), s32[]{:S(2)}) async-start(), calls=%async_computation | async-start | bytes 6758400 | tf_op jit(solution)/shard_map/all_gather | solution.py:462
  9.7 193.0 %all-gather.5.cloned.1.call-start = ((), (), s32[]{:S(2)}) async-start(), calls=%async_computation.1 | async-start | bytes 11894784 | tf_op jit(solution)/shard_map/all_gather | solution.py:465
  13.7 30.9 %collective-permute-start.3 = (bf16[88,1024]{1,0:T(8,128)(2,1)S(1)}, bf16[88,1024]{1,0:T(8,128)(2,1)S(1)}, u32[]{:S(2)}, u32[]{:S(2)}) collective-permute-start(bf16[88,1024]{1,0:T(8,128)(2,1)S(1)} %copy-done.50), channel_id=1, source_target_pairs={{0,2},{1,3},{2,0},{3,1},{4,6},{5,7},{6,4},{7,5},{8,10},{9,11},{10,... | collective-permute-start | bytes 540680 | tf_op jit(solution)/shard_map/ppermute | solution.py:313
  16.8 27.8 %collective-permute-start.4 = (bf16[88,1024]{1,0:T(8,128)(2,1)S(1)}, bf16[88,1024]{1,0:T(8,128)(2,1)S(1)}, u32[]{:S(2)}, u32[]{:S(2)}) collective-permute-start(bf16[88,1024]{1,0:T(8,128)(2,1)S(1)} %copy-done.50), channel_id=1, source_target_pairs={{0,4},{1,5},{2,6},{3,7},{4,0},{5,1},{6,2},{7,3},{8,12},{9,13},{10,... | collective-permute-start | bytes 540680 | tf_op jit(solution)/shard_map/ppermute | solution.py:313
  19.4 25.2 %collective-permute-start.5 = (bf16[88,1024]{1,0:T(8,128)(2,1)S(1)}, bf16[88,1024]{1,0:T(8,128)(2,1)S(1)}, u32[]{:S(2)}, u32[]{:S(2)}) collective-permute-start(bf16[88,1024]{1,0:T(8,128)(2,1)S(1)} %copy-done.50), channel_id=1, source_target_pairs={{0,6},{1,7},{2,4},{3,5},{4,2},{5,3},{6,0},{7,1},{8,14},{9,15},{10,... | collective-permute-start | bytes 540680 | tf_op jit(solution)/shard_map/ppermute | solution.py:313
  20.3 24.3 %collective-permute-start.1 = (bf16[32,1024]{1,0:T(8,128)(2,1)S(1)}, bf16[32,1024]{1,0:T(8,128)(2,1)S(1)}, u32[]{:S(2)}, u32[]{:S(2)}) collective-permute-start(bf16[32,1024]{1,0:T(8,128)(2,1)S(1)} %copy-done.51), channel_id=1, source_target_pairs={{0,4},{1,5},{2,6},{3,7},{4,0},{5,1},{6,2},{7,3},{8,12},{9,13},{10,... | collective-permute-start | bytes 196616 | tf_op jit(solution)/shard_map/ppermute | solution.py:313
  46.7 104.5 %collective-permute-start.10 = (bf16[352,1024]{1,0:T(8,128)(2,1)}, bf16[352,1024]{1,0:T(8,128)(2,1)S(1)}, u32[]{:S(2)}, u32[]{:S(2)}) collective-permute-start(bf16[352,1024]{1,0:T(8,128)(2,1)} %bitcast_select_fusion.6), channel_id=1, source_target_pairs={{0,16},{1,17},{2,18},{3,19},{4,20},{5,21},{6,22},{7,23},{8,24},{9,... | collective-permute-start | bytes 2162696 | tf_op jit(solution)/shard_map/ppermute | solution.py:313
  48.2 103.0 %collective-permute-start.11 = (bf16[352,1024]{1,0:T(8,128)(2,1)}, bf16[352,1024]{1,0:T(8,128)(2,1)S(1)}, u32[]{:S(2)}, u32[]{:S(2)}) collective-permute-start(bf16[352,1024]{1,0:T(8,128)(2,1)} %bitcast_select_fusion.6), channel_id=1, source_target_pairs={{0,17},{1,16},{2,19},{3,18},{4,21},{5,20},{6,23},{7,22},{8,25},{9,... | collective-permute-start | bytes 2162696 | tf_op jit(solution)/shard_map/ppermute | solution.py:313
  49.6 101.5 %collective-permute-start.9 = (bf16[352,1024]{1,0:T(8,128)(2,1)}, bf16[352,1024]{1,0:T(8,128)(2,1)}, u32[]{:S(2)}, u32[]{:S(2)}) collective-permute-start(bf16[352,1024]{1,0:T(8,128)(2,1)} %bitcast_select_fusion.6), channel_id=1, source_target_pairs={{0,1},{1,0},{2,3},{3,2},{4,5},{5,4},{6,7},{7,6},{8,9},{9,8},{10,11... | collective-permute-start | bytes 2162696 | tf_op jit(solution)/shard_map/ppermute | solution.py:313
  50.2 61.4 %collective-permute-start.6 = (bf16[128,1024]{1,0:T(8,128)(2,1)}, bf16[128,1024]{1,0:T(8,128)(2,1)}, u32[]{:S(2)}, u32[]{:S(2)}) collective-permute-start(bf16[128,1024]{1,0:T(8,128)(2,1)} %bitcast_select_fusion.11), channel_id=1, source_target_pairs={{0,1},{1,0},{2,3},{3,2},{4,5},{5,4},{6,7},{7,6},{8,9},{9,8},{10,11... | collective-permute-start | bytes 786440 | tf_op jit(solution)/shard_map/ppermute | solution.py:313
  51.7 99.4 %collective-permute-start.7 = (bf16[128,1024]{1,0:T(8,128)(2,1)}, bf16[128,1024]{1,0:T(8,128)(2,1)}, u32[]{:S(2)}, u32[]{:S(2)}) collective-permute-start(bf16[128,1024]{1,0:T(8,128)(2,1)} %bitcast_select_fusion.11), channel_id=1, source_target_pairs={{0,16},{1,17},{2,18},{3,19},{4,20},{5,21},{6,22},{7,23},{8,24},{9,... | collective-permute-start | bytes 786440 | tf_op jit(solution)/shard_map/ppermute | solution.py:313
  111.6 39.6 %collective-permute-start.8 = (bf16[128,1024]{1,0:T(8,128)(2,1)}, bf16[128,1024]{1,0:T(8,128)(2,1)S(1)}, u32[]{:S(2)}, u32[]{:S(2)}) collective-permute-start(bf16[128,1024]{1,0:T(8,128)(2,1)} %bitcast_select_fusion.11), channel_id=1, source_target_pairs={{0,17},{1,16},{2,19},{3,18},{4,21},{5,20},{6,23},{7,22},{8,25},{9,... | collective-permute-start | bytes 786440 | tf_op jit(solution)/shard_map/ppermute | solution.py:313
  236.8 20.6 %collective-permute-start.14 = (bf16[1,1408,1024]{2,1,0:T(8,128)(2,1)}, bf16[1,1408,1024]{2,1,0:T(8,128)(2,1)}, u32[]{:S(2)}, u32[]{:S(2)}) collective-permute-start(bf16[1,1408,1024]{2,1,0:T(8,128)(2,1)} %bitcast.52), channel_id=1, source_target_pairs={{0,8},{1,9},{2,10},{3,11},{4,12},{5,13},{6,14},{7,15},{8,0},{9,1},... | collective-permute-start | bytes 8650760 | tf_op jit(solution)/shard_map/ppermute | solution.py:313
  278.8 23.7 %collective-permute-start.15 = (bf16[1,512,2816]{2,1,0:T(8,128)(2,1)S(1)}, bf16[1,512,2816]{2,1,0:T(8,128)(2,1)S(1)}, u32[]{:S(2)}, u32[]{:S(2)}) collective-permute-start(bf16[1,512,2816]{2,1,0:T(8,128)(2,1)S(1)} %bitcast.346), channel_id=1, source_target_pairs={{0,8},{1,9},{2,10},{3,11},{4,12},{5,13},{6,14},{7,15},{8,0},{9,1},... | collective-permute-start | bytes 8650760 | tf_op jit(solution)/shard_map/ppermute | solution.py:313
  279.1 23.4 %collective-permute-start.16 = (bf16[1,512,2816]{2,1,0:T(8,128)(2,1)S(1)}, bf16[1,512,2816]{2,1,0:T(8,128)(2,1)S(1)}, u32[]{:S(2)}, u32[]{:S(2)}) collective-permute-start(bf16[1,512,2816]{2,1,0:T(8,128)(2,1)S(1)} %bitcast.345), channel_id=1, source_target_pairs={{0,8},{1,9},{2,10},{3,11},{4,12},{5,13},{6,14},{7,15},{8,0},{9,1},... | collective-permute-start | bytes 8650760 | tf_op jit(solution)/shard_map/ppermute | solution.py:313
  279.4 42.7 %collective-permute-start.17 = (bf16[1,704,1024]{2,1,0:T(8,128)(2,1)S(1)}, bf16[1,704,1024]{2,1,0:T(8,128)(2,1)}, u32[]{:S(2)}, u32[]{:S(2)}) collective-permute-start(bf16[1,704,1024]{2,1,0:T(8,128)(2,1)S(1)} %dynamic-slice_bitcast_fusion.1), channel_id=1, source_target_pairs={{0,16},{1,17},{2,18},{3,19},{4,20},{5,21},{6,22},{7,23},{8,24},{9,... | collective-permute-start | bytes 4325384 | tf_op jit(solution)/shard_map/ppermute | solution.py:313
  308.9 33.9 %collective-permute-start.18 = (bf16[1,256,2816]{2,1,0:T(8,128)(2,1)}, bf16[1,256,2816]{2,1,0:T(8,128)(2,1)}, u32[]{:S(2)}, u32[]{:S(2)}) collective-permute-start(bf16[1,256,2816]{2,1,0:T(8,128)(2,1)} %bitcast.65), channel_id=1, source_target_pairs={{0,1},{1,0},{2,3},{3,2},{4,5},{5,4},{6,7},{7,6},{8,9},{9,8},{10,11... | collective-permute-start | bytes 4325384 | tf_op jit(solution)/shard_map/ppermute | solution.py:313
  309.5 34.6 %collective-permute-start.19 = (bf16[1,256,2816]{2,1,0:T(8,128)(2,1)}, bf16[1,256,2816]{2,1,0:T(8,128)(2,1)}, u32[]{:S(2)}, u32[]{:S(2)}) collective-permute-start(bf16[1,256,2816]{2,1,0:T(8,128)(2,1)} %dynamic-slice_bitcast_fusion), channel_id=1, source_target_pairs={{0,16},{1,17},{2,18},{3,19},{4,20},{5,21},{6,22},{7,23},{8,24},{9,... | collective-permute-start | bytes 4325384 | tf_op jit(solution)/shard_map/ppermute | solution.py:313
  356.6 18.8 %collective-permute-start.20 = (bf16[5,512,512]{2,1,0:T(8,128)(2,1)}, bf16[5,512,512]{2,1,0:T(8,128)(2,1)}, u32[]{:S(2)}, u32[]{:S(2)}) collective-permute-start(bf16[5,512,512]{2,1,0:T(8,128)(2,1)} %bitcast.87), channel_id=1, source_target_pairs={{0,8},{1,9},{2,10},{3,11},{4,12},{5,13},{6,14},{7,15},{8,0},{9,1},... | collective-permute-start | bytes 7864328 | tf_op jit(solution)/shard_map/ppermute | solution.py:313
  356.6 18.8 %collective-permute-start.21 = (bf16[1,352,1024]{2,1,0:T(8,128)(2,1)}, bf16[1,352,1024]{2,1,0:T(8,128)(2,1)S(1)}, u32[]{:S(2)}, u32[]{:S(2)}) collective-permute-start(bf16[1,352,1024]{2,1,0:T(8,128)(2,1)} %bitcast.370), channel_id=1, source_target_pairs={{0,1},{1,0},{2,3},{3,2},{4,5},{5,4},{6,7},{7,6},{8,9},{9,8},{10,11... | collective-permute-start | bytes 2162696 | tf_op jit(solution)/shard_map/ppermute | solution.py:313
  405.5 26.8 %collective-permute-start.22 = (bf16[3,512,512]{2,1,0:T(8,128)(2,1)S(1)}, bf16[3,512,512]{2,1,0:T(8,128)(2,1)S(1)}, u32[]{:S(2)}, u32[]{:S(2)}) collective-permute-start(bf16[3,512,512]{2,1,0:T(8,128)(2,1)S(1)} %bitcast.357), channel_id=1, source_target_pairs={{0,8},{1,9},{2,10},{3,11},{4,12},{5,13},{6,14},{7,15},{8,0},{9,1},... | collective-permute-start | bytes 4718600 | tf_op jit(solution)/shard_map/ppermute | solution.py:313
  406.6 18.1 %collective-permute-start.23 = (bf16[1,128,2816]{2,1,0:T(8,128)(2,1)S(1)}, bf16[1,128,2816]{2,1,0:T(8,128)(2,1)S(1)}, u32[]{:S(2)}, u32[]{:S(2)}) collective-permute-start(bf16[1,128,2816]{2,1,0:T(8,128)(2,1)S(1)} %copy-done.27), channel_id=1, source_target_pairs={{0,16},{1,17},{2,18},{3,19},{4,20},{5,21},{6,22},{7,23},{8,24},{9,... | collective-permute-start | bytes 2162696 | tf_op jit(solution)/shard_map/ppermute | solution.py:313
  408.0 19.9 %collective-permute-start.24 = (bf16[1,128,2816]{2,1,0:T(8,128)(2,1)S(1)}, bf16[1,128,2816]{2,1,0:T(8,128)(2,1)S(1)}, u32[]{:S(2)}, u32[]{:S(2)}) collective-permute-start(bf16[1,128,2816]{2,1,0:T(8,128)(2,1)S(1)} %bitcast.369), channel_id=1, source_target_pairs={{0,1},{1,0},{2,3},{3,2},{4,5},{5,4},{6,7},{7,6},{8,9},{9,8},{10,11... | collective-permute-start | bytes 2162696 | tf_op jit(solution)/shard_map/ppermute | solution.py:313
  408.6 20.9 %collective-permute-start.25 = (bf16[1,88,1024]{2,1,0:T(8,128)(2,1)S(1)}, bf16[1,88,1024]{2,1,0:T(8,128)(2,1)S(1)}, u32[]{:S(2)}, u32[]{:S(2)}) collective-permute-start(bf16[1,88,1024]{2,1,0:T(8,128)(2,1)S(1)} %copy-done.49), channel_id=1, source_target_pairs={{0,2},{1,3},{2,0},{3,1},{4,6},{5,7},{6,4},{7,5},{8,10},{9,11},{10,... | collective-permute-start | bytes 540680 | tf_op jit(solution)/shard_map/ppermute | solution.py:313
  410.0 20.2 %collective-permute-start.26 = (bf16[1,88,1024]{2,1,0:T(8,128)(2,1)S(1)}, bf16[1,88,1024]{2,1,0:T(8,128)(2,1)S(1)}, u32[]{:S(2)}, u32[]{:S(2)}) collective-permute-start(bf16[1,88,1024]{2,1,0:T(8,128)(2,1)S(1)} %copy-done.48), channel_id=1, source_target_pairs={{0,4},{1,5},{2,6},{3,7},{4,0},{5,1},{6,2},{7,3},{8,12},{9,13},{10,... | collective-permute-start | bytes 540680 | tf_op jit(solution)/shard_map/ppermute | solution.py:313
  428.0 17.9 %collective-permute-start.28 = (bf16[5,128,512]{2,1,0:T(8,128)(2,1)}, bf16[5,128,512]{2,1,0:T(8,128)(2,1)S(1)}, u32[]{:S(2)}, u32[]{:S(2)}) collective-permute-start(bf16[5,128,512]{2,1,0:T(8,128)(2,1)} %bitcast.91), channel_id=1, source_target_pairs={{0,16},{1,17},{2,18},{3,19},{4,20},{5,21},{6,22},{7,23},{8,24},{9,... | collective-permute-start | bytes 1966088 | tf_op jit(solution)/shard_map/ppermute | solution.py:313
  429.5 17.4 %collective-permute-start.29 = (bf16[5,128,512]{2,1,0:T(8,128)(2,1)S(1)}, bf16[5,128,512]{2,1,0:T(8,128)(2,1)S(1)}, u32[]{:S(2)}, u32[]{:S(2)}) collective-permute-start(bf16[5,128,512]{2,1,0:T(8,128)(2,1)S(1)} %bitcast.371), channel_id=1, source_target_pairs={{0,1},{1,0},{2,3},{3,2},{4,5},{5,4},{6,7},{7,6},{8,9},{9,8},{10,11... | collective-permute-start | bytes 1966088 | tf_op jit(solution)/shard_map/ppermute | solution.py:313
  430.2 28.8 %collective-permute-start.30 = (bf16[5,128,512]{2,1,0:T(8,128)(2,1)}, bf16[5,128,512]{2,1,0:T(8,128)(2,1)}, u32[]{:S(2)}, u32[]{:S(2)}) collective-permute-start(bf16[5,128,512]{2,1,0:T(8,128)(2,1)} %bitcast.95), channel_id=1, source_target_pairs={{0,17},{1,16},{2,19},{3,18},{4,21},{5,20},{6,23},{7,22},{8,25},{9,... | collective-permute-start | bytes 1966088 | tf_op jit(solution)/shard_map/ppermute | solution.py:313
  435.3 48.5 %collective-permute-start.43 = (bf16[1,32,2816]{2,1,0:T(8,128)(2,1)}, bf16[1,32,2816]{2,1,0:T(8,128)(2,1)S(1)}, u32[]{:S(2)}, u32[]{:S(2)}) collective-permute-start(bf16[1,32,2816]{2,1,0:T(8,128)(2,1)} %get-tuple-element.248), channel_id=1, source_target_pairs={{0,2},{1,3},{2,0},{3,1},{4,6},{5,7},{6,4},{7,5},{8,10},{9,11},{10,... | collective-permute-start | bytes 540680 | tf_op jit(solution)/shard_map/ppermute | solution.py:313
  438.7 47.2 %collective-permute-start.44 = (bf16[1,32,2816]{2,1,0:T(8,128)(2,1)}, bf16[1,32,2816]{2,1,0:T(8,128)(2,1)S(1)}, u32[]{:S(2)}, u32[]{:S(2)}) collective-permute-start(bf16[1,32,2816]{2,1,0:T(8,128)(2,1)} %get-tuple-element.249), channel_id=1, source_target_pairs={{0,4},{1,5},{2,6},{3,7},{4,0},{5,1},{6,2},{7,3},{8,12},{9,13},{10,... | collective-permute-start | bytes 540680 | tf_op jit(solution)/shard_map/ppermute | solution.py:313
  461.1 17.5 %collective-permute-start.35 = (bf16[5,32,512]{2,1,0:T(8,128)(2,1)S(1)}, bf16[5,32,512]{2,1,0:T(8,128)(2,1)S(1)}, u32[]{:S(2)}, u32[]{:S(2)}) collective-permute-start(bf16[5,32,512]{2,1,0:T(8,128)(2,1)S(1)} %get-tuple-element.240), channel_id=1, source_target_pairs={{0,4},{1,5},{2,6},{3,7},{4,0},{5,1},{6,2},{7,3},{8,12},{9,13},{10,... | collective-permute-start | bytes 491528 | tf_op jit(solution)/shard_map/ppermute | solution.py:313
  478.6 18.9 %collective-permute-start.41 = (bf16[1,32,2816]{2,1,0:T(8,128)(2,1)S(1)}, bf16[1,32,2816]{2,1,0:T(8,128)(2,1)S(1)}, u32[]{:S(2)}, u32[]{:S(2)}) collective-permute-start(bf16[1,32,2816]{2,1,0:T(8,128)(2,1)S(1)} %copy-done.39), channel_id=1, source_target_pairs={{0,4},{1,5},{2,6},{3,7},{4,0},{5,1},{6,2},{7,3},{8,12},{9,13},{10,... | collective-permute-start | bytes 540680 | tf_op jit(solution)/shard_map/ppermute | solution.py:313
  (100 other events, 1102.7 us)
Sparse Core Ops, SparseCore 0:
  11.5 98.6 all-gather.2
  113.6 89.0 all-gather.4

commit v4 on v3

--- a/solution.py
+++ b/solution.py
@@ -191,7 +191,8 @@
     sin_ref,
     *rest,
 ):
-    grads_ref, first_ref, dk_ref, dv_ref = rest[-4:]
+    normed_t_ref = rest[0]
+    grads_ref, first_ref, weights_ref, dk_ref, dv_ref = rest[-5:]
     half_size = head_size // 2
     score_scale = head_size ** (-0.5)
     width = q_ref.shape[1]
@@ -260,10 +261,25 @@
                 ).astype(jnp.bfloat16)
             first_ref[rows, low : low + PAIR] = 0.5 * dv
             grads_ref[2, rows, low : low + PAIR] = (0.5 * dv).astype(jnp.bfloat16)
+    for index in range(3):
+        weights_ref[index] = forward_dot(normed_t_ref[...], grads_ref[index]).astype(jnp.bfloat16)
 
 
 def attend_back(
-    queries, keys, values, grads, lse, bias, cosine, sine, head_size, width, first_step, steps, first
+    queries,
+    keys,
+    values,
+    grads,
+    lse,
+    bias,
+    cosine,
+    sine,
+    normed_t,
+    head_size,
+    width,
+    first_step,
+    steps,
+    first,
 ):
     token_count, model_width = queries.shape
     bucket_count, slot_count = bias.shape[:2]
@@ -285,24 +301,81 @@
             pl.BlockSpec((bucket_count, slot_count, slot_count), lambda step: (0, 0, 0)),
             table,
             table,
+            pl.BlockSpec((model_width, token_count), lambda step: (0, 0)),
         ]
         + [pl.BlockSpec(memory_space=pl.ANY)] * len(shared),
         out_specs=[
             pl.BlockSpec((3, token_count, width), lambda step: (0, 0, step)),
             block,
+            pl.BlockSpec((3, model_width, width), lambda step: (0, 0, step)),
         ],
         out_shape=[
             jax.ShapeDtypeStruct((3, token_count, steps * width), jnp.bfloat16),
             jax.ShapeDtypeStruct((token_count, model_width), jnp.float32),
+            jax.ShapeDtypeStruct((3, model_width, steps * width), jnp.bfloat16),
         ],
         scratch_shapes=[
             pltpu.VMEM((PAIR // head_size, slot_count, PAIR), jnp.float32),
             pltpu.VMEM((PAIR // head_size, slot_count, PAIR), jnp.float32),
         ],
-        input_output_aliases={8: 1} if shared else {},
+        input_output_aliases={9: 1} if shared else {},
         compiler_params=pltpu.CompilerParams(vmem_limit_bytes=56 << 20),
+        cost_estimate=pl.CostEstimate(flops=1, transcendentals=0, bytes_accessed=1),
         name="attend_back",
-    )(queries, keys, values, grads, lse, bias, cosine, sine, *shared)
+    )(queries, keys, values, grads, lse, bias, cosine, sine, normed_t, *shared)
+
+
+def finish_kernel(
+    low_one_ref,
+    low_two_ref,
+    wq_ref,
+    wk_ref,
+    wv_ref,
+    hidden_ref,
+    x_ref,
+    scale_ref,
+    gain_ref,
+    out_ref,
+):
+    half = low_one_ref.shape[2]
+    total = None
+    for index, w_ref in enumerate((wq_ref, wk_ref, wv_ref)):
+        for low_ref, start in ((low_one_ref, 0), (low_two_ref, half)):
+            part = contract_last(low_ref[index], w_ref[:, start : start + half])
+            total = part if total is None else total + part
+    inner = total * gain_ref[...]
+    inputs = x_ref[...].astype(jnp.float32)
+    scale = scale_ref[...]
+    mean = jnp.mean(inner * inputs, axis=-1, keepdims=True)
+    out_ref[...] = hidden_ref[...] + scale * inner - inputs * scale**3 * mean
+
+
+def finish(low_one, low_two, weights, grad_hidden, inputs, scale, gain):
+    token_count, model_width = inputs.shape
+    rows = token_count // 4
+    row_block = pl.BlockSpec((rows, model_width), lambda step: (step, 0))
+    low_block = pl.BlockSpec((3, rows, model_width // 2), lambda step: (0, step, 0))
+    weight_blocks = [
+        pl.BlockSpec((model_width, model_width), lambda step, index=index: (0, index))
+        for index in range(3)
+    ]
+    return pl.pallas_call(
+        finish_kernel,
+        grid=(4,),
+        in_specs=[low_block, low_block]
+        + weight_blocks
+        + [
+            row_block,
+            row_block,
+            pl.BlockSpec((rows, 1), lambda step: (step, 0)),
+            pl.BlockSpec((1, model_width), lambda step: (0, 0)),
+        ],
+        out_specs=row_block,
+        out_shape=jax.ShapeDtypeStruct((token_count, model_width), jnp.float32),
+        compiler_params=pltpu.CompilerParams(vmem_limit_bytes=56 << 20),
+        cost_estimate=pl.CostEstimate(flops=1, transcendentals=0, bytes_accessed=1),
+        name="finish",
+    )(low_one, low_two, weights, weights, weights, grad_hidden, inputs, scale, gain)
 
 
 AXES = ("dp", "fsdp")
@@ -416,13 +489,12 @@
     rest = list(range(1, core_bit))
     pairs = [rest[index : index + 2] for index in range(0, len(rest), 2)]
     core = [core_bit]
+    singles = [[bit] for bit in rest]
     return {
-        "high_first": [core, high, [0]] + pairs,
-        "low_first": [core, [0], high] + pairs,
+        "high_first": [core, high, [0]] + singles,
+        "low_first": [core, [0], high] + singles,
         "short": [core, high + [0]] + pairs,
         "gather": pairs[::-1] + [[0] + high, core],
-        "gather_low_first": pairs[::-1] + [[0], high, core],
-        "gather_high_first": pairs[::-1] + [high, [0], core],
     }
 
 
@@ -484,10 +556,12 @@
     scale_one = rms_scale(inputs)
 
     scale_one = tick(scale_one, [], [out_rows, down_rows])
-    scale_one = tick(scale_one, [out_rows, down_rows], [out_rows, down_rows])
+    scale_one = tick(scale_one, [out_rows, down_rows], [out_rows])
+    scale_one = tick(scale_one, [out_rows], [])
     gain_first_f = first_set[:, 3 * model_width].astype(jnp.float32)[None, :]
     gain_second_f = first_set[:, 3 * model_width + 1].astype(jnp.float32)[None, :]
     normed = (inputs * scale_one * gain_first_f).astype(jnp.bfloat16)
+    normed = tick(normed, [], [out_rows, down_rows])
     query_rot, key_rot, value_mix, context, lse = attend(
         normed, first_set, first_values, bias, cosine, sine, head_size, width
     )
@@ -503,32 +577,31 @@
     while down_rows.steps:
         normed_two = tick(normed_two, [down_rows], [down_rows])
     down_w = down_rows.current
+    grad_y = cotangent.astype(jnp.float32) * valid.astype(jnp.float32)[:, None]
+    grad_y_low = grad_y.astype(jnp.bfloat16)
+    grad_product = contract_last(grad_y_low, down_w)
+    normed_two, grad_product = lax.optimization_barrier((normed_two, grad_product))
     gate_values = forward_dot(normed_two, gate_w)
     upward = forward_dot(normed_two, up_w)
     sigmoid_gate = jax.nn.sigmoid(gate_values)
     silu_gate = gate_values * sigmoid_gate
     product = (silu_gate * upward).astype(jnp.bfloat16)
-    grad_y = cotangent.astype(jnp.float32) * valid.astype(jnp.float32)[:, None]
-    grad_y_low = grad_y.astype(jnp.bfloat16)
-    down = exchange(
-        contract_first(product, grad_y_low).astype(jnp.bfloat16)[None], plans["high_first"]
-    )
-    grad_y_low = tick(grad_y_low, [], [down])
-    grad_product = contract_last(grad_y_low, down_w)
     grad_upward = (grad_product * silu_gate).astype(jnp.bfloat16)
     grad_gate_low = (
         grad_product * upward * sigmoid_gate * (1.0 + gate_values * (1.0 - sigmoid_gate))
     ).astype(jnp.bfloat16)
-    grad_upward, grad_gate_low = tick((grad_upward, grad_gate_low), [down], [down])
     gate = exchange(
         contract_first(normed_two, grad_gate_low).astype(jnp.bfloat16)[None], plans["low_first"]
     )
     up = exchange(
         contract_first(normed_two, grad_upward).astype(jnp.bfloat16)[None], plans["high_first"]
     )
-    grad_upward, grad_gate_low = tick((grad_upward, grad_gate_low), [], [gate, up])
+    down = exchange(
+        contract_first(product, grad_y_low).astype(jnp.bfloat16)[None], plans["high_first"]
+    )
+    grad_upward, grad_gate_low = tick((grad_upward, grad_gate_low), [], [gate, up, down])
     grad_normed_two = contract_last(grad_gate_low, gate_w) + contract_last(grad_upward, up_w)
-    grad_normed_two = tick(grad_normed_two, [gate, up], [gate, up])
+    grad_normed_two = tick(grad_normed_two, [gate, up, down], [gate, up])
     inner_two = grad_normed_two * gain_second_f
     grad_hidden = (
         grad_y
@@ -543,7 +616,10 @@
             for low in (0, half_width)
         ]
     ).astype(jnp.bfloat16)
-    grad_context, grad_out_w = tick((grad_context, grad_out_w), [down], [down])
+    normed_t = normed.T
+    grad_context, grad_out_w, normed_t = lax.optimization_barrier(
+        (grad_context, grad_out_w, normed_t)
+    )
 
     def attend_back_half(half, grad_context, first):
         return attend_back(
@@ -555,6 +631,7 @@
             bias,
             cosine,
             sine,
+            normed_t,
             head_size,
             width,
             half * half_steps,
@@ -562,49 +639,23 @@
             first,
         )
 
-    def weight_parts(low):
-        return [contract_first(normed, low[index]).astype(jnp.bfloat16) for index in range(3)]
-
-    low_one, first_part = attend_back_half(0, grad_context, None)
-    low_one, grad_context = tick((low_one, grad_context), [gate, up], [gate, up])
-    one = exchange(
-        jnp.concatenate([jnp.stack(weight_parts(low_one)), grad_out_w]), plans["short"]
-    )
-    grad_context, product = tick((grad_context, product), [], [one])
+    low_one, first_part, weights_one = attend_back_half(0, grad_context, None)
+    one = exchange(jnp.concatenate([weights_one, grad_out_w]), plans["low_first"])
+    grad_context, product = tick((grad_context, product), [gate, up], [gate, up, one])
     out_tokens = (hidden + forward_dot(product, down_w)).astype(jnp.bfloat16)
-    grad_context, out_tokens = tick((grad_context, out_tokens), [one, down], [one, down])
-    low_two, grad_first = attend_back_half(1, grad_context, first_part)
-    two = exchange(jnp.stack(weight_parts(low_two)), plans["short"])
-    low_one, low_two = tick((low_one, low_two), [], [two])
-
-    def normed_part(low, half):
-        return sum(
-            contract_last(low[index], first_set[:, start : start + half_width])
-            for index in range(3)
-            for start in [index * model_width + half * half_width]
-        )
-
-    part_one = normed_part(low_one, 0)
-    part_one, low_two = tick((part_one, low_two), [two, gate, up, down], [two, gate, up, down])
-    grad_normed = part_one + normed_part(low_two, 1)
-    grad_normed = tick(grad_normed, [one], [one])
-    inner_one = grad_normed * gain_first_f
-    grad_tokens = (
-        grad_hidden
-        + scale_one * inner_one
-        - inputs * scale_one**3 * jnp.mean(inner_one * inputs, axis=-1, keepdims=True)
-    )
-    grad_tokens = tick(grad_tokens, [two], [two])
-    pending = [gate, up, down, one, two]
-    while True:
-        pending = [item for item in pending if item.steps]
-        if not pending:
-            break
-        for item in pending:
-            if item.got is not None:
-                item.settle(item.got)
-            if item.steps:
-                item.launch(item.outgoing())
+    grad_context, out_tokens = tick(
+        (grad_context, out_tokens), [gate, up, one], [down, one, gate, up]
+    )
+    low_two, grad_first, weights_two = attend_back_half(1, grad_context, first_part)
+    two = exchange(weights_two, plans["short"])
+    low_two = tick(low_two, [down, one, gate, up], [two, down, one, gate, up])
+    grad_tokens = finish(
+        low_one, low_two, first_set, grad_hidden, tokens, scale_one, gain_first_f
+    )
+    grad_tokens = tick(grad_tokens, [two, down, one, gate, up], [two, down, one])
+    pending = [two, down, one, gate, up]
+    while any(item.steps for item in pending):
+        grad_tokens = tick(grad_tokens, pending, pending)
     projection_sums = [
         jnp.concatenate([one.current[index], two.current[index]], axis=1) for index in range(3)
     ]

time: 529 us -> 488 us (0.922)
  waiting for transfers between devices: 141 us -> 111 us
  matrix products: 127 us -> 106 us
  Pallas kernels: 70.5 us -> 90.6 us
  starting transfers between devices: 64.2 us -> 47.9 us
  local copies, waits for them, and re-layouts: 35.3 us -> 47.7 us
  other arithmetic: 69.9 us -> 64.1 us
    all_gather x1, waiting for transfers between devices: 54.3 us -> 25.4 us  [shards(): lax.all_gather(jnp.concatenate([*projections, gain_columns], axis=1), AXE...]
    dot_general x10 -> x4, matrix products: 53.6 us -> 36 us  [contract_last(): lax.dot_general(left, right, (((1,), (1,)), ((), ())), preferred_element_...]
    ppermute x46 -> x41, starting transfers between devices: 64.2 us -> 47.8 us  [flip(): return lax.ppermute(value, AXES, pairs)]
    pallas_call x0 -> x1, Pallas kernels: none -> 13.5 us  [finish(): pl.pallas_call(finish_kernel, grid=(4,), in_specs=[low_block, low_block]...]
    dot_general x11 -> x5, matrix products: 34.6 us -> 25.5 us  [contract_first(): lax.dot_general(left, right, (((0,), (0,)), ((), ())), preferred_element_...]
    pallas_call x2, Pallas kernels: 34.4 us -> 41.3 us  [attend_back(): pl.pallas_call(partial(attend_back_kernel, slot_count, head_size), grid=(...]
    dot_general x4, matrix products: 38.9 us -> 44.9 us  [forward_dot(): return jnp.dot(left, right, preferred_element_type=jnp.float32)]
    unnamed x168 -> x122, local copies, waits for them, and re-layouts: 9.16 us -> 15.1 us
  transfers between devices with their start and end apart: 48 -> 43, of which waited for: 15 -> 15; matrix products, arithmetic and copies ran while one was open for 26% -> 22% of each run, Pallas kernels for 10% -> 19%
where the time goes in v4:
time: 488 us; the launch traced here: 483 us
  waiting for transfers between devices  111 us (23%)
  matrix products  106 us (22%)
  Pallas kernels  90.6 us (19%)
  other arithmetic  64.1 us (13%)
  starting transfers between devices  47.9 us (10%)
  local copies, waits for them, and re-layouts  47.7 us (10%)
  between operations  15.4 us (3%)
    ppermute x41, waiting for transfers between devices, flip(): return lax.ppermute(value, AXES, pairs)  67.1 us
    ppermute x41, starting transfers between devices, flip(): return lax.ppermute(value, AXES, pairs)  47.8 us
    dot_general x4, matrix products, forward_dot(): return jnp.dot(left, right, preferred_element_type=jnp.float32)  44.9 us
    pallas_call x2, Pallas kernels, attend_back(): pl.pallas_call(partial(attend_back_kernel, slot_count, head_size), grid=(...  41.3 us
    dot_general x4, matrix products, contract_last(): lax.dot_general(left, right, (((1,), (1,)), ((), ())), preferred_element_...  36 us
    pallas_call x1, Pallas kernels, attend(): pl.pallas_call(partial(attend_kernel, slot_count, head_size), grid=(steps...  35.8 us
    dot_general x5, matrix products, contract_first(): lax.dot_general(left, right, (((0,), (0,)), ((), ())), preferred_element_...  25.5 us
    all_gather x1, waiting for transfers between devices, shards(): lax.all_gather(jnp.concatenate([*projections, gain_columns], axis=1), AXE...  25.4 us
  transfers between devices with their start and end apart: 43, of which 15 were waited for; matrix products, arithmetic and copies ran while one was open for 22% of the time, Pallas kernels for 19%

profile of v4, /device:TPU:0, one launch (start us, length us, event | category | flops | bytes accessed | tf_op | source)
XLA Modules:
  0.0 483.1 jit_solution(8703071043020964416)
XLA Ops:
  13.7 3.1 collective-permute-start.3
  16.8 2.6 collective-permute-start.4
  20.3 3.5 collective-permute-start.1
  27.4 5.5 %collective-permute-done = bf16[32,1024]{1,0:T(8,128)(2,1)S(1)} collective-permute-done((bf16[32,1024]{1,0:T(8,128)(2,1)S(1)}, bf16[32,1024]{1,0:T(8,128)(2,1)S(1)}, u32[]{:S(2)}, u32[]{:S(2)}) %collective-permute-start) | collective-permute-done | bytes 65568 | tf_op jit(solution)/shard_map/ppermute | solution.py:386
  32.8 3.5 collective-permute-start.2
  36.4 8.2 %collective-permute-done.1 = bf16[32,1024]{1,0:T(8,128)(2,1)S(1)} collective-permute-done((bf16[32,1024]{1,0:T(8,128)(2,1)S(1)}, bf16[32,1024]{1,0:T(8,128)(2,1)S(1)}, u32[]{:S(2)}, u32[]{:S(2)}) %collective-permute-start.1) | collective-permute-done | bytes 65568 | tf_op jit(solution)/shard_map/ppermute | solution.py:386
  51.8 3.6 collective-permute-done.6
  55.4 5.0 %collective-permute-done.7 = bf16[128,1024]{1,0:T(8,128)(2,1)} collective-permute-done((bf16[128,1024]{1,0:T(8,128)(2,1)}, bf16[128,1024]{1,0:T(8,128)(2,1)}, u32[]{:S(2)}, u32[]{:S(2)}) %collective-permute-start.7) | collective-permute-done | bytes 262176 | tf_op jit(solution)/shard_map/ppermute | solution.py:386
  60.3 4.7 collective-permute-done.8
  68.4 25.4 %all-gather.3.cloned.1.call-done.wq_ref.wk_ref.wv_ref = bf16[1024,3200]{1,0:T(8,128)(2,1)} async-done(((bf16[32,3200]{1,0:T(8,128)(2,1)}), bf16[1024,3200]{1,0:T(8,128)(2,1)}) %all-gather.3.cloned.1.call-update) | async-done | bytes 6553616 | tf_op jit(solution)/shard_map/all_gather | solution.py:534
  111.2 35.8 %attend.1 = (bf16[1024,1024]{1,0:T(8,128)(2,1)}, bf16[1024,1024]{1,0:T(8,128)(2,1)}, bf16[1024,1024]{1,0:T(8,128)(2,1)}, bf16[1024,1024]{1,0:T(8,128)(2,1)}, f32[2,4,4,512]{3,2,1,0:T(4,128)}) custom-call(bf16[1024,1024]{1,0:T(8,128)(2,1)} %fusion.15.normed_ref, bf16[1024,3200]{1,0:T(8,128)(2,1)} %all-gather.3.cloned.1.call-done.wq_ref.wk_ref.wv_ref, ...), custom_call_target="tpu_custom_call" | custom-call | tf_op jit(solution)/shard_map/attend/pallas_call | solution.py:154
  163.0 2.7 bitcast_select_fusion
  168.3 10.5 %fusion.42 = f32[1024,2816]{1,0:T(8,128)} fusion(bf16[2816,1024]{1,0:T(8,128)(2,1)S(1)} %bitcast_select_fusion, bf16[1024,1024]{1,0:T(8,128)(2,1)} %param.15, f32[1024]{0:T(1024)S(1)} %add_convert_fusion.2), kind=kOutput, calls=%fused_computation.86 | convolution fusion | flops 5908725760 | bytes 19402752 | tf_op jit(solution)/shard_map/dot_general | solution.py:22
  178.7 18.6 %all-gather.5.cloned.1.call-done = bf16[1024,5632]{1,0:T(8,128)(2,1)} async-done(((bf16[32,5632]{1,0:T(8,128)(2,1)}), bf16[1024,5632]{1,0:T(8,128)(2,1)}) %all-gather.5.cloned.1.call-update) | async-done | bytes 11534352 | tf_op jit(solution)/shard_map/all_gather | solution.py:537
  197.3 11.7 %fusion.11 = f32[1024,2816]{1,0:T(8,128)} fusion(bf16[1024,1024]{1,0:T(8,128)(2,1)} %multiply_convert_fusion.3, bf16[1024,5632]{1,0:T(8,128)(2,1)} %all-gather.5.cloned.1.call-done), kind=kOutput, calls=%fused_computation.27 | convolution fusion | flops 5905580032 | bytes 19398656 | tf_op jit(solution)/shard_map/dot_general | solution.py:18
  209.0 21.1 %multiply_convert_fusion = (bf16[1024,2816]{1,0:T(8,128)(2,1)}, bf16[1024,2816]{1,0:T(8,128)(2,1)}, bf16[1024,2816]{1,0:T(8,128)(2,1)}) fusion(f32[1024,2816]{1,0:T(8,128)} %fusion.11, f32[1024,2816]{1,0:T(8,128)} %fusion.42, bf16[1024,1024]{1,0:T(8,128)(2,1)S(1)} %copy-done.24, bf16[1024,5632]{1,0:T(8,128)(2,1)} %all-gather.5.cloned.1.call-done), kind=kOutput, calls=%fused_computation | convolution fusion | flops 5948833792 | bytes 48234496 | tf_op jit(solution)/shard_map/dot_general | solution.py:18
  230.2 9.3 %convolution_convert_fusion.1 = bf16[1024,2816]{1,0:T(8,128)(2,1)S(1)} fusion(bf16[1024,1024]{1,0:T(8,128)(2,1)S(1)} %copy-done.24, bf16[1024,2816]{1,0:T(8,128)(2,1)} %get-tuple-element.161), kind=kOutput, calls=%fused_computation.16 | convolution fusion | flops 5908463616 | bytes 13631488 | tf_op jit(solution)/shard_map/dot_general | solution.py:28
  239.5 7.1 %convolution_convert_fusion = bf16[2816,1024]{1,0:T(8,128)(2,1)S(1)} fusion(bf16[1024,2816]{1,0:T(8,128)(2,1)S(1)} %copy-done.56, bf16[1024,1024]{1,0:T(8,128)(2,1)S(1)} %copy-done.25, f32[1024]{0:T(1024)S(1)} %add_convert_fusion.2), kind=kOutput, calls=%fused_computation.15 | convolution fusion | flops 5911609344 | bytes 13635584 | tf_op jit(solution)/shard_map/dot_general | solution.py:28
  250.5 6.5 %convolution_convert_fusion.2 = bf16[1024,2816]{1,0:T(8,128)(2,1)S(1)} fusion(bf16[1024,1024]{1,0:T(8,128)(2,1)S(1)} %copy-done.24, bf16[1024,2816]{1,0:T(8,128)(2,1)S(1)} %bitcast.338), kind=kOutput, calls=%fused_computation.17 | convolution fusion | flops 5908463616 | bytes 13631488 | tf_op jit(solution)/shard_map/dot_general | solution.py:28
  258.2 11.2 %fusion.5 = f32[1024,1024]{1,0:T(8,128)} fusion(bf16[1024,2816]{1,0:T(8,128)(2,1)} %get-tuple-element.161, bf16[1024,5632]{1,0:T(8,128)(2,1)} %all-gather.5.cloned.1.call-done), kind=kOutput, calls=%fused_computation.21 | convolution fusion | flops 5905580032 | bytes 15728640 | tf_op jit(solution)/shard_map/dot_general | solution.py:22
  269.3 10.7 %fusion.22 = f32[1024,1024]{1,0:T(8,128)S(1)} fusion(f32[1024,1024]{1,0:T(8,128)} %fusion.5, bf16[1024,2816]{1,0:T(8,128)(2,1)} %get-tuple-element.160, bf16[1024,5632]{1,0:T(8,128)(2,1)} %all-gather.5.cloned.1.call-done), kind=kOutput, calls=%fused_computation.54 | convolution fusion | flops 5906628608 | bytes 19922944 | tf_op jit(solution)/shard_map/dot_general | solution.py:22
  288.2 3.0 fusion.61
  298.2 3.7 convolution_convert_fusion.3.grad_ref
  301.9 2.6 copy.113.rest_0_
  304.4 20.8 %attend_back.2 = (bf16[3,1024,512]{2,1,0:T(8,128)(2,1)}, f32[1024,1024]{1,0:T(8,128)}, bf16[3,1024,512]{2,1,0:T(8,128)(2,1)}) custom-call(bf16[1024,1024]{1,0:T(8,128)(2,1)} %get-tuple-element.176.q_ref, bf16[1024,1024]{1,0:T(8,128)(2,1)} %get-tuple-element.177.k_ref, bf16[1024,1024]{1,0:T(8,128)(2,1)} %get-tuple-element.178.v_ref, ...), custom_call_target="tpu_custom_call" | custom-call | flops 1 | bytes 1 | tf_op jit(solution)/shard_map/attend_back/pallas_call | solution.py:290
  339.4 9.6 %add_convert_fusion = bf16[1024,1024]{1,0:T(8,128)(2,1)} fusion(f32[1024,1024]{1,0:T(8,128)S(1)} %copy-done.2, bf16[1024,2816]{1,0:T(8,128)(2,1)} %get-tuple-element.184, bf16[2816,1024]{1,0:T(8,128)(2,1)S(1)} %bitcast.286), kind=kOutput, calls=%fused_computation.32 | convolution fusion | flops 5907677184 | bytes 17825792 | tf_op jit(solution)/shard_map/dot_general | solution.py:18
  349.0 6.1 %collective-permute-done.19 = bf16[1,128,2816]{2,1,0:T(8,128)(2,1)S(1)} collective-permute-done((bf16[1,128,2816]{2,1,0:T(8,128)(2,1)S(1)}, bf16[1,128,2816]{2,1,0:T(8,128)(2,1)S(1)}, u32[]{:S(2)}, u32[]{:S(2)}) %collective-permute-start.19) | collective-permute-done | bytes 720928 | tf_op jit(solution)/shard_map/ppermute | solution.py:386
  365.2 20.6 %attend_back.3 = (bf16[3,1024,512]{2,1,0:T(8,128)(2,1)}, f32[1024,1024]{1,0:T(8,128)}, bf16[3,1024,512]{2,1,0:T(8,128)(2,1)}) custom-call(bf16[1024,1024]{1,0:T(8,128)(2,1)} %get-tuple-element.176.q_ref, bf16[1024,1024]{1,0:T(8,128)(2,1)} %get-tuple-element.177.k_ref, bf16[1024,1024]{1,0:T(8,128)(2,1)} %get-tuple-element.178.v_ref, ...), custom_call_target="tpu_custom_call", output_to_operand_aliasing={{1}: (9, {})} | custom-call | flops 1 | bytes 1 | tf_op jit(solution)/shard_map/attend_back/pallas_call | solution.py:290
  385.8 3.8 constant_dynamic-slice_fusion.13
  409.2 13.5 %finish.1 = f32[1024,1024]{1,0:T(8,128)} custom-call(bf16[3,1024,512]{2,1,0:T(8,128)(2,1)} %get-tuple-element.195.low_one_ref, bf16[3,1024,512]{2,1,0:T(8,128)(2,1)} %get-tuple-element.209.low_two_ref, bf16[1024,3200]{1,0:T(8,128)(2,1)} %all-gather.3.cloned.1.call-done.wq_ref.wk_ref.wv_ref, ...), custom_call_target="tpu_custom_call" | custom-call | flops 1 | bytes 1 | tf_op jit(solution)/shard_map/finish/pallas_call | solution.py:362
  435.9 12.8 %collective-permute-done.35 = bf16[5,64,512]{2,1,0:T(8,128)(2,1)S(1)} collective-permute-done((bf16[5,64,512]{2,1,0:T(8,128)(2,1)S(1)}, bf16[5,64,512]{2,1,0:T(8,128)(2,1)S(1)}, u32[]{:S(2)}, u32[]{:S(2)}) %collective-permute-start.35) | collective-permute-done | bytes 327712 | tf_op jit(solution)/shard_map/ppermute | solution.py:386
  459.5 12.1 %collective-permute-done.37 = bf16[3,32,512]{2,1,0:T(8,128)(2,1)S(1)} collective-permute-done((bf16[3,32,512]{2,1,0:T(8,128)(2,1)S(1)}, bf16[3,32,512]{2,1,0:T(8,128)(2,1)S(1)}, u32[]{:S(2)}, u32[]{:S(2)}) %collective-permute-start.37) | collective-permute-done | bytes 98336 | tf_op jit(solution)/shard_map/ppermute | solution.py:386
  (338 shorter events, 149.0 us)
Async XLA Ops:
  7.2 86.6 %all-gather.3.cloned.1.call-start = ((), (), s32[]{:S(2)}) async-start(), calls=%async_computation | async-start | bytes 6758400 | tf_op jit(solution)/shard_map/all_gather | solution.py:534
  9.7 187.6 %all-gather.5.cloned.1.call-start = ((), (), s32[]{:S(2)}) async-start(), calls=%async_computation.1 | async-start | bytes 11894784 | tf_op jit(solution)/shard_map/all_gather | solution.py:537
  13.7 30.9 %collective-permute-start.3 = (bf16[88,1024]{1,0:T(8,128)(2,1)S(1)}, bf16[88,1024]{1,0:T(8,128)(2,1)S(1)}, u32[]{:S(2)}, u32[]{:S(2)}) collective-permute-start(bf16[88,1024]{1,0:T(8,128)(2,1)S(1)} %copy-done.37), channel_id=1, source_target_pairs={{0,2},{1,3},{2,0},{3,1},{4,6},{5,7},{6,4},{7,5},{8,10},{9,11},{10,... | collective-permute-start | bytes 540680 | tf_op jit(solution)/shard_map/ppermute | solution.py:386
  16.8 27.8 %collective-permute-start.4 = (bf16[88,1024]{1,0:T(8,128)(2,1)S(1)}, bf16[88,1024]{1,0:T(8,128)(2,1)S(1)}, u32[]{:S(2)}, u32[]{:S(2)}) collective-permute-start(bf16[88,1024]{1,0:T(8,128)(2,1)S(1)} %copy-done.37), channel_id=1, source_target_pairs={{0,4},{1,5},{2,6},{3,7},{4,0},{5,1},{6,2},{7,3},{8,12},{9,13},{10,... | collective-permute-start | bytes 540680 | tf_op jit(solution)/shard_map/ppermute | solution.py:386
  19.4 25.2 %collective-permute-start.5 = (bf16[88,1024]{1,0:T(8,128)(2,1)S(1)}, bf16[88,1024]{1,0:T(8,128)(2,1)S(1)}, u32[]{:S(2)}, u32[]{:S(2)}) collective-permute-start(bf16[88,1024]{1,0:T(8,128)(2,1)S(1)} %copy-done.37), channel_id=1, source_target_pairs={{0,6},{1,7},{2,4},{3,5},{4,2},{5,3},{6,0},{7,1},{8,14},{9,15},{10,... | collective-permute-start | bytes 540680 | tf_op jit(solution)/shard_map/ppermute | solution.py:386
  20.3 24.3 %collective-permute-start.1 = (bf16[32,1024]{1,0:T(8,128)(2,1)S(1)}, bf16[32,1024]{1,0:T(8,128)(2,1)S(1)}, u32[]{:S(2)}, u32[]{:S(2)}) collective-permute-start(bf16[32,1024]{1,0:T(8,128)(2,1)S(1)} %copy-done.42), channel_id=1, source_target_pairs={{0,4},{1,5},{2,6},{3,7},{4,0},{5,1},{6,2},{7,3},{8,12},{9,13},{10,... | collective-permute-start | bytes 196616 | tf_op jit(solution)/shard_map/ppermute | solution.py:386
  97.0 50.1 %collective-permute-start.9 = (bf16[512,1024]{1,0:T(8,128)(2,1)}, bf16[512,1024]{1,0:T(8,128)(2,1)}, u32[]{:S(2)}, u32[]{:S(2)}) collective-permute-start(bf16[512,1024]{1,0:T(8,128)(2,1)} %bitcast_select_fusion.5), channel_id=1, source_target_pairs={{0,8},{1,9},{2,10},{3,11},{4,12},{5,13},{6,14},{7,15},{8,0},{9,1},... | collective-permute-start | bytes 3145736 | tf_op jit(solution)/shard_map/ppermute | solution.py:386
  98.5 48.6 %collective-permute-start.10 = (bf16[352,1024]{1,0:T(8,128)(2,1)}, bf16[352,1024]{1,0:T(8,128)(2,1)}, u32[]{:S(2)}, u32[]{:S(2)}) collective-permute-start(bf16[352,1024]{1,0:T(8,128)(2,1)} %bitcast_select_fusion.6), channel_id=1, source_target_pairs={{0,1},{1,0},{2,3},{3,2},{4,5},{5,4},{6,7},{7,6},{8,9},{9,8},{10,11... | collective-permute-start | bytes 2162696 | tf_op jit(solution)/shard_map/ppermute | solution.py:386
  100.0 47.1 %collective-permute-start.11 = (bf16[352,1024]{1,0:T(8,128)(2,1)}, bf16[352,1024]{1,0:T(8,128)(2,1)}, u32[]{:S(2)}, u32[]{:S(2)}) collective-permute-start(bf16[352,1024]{1,0:T(8,128)(2,1)} %bitcast_select_fusion.6), channel_id=1, source_target_pairs={{0,16},{1,17},{2,18},{3,19},{4,20},{5,21},{6,22},{7,23},{8,24},{9,... | collective-permute-start | bytes 2162696 | tf_op jit(solution)/shard_map/ppermute | solution.py:386
  100.5 46.6 %collective-permute-start.12 = (bf16[352,1024]{1,0:T(8,128)(2,1)}, bf16[352,1024]{1,0:T(8,128)(2,1)}, u32[]{:S(2)}, u32[]{:S(2)}) collective-permute-start(bf16[352,1024]{1,0:T(8,128)(2,1)} %bitcast_select_fusion.6), channel_id=1, source_target_pairs={{0,17},{1,16},{2,19},{3,18},{4,21},{5,20},{6,23},{7,22},{8,25},{9,... | collective-permute-start | bytes 2162696 | tf_op jit(solution)/shard_map/ppermute | solution.py:386
  257.3 22.7 %collective-permute-start.14 = (bf16[1,512,2816]{2,1,0:T(8,128)(2,1)S(1)}, bf16[1,512,2816]{2,1,0:T(8,128)(2,1)S(1)}, u32[]{:S(2)}, u32[]{:S(2)}) collective-permute-start(bf16[1,512,2816]{2,1,0:T(8,128)(2,1)S(1)} %bitcast.304), channel_id=1, source_target_pairs={{0,8},{1,9},{2,10},{3,11},{4,12},{5,13},{6,14},{7,15},{8,0},{9,1},... | collective-permute-start | bytes 8650760 | tf_op jit(solution)/shard_map/ppermute | solution.py:386
  257.7 22.4 %collective-permute-start.15 = (bf16[1,512,2816]{2,1,0:T(8,128)(2,1)S(1)}, bf16[1,512,2816]{2,1,0:T(8,128)(2,1)S(1)}, u32[]{:S(2)}, u32[]{:S(2)}) collective-permute-start(bf16[1,512,2816]{2,1,0:T(8,128)(2,1)S(1)} %bitcast.302), channel_id=1, source_target_pairs={{0,8},{1,9},{2,10},{3,11},{4,12},{5,13},{6,14},{7,15},{8,0},{9,1},... | collective-permute-start | bytes 8650760 | tf_op jit(solution)/shard_map/ppermute | solution.py:386
  257.9 22.2 %collective-permute-start.16 = (bf16[1,1408,1024]{2,1,0:T(8,128)(2,1)S(1)}, bf16[1,1408,1024]{2,1,0:T(8,128)(2,1)S(1)}, u32[]{:S(2)}, u32[]{:S(2)}) collective-permute-start(bf16[1,1408,1024]{2,1,0:T(8,128)(2,1)S(1)} %bitcast.303), channel_id=1, source_target_pairs={{0,8},{1,9},{2,10},{3,11},{4,12},{5,13},{6,14},{7,15},{8,0},{9,1},... | collective-permute-start | bytes 8650760 | tf_op jit(solution)/shard_map/ppermute | solution.py:386
  292.5 35.5 %collective-permute-start.17 = (bf16[1,256,2816]{2,1,0:T(8,128)(2,1)}, bf16[1,256,2816]{2,1,0:T(8,128)(2,1)}, u32[]{:S(2)}, u32[]{:S(2)}) collective-permute-start(bf16[1,256,2816]{2,1,0:T(8,128)(2,1)} %bitcast.62), channel_id=1, source_target_pairs={{0,1},{1,0},{2,3},{3,2},{4,5},{5,4},{6,7},{7,6},{8,9},{9,8},{10,11... | collective-permute-start | bytes 4325384 | tf_op jit(solution)/shard_map/ppermute | solution.py:386
  294.0 33.9 %collective-permute-start.18 = (bf16[1,256,2816]{2,1,0:T(8,128)(2,1)}, bf16[1,256,2816]{2,1,0:T(8,128)(2,1)}, u32[]{:S(2)}, u32[]{:S(2)}) collective-permute-start(bf16[1,256,2816]{2,1,0:T(8,128)(2,1)} %dynamic-slice_bitcast_fusion.1), channel_id=1, source_target_pairs={{0,16},{1,17},{2,18},{3,19},{4,20},{5,21},{6,22},{7,23},{8,24},{9,... | collective-permute-start | bytes 4325384 | tf_op jit(solution)/shard_map/ppermute | solution.py:386
  333.3 23.0 %collective-permute-start.21 = (bf16[5,512,512]{2,1,0:T(8,128)(2,1)S(1)}, bf16[5,512,512]{2,1,0:T(8,128)(2,1)S(1)}, u32[]{:S(2)}, u32[]{:S(2)}) collective-permute-start(bf16[5,512,512]{2,1,0:T(8,128)(2,1)S(1)} %bitcast.306), channel_id=1, source_target_pairs={{0,8},{1,9},{2,10},{3,11},{4,12},{5,13},{6,14},{7,15},{8,0},{9,1},... | collective-permute-start | bytes 7864328 | tf_op jit(solution)/shard_map/ppermute | solution.py:386
  337.4 17.7 %collective-permute-start.19 = (bf16[1,128,2816]{2,1,0:T(8,128)(2,1)S(1)}, bf16[1,128,2816]{2,1,0:T(8,128)(2,1)S(1)}, u32[]{:S(2)}, u32[]{:S(2)}) collective-permute-start(bf16[1,128,2816]{2,1,0:T(8,128)(2,1)S(1)} %dynamic-slice_bitcast_fusion.2), channel_id=1, source_target_pairs={{0,16},{1,17},{2,18},{3,19},{4,20},{5,21},{6,22},{7,23},{8,24},{9,... | collective-permute-start | bytes 2162696 | tf_op jit(solution)/shard_map/ppermute | solution.py:386
  338.9 17.5 %collective-permute-start.20 = (bf16[1,128,2816]{2,1,0:T(8,128)(2,1)S(1)}, bf16[1,128,2816]{2,1,0:T(8,128)(2,1)S(1)}, u32[]{:S(2)}, u32[]{:S(2)}) collective-permute-start(bf16[1,128,2816]{2,1,0:T(8,128)(2,1)S(1)} %bitcast.325), channel_id=1, source_target_pairs={{0,1},{1,0},{2,3},{3,2},{4,5},{5,4},{6,7},{7,6},{8,9},{9,8},{10,11... | collective-permute-start | bytes 2162696 | tf_op jit(solution)/shard_map/ppermute | solution.py:386
  361.2 32.4 %collective-permute-start.22 = (bf16[1,704,1024]{2,1,0:T(8,128)(2,1)}, bf16[1,704,1024]{2,1,0:T(8,128)(2,1)}, u32[]{:S(2)}, u32[]{:S(2)}) collective-permute-start(bf16[1,704,1024]{2,1,0:T(8,128)(2,1)} %dynamic-slice_bitcast_fusion), channel_id=1, source_target_pairs={{0,16},{1,17},{2,18},{3,19},{4,20},{5,21},{6,22},{7,23},{8,24},{9,... | collective-permute-start | bytes 4325384 | tf_op jit(solution)/shard_map/ppermute | solution.py:386
  361.7 29.3 %collective-permute-start.23 = (bf16[5,256,512]{2,1,0:T(8,128)(2,1)}, bf16[5,256,512]{2,1,0:T(8,128)(2,1)}, u32[]{:S(2)}, u32[]{:S(2)}) collective-permute-start(bf16[5,256,512]{2,1,0:T(8,128)(2,1)} %bitcast.82), channel_id=1, source_target_pairs={{0,1},{1,0},{2,3},{3,2},{4,5},{5,4},{6,7},{7,6},{8,9},{9,8},{10,11... | collective-permute-start | bytes 3932168 | tf_op jit(solution)/shard_map/ppermute | solution.py:386
  363.2 26.5 %collective-permute-start.24 = (bf16[1,64,2816]{2,1,0:T(8,128)(2,1)}, bf16[1,64,2816]{2,1,0:T(8,128)(2,1)}, u32[]{:S(2)}, u32[]{:S(2)}) collective-permute-start(bf16[1,64,2816]{2,1,0:T(8,128)(2,1)} %bitcast.85), channel_id=1, source_target_pairs={{0,2},{1,3},{2,0},{3,1},{4,6},{5,7},{6,4},{7,5},{8,10},{9,11},{10,... | collective-permute-start | bytes 1081352 | tf_op jit(solution)/shard_map/ppermute | solution.py:386
  364.5 25.2 %collective-permute-start.25 = (bf16[1,64,2816]{2,1,0:T(8,128)(2,1)}, bf16[1,64,2816]{2,1,0:T(8,128)(2,1)}, u32[]{:S(2)}, u32[]{:S(2)}) collective-permute-start(bf16[1,64,2816]{2,1,0:T(8,128)(2,1)} %bitcast.88), channel_id=1, source_target_pairs={{0,2},{1,3},{2,0},{3,1},{4,6},{5,7},{6,4},{7,5},{8,10},{9,11},{10,... | collective-permute-start | bytes 1081352 | tf_op jit(solution)/shard_map/ppermute | solution.py:386
  403.3 21.1 %collective-permute-start.26 = (bf16[3,512,512]{2,1,0:T(8,128)(2,1)}, bf16[3,512,512]{2,1,0:T(8,128)(2,1)S(1)}, u32[]{:S(2)}, u32[]{:S(2)}) collective-permute-start(bf16[3,512,512]{2,1,0:T(8,128)(2,1)} %bitcast.90), channel_id=1, source_target_pairs={{0,8},{1,9},{2,10},{3,11},{4,12},{5,13},{6,14},{7,15},{8,0},{9,1},... | collective-permute-start | bytes 4718600 | tf_op jit(solution)/shard_map/ppermute | solution.py:386
  403.3 21.1 %collective-permute-start.27 = (bf16[1,352,1024]{2,1,0:T(8,128)(2,1)}, bf16[1,352,1024]{2,1,0:T(8,128)(2,1)}, u32[]{:S(2)}, u32[]{:S(2)}) collective-permute-start(bf16[1,352,1024]{2,1,0:T(8,128)(2,1)} %bitcast.93), channel_id=1, source_target_pairs={{0,1},{1,0},{2,3},{3,2},{4,5},{5,4},{6,7},{7,6},{8,9},{9,8},{10,11... | collective-permute-start | bytes 2162696 | tf_op jit(solution)/shard_map/ppermute | solution.py:386
  403.8 20.5 %collective-permute-start.28 = (bf16[5,128,512]{2,1,0:T(8,128)(2,1)}, bf16[5,128,512]{2,1,0:T(8,128)(2,1)}, u32[]{:S(2)}, u32[]{:S(2)}) collective-permute-start(bf16[5,128,512]{2,1,0:T(8,128)(2,1)} %dynamic-slice_bitcast_fusion.3), channel_id=1, source_target_pairs={{0,16},{1,17},{2,18},{3,19},{4,20},{5,21},{6,22},{7,23},{8,24},{9,... | collective-permute-start | bytes 1966088 | tf_op jit(solution)/shard_map/ppermute | solution.py:386
  405.2 17.4 %collective-permute-start.29 = (bf16[1,32,2816]{2,1,0:T(8,128)(2,1)}, bf16[1,32,2816]{2,1,0:T(8,128)(2,1)S(1)}, u32[]{:S(2)}, u32[]{:S(2)}) collective-permute-start(bf16[1,32,2816]{2,1,0:T(8,128)(2,1)} %dynamic-slice_bitcast_fusion.6), channel_id=1, source_target_pairs={{0,4},{1,5},{2,6},{3,7},{4,0},{5,1},{6,2},{7,3},{8,12},{9,13},{10,... | collective-permute-start | bytes 540680 | tf_op jit(solution)/shard_map/ppermute | solution.py:386
  428.3 20.3 %collective-permute-start.31 = (bf16[3,128,512]{2,1,0:T(8,128)(2,1)S(1)}, bf16[3,128,512]{2,1,0:T(8,128)(2,1)S(1)}, u32[]{:S(2)}, u32[]{:S(2)}) collective-permute-start(bf16[3,128,512]{2,1,0:T(8,128)(2,1)S(1)} %bitcast.328), channel_id=1, source_target_pairs={{0,16},{1,17},{2,18},{3,19},{4,20},{5,21},{6,22},{7,23},{8,24},{9,... | collective-permute-start | bytes 1179656 | tf_op jit(solution)/shard_map/ppermute | solution.py:386
  429.0 19.6 %collective-permute-start.32 = (bf16[3,128,512]{2,1,0:T(8,128)(2,1)S(1)}, bf16[3,128,512]{2,1,0:T(8,128)(2,1)S(1)}, u32[]{:S(2)}, u32[]{:S(2)}) collective-permute-start(bf16[3,128,512]{2,1,0:T(8,128)(2,1)S(1)} %bitcast.327), channel_id=1, source_target_pairs={{0,1},{1,0},{2,3},{3,2},{4,5},{5,4},{6,7},{7,6},{8,9},{9,8},{10,11... | collective-permute-start | bytes 1179656 | tf_op jit(solution)/shard_map/ppermute | solution.py:386
  430.4 18.2 %collective-permute-start.33 = (bf16[3,128,512]{2,1,0:T(8,128)(2,1)S(1)}, bf16[3,128,512]{2,1,0:T(8,128)(2,1)S(1)}, u32[]{:S(2)}, u32[]{:S(2)}) collective-permute-start(bf16[3,128,512]{2,1,0:T(8,128)(2,1)S(1)} %bitcast.326), channel_id=1, source_target_pairs={{0,17},{1,16},{2,19},{3,18},{4,21},{5,20},{6,23},{7,22},{8,25},{9,... | collective-permute-start | bytes 1179656 | tf_op jit(solution)/shard_map/ppermute | solution.py:386
  449.3 22.3 %collective-permute-start.39 = (bf16[1,88,1024]{2,1,0:T(8,128)(2,1)S(1)}, bf16[1,88,1024]{2,1,0:T(8,128)(2,1)S(1)}, u32[]{:S(2)}, u32[]{:S(2)}) collective-permute-start(bf16[1,88,1024]{2,1,0:T(8,128)(2,1)S(1)} %dynamic-slice_bitcast_fusion.4), channel_id=1, source_target_pairs={{0,4},{1,5},{2,6},{3,7},{4,0},{5,1},{6,2},{7,3},{8,12},{9,13},{10,... | collective-permute-start | bytes 540680 | tf_op jit(solution)/shard_map/ppermute | solution.py:386
  450.0 21.6 %collective-permute-start.40 = (bf16[5,32,512]{2,1,0:T(8,128)(2,1)S(1)}, bf16[5,32,512]{2,1,0:T(8,128)(2,1)S(1)}, u32[]{:S(2)}, u32[]{:S(2)}) collective-permute-start(bf16[5,32,512]{2,1,0:T(8,128)(2,1)S(1)} %dynamic-slice_bitcast_fusion.7), channel_id=1, source_target_pairs={{0,4},{1,5},{2,6},{3,7},{4,0},{5,1},{6,2},{7,3},{8,12},{9,13},{10,... | collective-permute-start | bytes 491528 | tf_op jit(solution)/shard_map/ppermute | solution.py:386
  452.6 19.0 %collective-permute-start.37 = (bf16[3,32,512]{2,1,0:T(8,128)(2,1)S(1)}, bf16[3,32,512]{2,1,0:T(8,128)(2,1)S(1)}, u32[]{:S(2)}, u32[]{:S(2)}) collective-permute-start(bf16[3,32,512]{2,1,0:T(8,128)(2,1)S(1)} %get-tuple-element.233), channel_id=1, source_target_pairs={{0,4},{1,5},{2,6},{3,7},{4,0},{5,1},{6,2},{7,3},{8,12},{9,13},{10,... | collective-permute-start | bytes 294920 | tf_op jit(solution)/shard_map/ppermute | solution.py:386
  (72 other events, 837.2 us)
Sparse Core Ops, SparseCore 0:
  11.5 82.2 all-gather.2
  97.2 100.0 all-gather.4

commit v5 on v4

--- a/solution.py
+++ b/solution.py
@@ -192,7 +192,7 @@
     *rest,
 ):
     normed_t_ref = rest[0]
-    grads_ref, first_ref, weights_ref, dk_ref, dv_ref = rest[-5:]
+    grads_ref, first_ref, kept_ref, sent_ref, dk_ref, dv_ref = rest[-6:]
     half_size = head_size // 2
     score_scale = head_size ** (-0.5)
     width = q_ref.shape[1]
@@ -261,8 +261,14 @@
                 ).astype(jnp.bfloat16)
             first_ref[rows, low : low + PAIR] = 0.5 * dv
             grads_ref[2, rows, low : low + PAIR] = (0.5 * dv).astype(jnp.bfloat16)
-    for index in range(3):
-        weights_ref[index] = forward_dot(normed_t_ref[...], grads_ref[index]).astype(jnp.bfloat16)
+    products = [(normed_t_ref, grads_ref.at[index]) for index in range(3)]
+    if kept_ref.shape[0] > 3:
+        products += [(rest[1], rest[2]), (rest[1], rest[3])]
+    half = kept_ref.shape[1]
+    for index, (left_ref, right_ref) in enumerate(products):
+        right = right_ref[...]
+        kept_ref[index] = forward_dot(left_ref[:half], right).astype(jnp.bfloat16)
+        sent_ref[index] = forward_dot(left_ref[half:], right).astype(jnp.bfloat16)
 
 
 def attend_back(
@@ -275,6 +281,8 @@
     cosine,
     sine,
     normed_t,
+    context_t,
+    grad_hidden_low,
     head_size,
     width,
     first_step,
@@ -286,6 +294,8 @@
     heads = width // head_size
     block = pl.BlockSpec((token_count, width), lambda step: (0, first_step + step))
     table = pl.BlockSpec((token_count, PAIR), lambda step: (0, 0))
+    lead = 3 if context_t is None else 5
+    out_args = [] if context_t is None else [context_t, grad_hidden_low, grad_hidden_low]
     shared = [] if first is None else [first]
     return pl.pallas_call(
         partial(attend_back_kernel, slot_count, head_size),
@@ -302,27 +312,101 @@
             table,
             table,
             pl.BlockSpec((model_width, token_count), lambda step: (0, 0)),
-        ]
+            pl.BlockSpec((model_width, token_count), lambda step: (0, 0)),
+            pl.BlockSpec((token_count, width), lambda step: (0, step)),
+            pl.BlockSpec((token_count, width), lambda step: (0, steps + step)),
+        ][: 9 + len(out_args)]
         + [pl.BlockSpec(memory_space=pl.ANY)] * len(shared),
         out_specs=[
             pl.BlockSpec((3, token_count, width), lambda step: (0, 0, step)),
             block,
-            pl.BlockSpec((3, model_width, width), lambda step: (0, 0, step)),
-        ],
+        ]
+        + [pl.BlockSpec((lead, model_width // 2, width), lambda step: (0, 0, step))] * 2,
         out_shape=[
             jax.ShapeDtypeStruct((3, token_count, steps * width), jnp.bfloat16),
             jax.ShapeDtypeStruct((token_count, model_width), jnp.float32),
-            jax.ShapeDtypeStruct((3, model_width, steps * width), jnp.bfloat16),
-        ],
+        ]
+        + [jax.ShapeDtypeStruct((lead, model_width // 2, steps * width), jnp.bfloat16)] * 2,
         scratch_shapes=[
             pltpu.VMEM((PAIR // head_size, slot_count, PAIR), jnp.float32),
             pltpu.VMEM((PAIR // head_size, slot_count, PAIR), jnp.float32),
         ],
-        input_output_aliases={9: 1} if shared else {},
+        input_output_aliases={9 + len(out_args): 1} if shared else {},
         compiler_params=pltpu.CompilerParams(vmem_limit_bytes=56 << 20),
         cost_estimate=pl.CostEstimate(flops=1, transcendentals=0, bytes_accessed=1),
         name="attend_back",
-    )(queries, keys, values, grads, lse, bias, cosine, sine, normed_t, *shared)
+    )(queries, keys, values, grads, lse, bias, cosine, sine, normed_t, *out_args, *shared)
+
+
+def feed_kernel(
+    normed_ref,
+    normed_t_ref,
+    grad_y_ref,
+    grad_product_ref,
+    gate_ref,
+    up_ref,
+    product_ref,
+    grad_gate_ref,
+    grad_up_ref,
+    gate_kept_ref,
+    gate_sent_ref,
+    up_kept_ref,
+    up_sent_ref,
+    down_ref,
+):
+    gate_values = forward_dot(normed_ref[...], gate_ref[...])
+    upward = forward_dot(normed_ref[...], up_ref[...])
+    grad_product = grad_product_ref[...]
+    sigmoid_gate = jax.nn.sigmoid(gate_values)
+    silu_gate = gate_values * sigmoid_gate
+    product = (silu_gate * upward).astype(jnp.bfloat16)
+    product_ref[...] = product
+    grad_up_ref[...] = (grad_product * silu_gate).astype(jnp.bfloat16)
+    grad_gate_ref[...] = (
+        grad_product * upward * sigmoid_gate * (1.0 + gate_values * (1.0 - sigmoid_gate))
+    ).astype(jnp.bfloat16)
+    half = gate_kept_ref.shape[0]
+    for grads_ref, kept_ref, sent_ref in (
+        (grad_gate_ref, gate_kept_ref, gate_sent_ref),
+        (grad_up_ref, up_kept_ref, up_sent_ref),
+    ):
+        grads = grads_ref[...]
+        kept_ref[...] = forward_dot(normed_t_ref[:half], grads).astype(jnp.bfloat16)
+        sent_ref[...] = forward_dot(normed_t_ref[half:], grads).astype(jnp.bfloat16)
+    down_ref[...] = forward_dot(product.T, grad_y_ref[...]).astype(jnp.bfloat16)
+
+
+def feed(normed, normed_t, grad_y, grad_product, weights):
+    token_count, model_width = normed.shape
+    hidden_width = grad_product.shape[1]
+    width = 256
+    steps = hidden_width // width
+    whole = lambda step: (0, 0)
+    wide = pl.BlockSpec((token_count, width), lambda step: (0, step))
+    half = pl.BlockSpec((model_width // 2, width), lambda step: (0, step))
+    wide_shape = jax.ShapeDtypeStruct((token_count, hidden_width), jnp.bfloat16)
+    half_shape = jax.ShapeDtypeStruct((model_width // 2, hidden_width), jnp.bfloat16)
+    return pl.pallas_call(
+        feed_kernel,
+        grid=(steps,),
+        in_specs=[
+            pl.BlockSpec((token_count, model_width), whole),
+            pl.BlockSpec((model_width, token_count), whole),
+            pl.BlockSpec((token_count, model_width), whole),
+            wide,
+            pl.BlockSpec((model_width, width), lambda step: (0, step)),
+            pl.BlockSpec((model_width, width), lambda step: (0, steps + step)),
+        ],
+        out_specs=[wide] * 3
+        + [half] * 4
+        + [pl.BlockSpec((width, model_width), lambda step: (step, 0))],
+        out_shape=[wide_shape] * 3
+        + [half_shape] * 4
+        + [jax.ShapeDtypeStruct((hidden_width, model_width), jnp.bfloat16)],
+        compiler_params=pltpu.CompilerParams(vmem_limit_bytes=56 << 20),
+        cost_estimate=pl.CostEstimate(flops=1, transcendentals=0, bytes_accessed=1),
+        name="feed",
+    )(normed, normed_t, grad_y, grad_product, weights, weights)
 
 
 def finish_kernel(
@@ -394,8 +478,9 @@
 
 
 class Exchange:
-    def __init__(self, partial_sum, steps, place, device_count):
+    def __init__(self, partial_sum, steps, place, device_count, first=None):
         self.current = partial_sum
+        self.first = first
         self.steps = [list(step) for step in steps]
         self.left = sorted([bit for step in steps for bit in step], reverse=True)
         self.place = place
@@ -416,6 +501,10 @@
         return value
 
     def outgoing(self):
+        if self.first is not None:
+            self.kept, sent = self.first
+            self.first = None
+            return [sent]
         masks = masks_of(self.steps[0])
         self.kept = self.part(0)
         return [self.part(mask) for mask in masks[1:]]
@@ -465,6 +554,22 @@
             ]
             self.have.append(bit)
         self.current = pieces[0]
+
+
+def split_columns(matrix, bit, place, device_count):
+    row_count, column_count = matrix.shape
+    low = (column_count // device_count) << bit
+    mine = (place >> bit) & 1
+    return [
+        jnp.concatenate(
+            [
+                lax.dynamic_slice(matrix, (0, start + side * low), (row_count, low))
+                for start in range(0, column_count, 2 * low)
+            ],
+            axis=1,
+        )
+        for side in (mine, 1 - mine)
+    ]
 
 
 def tick(chain, settled, launched):
@@ -580,25 +685,23 @@
     grad_y = cotangent.astype(jnp.float32) * valid.astype(jnp.float32)[:, None]
     grad_y_low = grad_y.astype(jnp.bfloat16)
     grad_product = contract_last(grad_y_low, down_w)
-    normed_two, grad_product = lax.optimization_barrier((normed_two, grad_product))
-    gate_values = forward_dot(normed_two, gate_w)
-    upward = forward_dot(normed_two, up_w)
-    sigmoid_gate = jax.nn.sigmoid(gate_values)
-    silu_gate = gate_values * sigmoid_gate
-    product = (silu_gate * upward).astype(jnp.bfloat16)
-    grad_upward = (grad_product * silu_gate).astype(jnp.bfloat16)
-    grad_gate_low = (
-        grad_product * upward * sigmoid_gate * (1.0 + gate_values * (1.0 - sigmoid_gate))
-    ).astype(jnp.bfloat16)
-    gate = exchange(
-        contract_first(normed_two, grad_gate_low).astype(jnp.bfloat16)[None], plans["low_first"]
-    )
-    up = exchange(
-        contract_first(normed_two, grad_upward).astype(jnp.bfloat16)[None], plans["high_first"]
-    )
-    down = exchange(
-        contract_first(product, grad_y_low).astype(jnp.bfloat16)[None], plans["high_first"]
-    )
+    core_bit = fsdp_size.bit_length() - 1
+    normed_t, context_t, two_t = [
+        jnp.concatenate(split_columns(matrix, core_bit, place, device_count), axis=1).T
+        for matrix in (normed, context, normed_two)
+    ]
+    normed_two, grad_product, normed_t, context_t, two_t = lax.optimization_barrier(
+        (normed_two, grad_product, normed_t, context_t, two_t)
+    )
+    product, grad_gate_low, grad_upward, *feed_parts = feed(
+        normed_two, two_t, grad_y_low, grad_product, second_set
+    )
+    gate_parts, up_parts = [
+        [part[None] for part in feed_parts[start : start + 2]] for start in (0, 2)
+    ]
+    gate = exchange(None, plans["low_first"], first=gate_parts)
+    up = exchange(None, plans["high_first"], first=up_parts)
+    down = exchange(feed_parts[4][None], plans["high_first"])
     grad_upward, grad_gate_low = tick((grad_upward, grad_gate_low), [], [gate, up, down])
     grad_normed_two = contract_last(grad_gate_low, gate_w) + contract_last(grad_upward, up_w)
     grad_normed_two = tick(grad_normed_two, [gate, up, down], [gate, up])
@@ -610,18 +713,7 @@
     )
     grad_hidden_low = grad_hidden.astype(jnp.bfloat16)
     grad_context = contract_last(grad_hidden_low, out_w).astype(jnp.bfloat16)
-    grad_out_w = jnp.stack(
-        [
-            contract_first(context, grad_hidden_low[:, low : low + half_width])
-            for low in (0, half_width)
-        ]
-    ).astype(jnp.bfloat16)
-    normed_t = normed.T
-    grad_context, grad_out_w, normed_t = lax.optimization_barrier(
-        (grad_context, grad_out_w, normed_t)
-    )
-
-    def attend_back_half(half, grad_context, first):
+    def attend_back_half(half, grad_context, first, outs):
         return attend_back(
             query_rot,
             key_rot,
@@ -632,6 +724,7 @@
             cosine,
             sine,
             normed_t,
+            *outs,
             head_size,
             width,
             half * half_steps,
@@ -639,15 +732,17 @@
             first,
         )
 
-    low_one, first_part, weights_one = attend_back_half(0, grad_context, None)
-    one = exchange(jnp.concatenate([weights_one, grad_out_w]), plans["low_first"])
+    low_one, first_part, *parts_one = attend_back_half(
+        0, grad_context, None, (context_t, grad_hidden_low)
+    )
+    one = exchange(None, plans["low_first"], first=parts_one)
     grad_context, product = tick((grad_context, product), [gate, up], [gate, up, one])
     out_tokens = (hidden + forward_dot(product, down_w)).astype(jnp.bfloat16)
     grad_context, out_tokens = tick(
         (grad_context, out_tokens), [gate, up, one], [down, one, gate, up]
     )
-    low_two, grad_first, weights_two = attend_back_half(1, grad_context, first_part)
-    two = exchange(weights_two, plans["short"])
+    low_two, grad_first, *parts_two = attend_back_half(1, grad_context, first_part, (None, None))
+    two = exchange(None, plans["short"], first=parts_two)
     low_two = tick(low_two, [down, one, gate, up], [two, down, one, gate, up])
     grad_tokens = finish(
         low_one, low_two, first_set, grad_hidden, tokens, scale_one, gain_first_f

time: 488 us -> 468 us (0.959)
  matrix products: 106 us -> 43.5 us
  Pallas kernels: 90.6 us -> 135 us
  waiting for transfers between devices: 111 us -> 95.2 us
  local copies, waits for them, and re-layouts: 47.7 us -> 59.8 us
    pallas_call x0 -> x1, Pallas kernels: none -> 40.1 us  [feed(): pl.pallas_call(feed_kernel, grid=(steps,), in_specs=[pl.BlockSpec((token_...]
    dot_general x4 -> x2, matrix products: 44.9 us -> 11.9 us  [forward_dot(): return jnp.dot(left, right, preferred_element_type=jnp.float32)]
    dot_general x5 -> x0, matrix products: 25.5 us -> none  [contract_first(): lax.dot_general(left, right, (((0,), (0,)), ((), ())), preferred_element_...]
    all_gather x1, waiting for transfers between devices: 18.6 us -> 0.01 us  [shards(): lax.all_gather(jnp.concatenate([w_gate, w_up], axis=1), AXES, axis=0, til...]
    optimization_barrier x1 -> x3, local copies, waits for them, and re-layouts: 2.56 us -> 11.1 us  [the longest x2 6.76 us: shards(): lax.optimization_barrier((normed_two, grad_product, normed_t, context_t,...]
    unnamed x122 -> x130, local copies, waits for them, and re-layouts: 15.1 us -> 17 us
    dynamic_slice x18 -> x14, local copies, waits for them, and re-layouts: 13.5 us -> 13.2 us  [part(): value = lax.dynamic_index_in_dim(view, chosen, 2, keepdims=False)]
  transfers between devices with their start and end apart: 43 -> 43, of which waited for: 15 -> 15; matrix products, arithmetic and copies ran while one was open for 22% -> 25% of each run, Pallas kernels for 19% -> 20%
where the time goes in v5:
time: 468 us; the launch traced here: 462 us
  Pallas kernels  135 us (29%)
  waiting for transfers between devices  95.2 us (20%)
  other arithmetic  66.7 us (14%)
  local copies, waits for them, and re-layouts  59.8 us (13%)
  starting transfers between devices  47 us (10%)
  matrix products  43.5 us (9%)
  between operations  15.4 us (3%)
    ppermute x41, waiting for transfers between devices, flip(): return lax.ppermute(value, AXES, pairs)  67.6 us
    ppermute x41, starting transfers between devices, flip(): return lax.ppermute(value, AXES, pairs)  46.9 us
    pallas_call x2, Pallas kernels, attend_back(): pl.pallas_call(partial(attend_back_kernel, slot_count, head_size), grid=(...  45.4 us
    pallas_call x1, Pallas kernels, feed(): pl.pallas_call(feed_kernel, grid=(steps,), in_specs=[pl.BlockSpec((token_...  40.1 us
    pallas_call x1, Pallas kernels, attend(): pl.pallas_call(partial(attend_kernel, slot_count, head_size), grid=(steps...  35.8 us
    dot_general x4, matrix products, contract_last(): lax.dot_general(left, right, (((1,), (1,)), ((), ())), preferred_element_...  31.5 us
    all_gather x1, waiting for transfers between devices, shards(): lax.all_gather(jnp.concatenate([*projections, gain_columns], axis=1), AXE...  27.6 us
    convert_element_type x18, other arithmetic, settle(): self.current = total.astype(jnp.bfloat16) if self.steps else total  17.5 us
  transfers between devices with their start and end apart: 43, of which 15 were waited for; matrix products, arithmetic and copies ran while one was open for 25% of the time, Pallas kernels for 20%

profile of v5, /device:TPU:0, one launch (start us, length us, event | category | flops | bytes accessed | tf_op | source)
XLA Modules:
  0.0 462.4 jit_solution(12658407100034761742)
XLA Ops:
  13.7 3.1 collective-permute-start.3
  16.8 2.6 collective-permute-start.4
  20.3 3.5 collective-permute-start.1
  29.0 3.8 collective-permute-done
  32.8 3.5 collective-permute-start.2
  36.4 8.2 %collective-permute-done.1 = bf16[32,1024]{1,0:T(8,128)(2,1)S(1)} collective-permute-done((bf16[32,1024]{1,0:T(8,128)(2,1)S(1)}, bf16[32,1024]{1,0:T(8,128)(2,1)S(1)}, u32[]{:S(2)}, u32[]{:S(2)}) %collective-permute-start.1) | collective-permute-done | bytes 65568 | tf_op jit(solution)/shard_map/ppermute | solution.py:470
  51.2 3.7 collective-permute-done.6
  54.9 5.2 %collective-permute-done.7 = bf16[128,1024]{1,0:T(8,128)(2,1)S(1)} collective-permute-done((bf16[128,1024]{1,0:T(8,128)(2,1)}, bf16[128,1024]{1,0:T(8,128)(2,1)S(1)}, u32[]{:S(2)}, u32[]{:S(2)}) %collective-permute-start.7) | collective-permute-done | bytes 262176 | tf_op jit(solution)/shard_map/ppermute | solution.py:470
  60.1 4.1 collective-permute-done.8
  66.5 27.6 %all-gather.3.cloned.1.call-done.wq_ref.wk_ref.wv_ref = bf16[1024,3200]{1,0:T(8,128)(2,1)} async-done(((bf16[32,3200]{1,0:T(8,128)(2,1)}), bf16[1024,3200]{1,0:T(8,128)(2,1)}) %all-gather.3.cloned.1.call-update) | async-done | bytes 6553616 | tf_op jit(solution)/shard_map/all_gather | solution.py:639
  113.5 35.8 %attend.1 = (bf16[1024,1024]{1,0:T(8,128)(2,1)}, bf16[1024,1024]{1,0:T(8,128)(2,1)}, bf16[1024,1024]{1,0:T(8,128)(2,1)}, bf16[1024,1024]{1,0:T(8,128)(2,1)}, f32[2,4,4,512]{3,2,1,0:T(4,128)}) custom-call(bf16[1024,1024]{1,0:T(8,128)(2,1)} %fusion.9.normed_ref, bf16[1024,3200]{1,0:T(8,128)(2,1)} %all-gather.3.cloned.1.call-done.wq_ref.wk_ref.wv_ref, ...), custom_call_target="tpu_custom_call" | custom-call | tf_op jit(solution)/shard_map/attend/pallas_call | solution.py:154
  159.3 4.3 copy.131
  174.2 5.7 %bitcast_select_fusion = bf16[2816,1024]{1,0:T(8,128)(2,1)} fusion(pred[2816]{0:T(1024)(128)(4,1)S(1)} %copy-done.54, bf16[2,704,1024]{2,1,0:T(8,128)(2,1)} %bitcast.52, bf16[2,704,1024]{2,1,0:T(8,128)(2,1)S(1)} %broadcast_select_fusion), kind=kLoop, calls=%fused_computation.13 | loop fusion | flops 2883584 | bytes 11537152 | tf_op jit(solution)/shard_map/jit(_where)/select_n | solution.py:550
  184.3 8.8 %fusion.48.grad_product_ref = f32[1024,2816]{1,0:T(8,128)} fusion(bf16[1024,1024]{1,0:T(8,128)(2,1)S(1)} %copy-done.12, bf16[2816,1024]{1,0:T(8,128)(2,1)S(1)} %copy-done.17), kind=kOutput, calls=%fused_computation.203 | convolution fusion | flops 5905580032 | bytes 19398656 | tf_op jit(solution)/shard_map/dot_general | solution.py:22
  193.1 4.1 copy.135.normed_t_ref
  197.2 2.7 copy.139.rest_0_
  199.9 40.1 %feed.1 = (bf16[1024,2816]{1,0:T(8,128)(2,1)}, bf16[1024,2816]{1,0:T(8,128)(2,1)}, bf16[1024,2816]{1,0:T(8,128)(2,1)}, bf16[512,2816]{1,0:T(8,128)(2,1)}, bf16[5...) custom-call(bf16[1024,1024]{1,0:T(8,128)(2,1)} %copy-done.5, ...), custom_call_target="tpu_custom_call" | custom-call | flops 1 | bytes 1 | tf_op jit(solution)/shard_map/feed/pallas_call | solution.py:389
  240.0 6.5 %constant_dynamic-slice_fusion.21 = (bf16[1,2,1,704,1024]{4,3,2,1,0:T(8,128)(2,1)}, bf16[1,2,1,704,1024]{4,3,2,1,0:T(8,128)(2,1)}) fusion(bf16[1,2,2,704,1024]{4,3,2,1,0:T(8,128)(2,1)} %bitcast.274, s32[]{:T(128)S(6)} %select_n.330, s32[]{:T(128)S(6)} %select_n.325), kind=kLoop, calls=%fused_computation.162 | loop fusion | bytes 11534344 | tf_op jit(solution)/shard_map/jit(dynamic_index_in_dim)/dynamic_slice | solution.py:498
  248.1 9.9 %fusion = f32[1024,1024]{1,0:T(8,128)} fusion(bf16[1024,2816]{1,0:T(8,128)(2,1)} %get-tuple-element.177, bf16[1024,5632]{1,0:T(8,128)(2,1)S(1)} %copy-done), kind=kOutput, calls=%fused_computation.3 | convolution fusion | flops 5905580032 | bytes 15728640 | tf_op jit(solution)/shard_map/dot_general | solution.py:22
  258.0 9.0 %fusion.15 = f32[1024,1024]{1,0:T(8,128)S(1)} fusion(f32[1024,1024]{1,0:T(8,128)} %fusion, bf16[1024,2816]{1,0:T(8,128)(2,1)} %get-tuple-element.176, bf16[1024,5632]{1,0:T(8,128)(2,1)S(1)} %copy-done), kind=kOutput, calls=%fused_computation.41 | convolution fusion | flops 5906628608 | bytes 19922944 | tf_op jit(solution)/shard_map/dot_general | solution.py:22
  278.6 3.0 fusion.47
  281.6 3.8 convolution_convert_fusion.grad_ref
  285.5 24.7 %attend_back.2 = (bf16[3,1024,512]{2,1,0:T(8,128)(2,1)}, f32[1024,1024]{1,0:T(8,128)}, bf16[5,512,512]{2,1,0:T(8,128)(2,1)}, bf16[5,512,512]{2,1,0:T(8,128)(2,1)}) custom-call(bf16[1024,1024]{1,0:T(8,128)(2,1)} %get-tuple-element.194.q_ref, bf16[1024,1024]{1,0:T(8,128)(2,1)} %get-tuple-element.195.k_ref, bf16[1024,1024]{1,0:T(8,128)(2,1)} %get-tuple-element.196.v_ref, ...), custom_call_target="tpu_custom_call" | custom-call | flops 1 | bytes 1 | tf_op jit(solution)/shard_map/attend_back/pallas_call | solution.py:300
  321.5 9.5 %add_convert_fusion.1 = bf16[1024,1024]{1,0:T(8,128)(2,1)} fusion(f32[1024,1024]{1,0:T(8,128)S(1)} %copy-done.2, bf16[1024,2816]{1,0:T(8,128)(2,1)} %get-tuple-element.202, bf16[2816,1024]{1,0:T(8,128)(2,1)S(1)} %bitcast.273), kind=kOutput, calls=%fused_computation.18 | convolution fusion | flops 5907677184 | bytes 17825792 | tf_op jit(solution)/shard_map/dot_general | solution.py:18
  331.0 5.5 %collective-permute-done.19 = bf16[1,128,2816]{2,1,0:T(8,128)(2,1)S(1)} collective-permute-done((bf16[1,128,2816]{2,1,0:T(8,128)(2,1)S(1)}, bf16[1,128,2816]{2,1,0:T(8,128)(2,1)S(1)}, u32[]{:S(2)}, u32[]{:S(2)}) %collective-permute-start.19) | collective-permute-done | bytes 720928 | tf_op jit(solution)/shard_map/ppermute | solution.py:470
  345.6 20.7 %attend_back.3 = (bf16[3,1024,512]{2,1,0:T(8,128)(2,1)}, f32[1024,1024]{1,0:T(8,128)}, bf16[3,512,512]{2,1,0:T(8,128)(2,1)}, bf16[3,512,512]{2,1,0:T(8,128)(2,1)}) custom-call(bf16[1024,1024]{1,0:T(8,128)(2,1)} %get-tuple-element.194.q_ref, bf16[1024,1024]{1,0:T(8,128)(2,1)} %get-tuple-element.195.k_ref, ...), custom_call_target="tpu_custom_call", output_to_operand_aliasing={{1}: (9, {})} | custom-call | flops 1 | bytes 1 | tf_op jit(solution)/shard_map/attend_back/pallas_call | solution.py:300
  366.4 4.9 %collective-permute-done.23 = bf16[5,256,512]{2,1,0:T(8,128)(2,1)} collective-permute-done((bf16[5,256,512]{2,1,0:T(8,128)(2,1)}, bf16[5,256,512]{2,1,0:T(8,128)(2,1)}, u32[]{:S(2)}, u32[]{:S(2)}) %collective-permute-start.23) | collective-permute-done | bytes 1310752 | tf_op jit(solution)/shard_map/ppermute | solution.py:470
  388.7 13.5 %finish.1 = f32[1024,1024]{1,0:T(8,128)} custom-call(bf16[3,1024,512]{2,1,0:T(8,128)(2,1)} %get-tuple-element.214.low_one_ref, bf16[3,1024,512]{2,1,0:T(8,128)(2,1)} %get-tuple-element.228.low_two_ref, bf16[1024,3200]{1,0:T(8,128)(2,1)} %all-gather.3.cloned.1.call-done.wq_ref.wk_ref.wv_ref, ...), custom_call_target="tpu_custom_call" | custom-call | flops 1 | bytes 1 | tf_op jit(solution)/shard_map/finish/pallas_call | solution.py:446
  415.3 12.6 %collective-permute-done.35 = bf16[5,64,512]{2,1,0:T(8,128)(2,1)S(1)} collective-permute-done((bf16[5,64,512]{2,1,0:T(8,128)(2,1)S(1)}, bf16[5,64,512]{2,1,0:T(8,128)(2,1)S(1)}, u32[]{:S(2)}, u32[]{:S(2)}) %collective-permute-start.35) | collective-permute-done | bytes 327712 | tf_op jit(solution)/shard_map/ppermute | solution.py:470
  428.9 2.6 collective-permute-start.40
  433.4 2.5 collective-permute-start.38
  438.6 12.2 %collective-permute-done.37 = bf16[3,32,512]{2,1,0:T(8,128)(2,1)S(1)} collective-permute-done((bf16[3,32,512]{2,1,0:T(8,128)(2,1)S(1)}, bf16[3,32,512]{2,1,0:T(8,128)(2,1)S(1)}, u32[]{:S(2)}, u32[]{:S(2)}) %collective-permute-start.37) | collective-permute-done | bytes 98336 | tf_op jit(solution)/shard_map/ppermute | solution.py:470
  (342 shorter events, 139.1 us)
Async XLA Ops:
  7.2 86.9 %all-gather.3.cloned.1.call-start = ((), (), s32[]{:S(2)}) async-start(), calls=%async_computation | async-start | bytes 6758400 | tf_op jit(solution)/shard_map/all_gather | solution.py:639
  9.7 190.2 %all-gather.5.cloned.1.call-start = ((), (), s32[]{:S(2)}) async-start(), calls=%async_computation.1 | async-start | bytes 11894784 | tf_op jit(solution)/shard_map/all_gather | solution.py:642
  13.7 30.9 %collective-permute-start.3 = (bf16[88,1024]{1,0:T(8,128)(2,1)S(1)}, bf16[88,1024]{1,0:T(8,128)(2,1)S(1)}, u32[]{:S(2)}, u32[]{:S(2)}) collective-permute-start(bf16[88,1024]{1,0:T(8,128)(2,1)S(1)} %copy-done.45), channel_id=1, source_target_pairs={{0,2},{1,3},{2,0},{3,1},{4,6},{5,7},{6,4},{7,5},{8,10},{9,11},{10,... | collective-permute-start | bytes 540680 | tf_op jit(solution)/shard_map/ppermute | solution.py:470
  16.8 27.8 %collective-permute-start.4 = (bf16[88,1024]{1,0:T(8,128)(2,1)S(1)}, bf16[88,1024]{1,0:T(8,128)(2,1)S(1)}, u32[]{:S(2)}, u32[]{:S(2)}) collective-permute-start(bf16[88,1024]{1,0:T(8,128)(2,1)S(1)} %copy-done.45), channel_id=1, source_target_pairs={{0,4},{1,5},{2,6},{3,7},{4,0},{5,1},{6,2},{7,3},{8,12},{9,13},{10,... | collective-permute-start | bytes 540680 | tf_op jit(solution)/shard_map/ppermute | solution.py:470
  19.4 25.2 %collective-permute-start.5 = (bf16[88,1024]{1,0:T(8,128)(2,1)S(1)}, bf16[88,1024]{1,0:T(8,128)(2,1)S(1)}, u32[]{:S(2)}, u32[]{:S(2)}) collective-permute-start(bf16[88,1024]{1,0:T(8,128)(2,1)S(1)} %copy-done.45), channel_id=1, source_target_pairs={{0,6},{1,7},{2,4},{3,5},{4,2},{5,3},{6,0},{7,1},{8,14},{9,15},{10,... | collective-permute-start | bytes 540680 | tf_op jit(solution)/shard_map/ppermute | solution.py:470
  20.3 24.3 %collective-permute-start.1 = (bf16[32,1024]{1,0:T(8,128)(2,1)S(1)}, bf16[32,1024]{1,0:T(8,128)(2,1)S(1)}, u32[]{:S(2)}, u32[]{:S(2)}) collective-permute-start(bf16[32,1024]{1,0:T(8,128)(2,1)S(1)} %copy-done.50), channel_id=1, source_target_pairs={{0,4},{1,5},{2,6},{3,7},{4,0},{5,1},{6,2},{7,3},{8,12},{9,13},{10,... | collective-permute-start | bytes 196616 | tf_op jit(solution)/shard_map/ppermute | solution.py:470
  97.5 51.9 %collective-permute-start.9 = (bf16[512,1024]{1,0:T(8,128)(2,1)}, bf16[512,1024]{1,0:T(8,128)(2,1)}, u32[]{:S(2)}, u32[]{:S(2)}) collective-permute-start(bf16[512,1024]{1,0:T(8,128)(2,1)} %bitcast_select_fusion.5), channel_id=1, source_target_pairs={{0,8},{1,9},{2,10},{3,11},{4,12},{5,13},{6,14},{7,15},{8,0},{9,1},... | collective-permute-start | bytes 3145736 | tf_op jit(solution)/shard_map/ppermute | solution.py:470
  98.0 51.4 %collective-permute-start.10 = (bf16[352,1024]{1,0:T(8,128)(2,1)}, bf16[352,1024]{1,0:T(8,128)(2,1)}, u32[]{:S(2)}, u32[]{:S(2)}) collective-permute-start(bf16[352,1024]{1,0:T(8,128)(2,1)} %bitcast_select_fusion.6), channel_id=1, source_target_pairs={{0,1},{1,0},{2,3},{3,2},{4,5},{5,4},{6,7},{7,6},{8,9},{9,8},{10,11... | collective-permute-start | bytes 2162696 | tf_op jit(solution)/shard_map/ppermute | solution.py:470
  99.5 49.8 %collective-permute-start.11 = (bf16[352,1024]{1,0:T(8,128)(2,1)}, bf16[352,1024]{1,0:T(8,128)(2,1)}, u32[]{:S(2)}, u32[]{:S(2)}) collective-permute-start(bf16[352,1024]{1,0:T(8,128)(2,1)} %bitcast_select_fusion.6), channel_id=1, source_target_pairs={{0,16},{1,17},{2,18},{3,19},{4,20},{5,21},{6,22},{7,23},{8,24},{9,... | collective-permute-start | bytes 2162696 | tf_op jit(solution)/shard_map/ppermute | solution.py:470
  100.1 49.3 %collective-permute-start.12 = (bf16[352,1024]{1,0:T(8,128)(2,1)}, bf16[352,1024]{1,0:T(8,128)(2,1)}, u32[]{:S(2)}, u32[]{:S(2)}) collective-permute-start(bf16[352,1024]{1,0:T(8,128)(2,1)} %bitcast_select_fusion.6), channel_id=1, source_target_pairs={{0,17},{1,16},{2,19},{3,18},{4,21},{5,20},{6,23},{7,22},{8,25},{9,... | collective-permute-start | bytes 2162696 | tf_op jit(solution)/shard_map/ppermute | solution.py:470
  153.4 20.5 %collective-permute-start.13 = (bf16[1408,1024]{1,0:T(8,128)(2,1)}, bf16[1408,1024]{1,0:T(8,128)(2,1)}, u32[]{:S(2)}, u32[]{:S(2)}) collective-permute-start(bf16[1408,1024]{1,0:T(8,128)(2,1)} %bitcast_select_fusion.1), channel_id=1, source_target_pairs={{0,8},{1,9},{2,10},{3,11},{4,12},{5,13},{6,14},{7,15},{8,0},{9,1},... | collective-permute-start | bytes 8650760 | tf_op jit(solution)/shard_map/ppermute | solution.py:470
  246.5 20.5 %collective-permute-start.14 = (bf16[1,512,2816]{2,1,0:T(8,128)(2,1)}, bf16[1,512,2816]{2,1,0:T(8,128)(2,1)S(1)}, u32[]{:S(2)}, u32[]{:S(2)}) collective-permute-start(bf16[1,512,2816]{2,1,0:T(8,128)(2,1)} %bitcast.321), channel_id=1, source_target_pairs={{0,8},{1,9},{2,10},{3,11},{4,12},{5,13},{6,14},{7,15},{8,0},{9,1},... | collective-permute-start | bytes 8650760 | tf_op jit(solution)/shard_map/ppermute | solution.py:470
  246.5 20.5 %collective-permute-start.15 = (bf16[1,512,2816]{2,1,0:T(8,128)(2,1)}, bf16[1,512,2816]{2,1,0:T(8,128)(2,1)S(1)}, u32[]{:S(2)}, u32[]{:S(2)}) collective-permute-start(bf16[1,512,2816]{2,1,0:T(8,128)(2,1)} %bitcast.320), channel_id=1, source_target_pairs={{0,8},{1,9},{2,10},{3,11},{4,12},{5,13},{6,14},{7,15},{8,0},{9,1},... | collective-permute-start | bytes 8650760 | tf_op jit(solution)/shard_map/ppermute | solution.py:470
  247.0 20.0 %collective-permute-start.16 = (bf16[1,1408,1024]{2,1,0:T(8,128)(2,1)}, bf16[1,1408,1024]{2,1,0:T(8,128)(2,1)S(1)}, u32[]{:S(2)}, u32[]{:S(2)}) collective-permute-start(bf16[1,1408,1024]{2,1,0:T(8,128)(2,1)} %bitcast.60), channel_id=1, source_target_pairs={{0,8},{1,9},{2,10},{3,11},{4,12},{5,13},{6,14},{7,15},{8,0},{9,1},... | collective-permute-start | bytes 8650760 | tf_op jit(solution)/shard_map/ppermute | solution.py:470
  276.5 33.7 %collective-permute-start.17 = (bf16[1,256,2816]{2,1,0:T(8,128)(2,1)}, bf16[1,256,2816]{2,1,0:T(8,128)(2,1)}, u32[]{:S(2)}, u32[]{:S(2)}) collective-permute-start(bf16[1,256,2816]{2,1,0:T(8,128)(2,1)} %bitcast.63), channel_id=1, source_target_pairs={{0,1},{1,0},{2,3},{3,2},{4,5},{5,4},{6,7},{7,6},{8,9},{9,8},{10,11... | collective-permute-start | bytes 4325384 | tf_op jit(solution)/shard_map/ppermute | solution.py:470
  278.0 33.0 %collective-permute-start.18 = (bf16[1,256,2816]{2,1,0:T(8,128)(2,1)}, bf16[1,256,2816]{2,1,0:T(8,128)(2,1)}, u32[]{:S(2)}, u32[]{:S(2)}) collective-permute-start(bf16[1,256,2816]{2,1,0:T(8,128)(2,1)} %dynamic-slice_bitcast_fusion.1), channel_id=1, source_target_pairs={{0,16},{1,17},{2,18},{3,19},{4,20},{5,21},{6,22},{7,23},{8,24},{9,... | collective-permute-start | bytes 4325384 | tf_op jit(solution)/shard_map/ppermute | solution.py:470
  315.1 21.9 %collective-permute-start.21 = (bf16[5,512,512]{2,1,0:T(8,128)(2,1)S(1)}, bf16[5,512,512]{2,1,0:T(8,128)(2,1)S(1)}, u32[]{:S(2)}, u32[]{:S(2)}) collective-permute-start(bf16[5,512,512]{2,1,0:T(8,128)(2,1)S(1)} %copy-done.62), channel_id=1, source_target_pairs={{0,8},{1,9},{2,10},{3,11},{4,12},{5,13},{6,14},{7,15},{8,0},{9,1},... | collective-permute-start | bytes 7864328 | tf_op jit(solution)/shard_map/ppermute | solution.py:470
  341.8 31.6 %collective-permute-start.22 = (bf16[1,704,1024]{2,1,0:T(8,128)(2,1)}, bf16[1,704,1024]{2,1,0:T(8,128)(2,1)}, u32[]{:S(2)}, u32[]{:S(2)}) collective-permute-start(bf16[1,704,1024]{2,1,0:T(8,128)(2,1)} %dynamic-slice_bitcast_fusion), channel_id=1, source_target_pairs={{0,16},{1,17},{2,18},{3,19},{4,20},{5,21},{6,22},{7,23},{8,24},{9,... | collective-permute-start | bytes 4325384 | tf_op jit(solution)/shard_map/ppermute | solution.py:470
  343.0 28.3 %collective-permute-start.23 = (bf16[5,256,512]{2,1,0:T(8,128)(2,1)}, bf16[5,256,512]{2,1,0:T(8,128)(2,1)}, u32[]{:S(2)}, u32[]{:S(2)}) collective-permute-start(bf16[5,256,512]{2,1,0:T(8,128)(2,1)} %bitcast.77), channel_id=1, source_target_pairs={{0,1},{1,0},{2,3},{3,2},{4,5},{5,4},{6,7},{7,6},{8,9},{9,8},{10,11... | collective-permute-start | bytes 3932168 | tf_op jit(solution)/shard_map/ppermute | solution.py:470
  343.6 22.8 %collective-permute-start.24 = (bf16[1,64,2816]{2,1,0:T(8,128)(2,1)}, bf16[1,64,2816]{2,1,0:T(8,128)(2,1)}, u32[]{:S(2)}, u32[]{:S(2)}) collective-permute-start(bf16[1,64,2816]{2,1,0:T(8,128)(2,1)} %bitcast.80), channel_id=1, source_target_pairs={{0,2},{1,3},{2,0},{3,1},{4,6},{5,7},{6,4},{7,5},{8,10},{9,11},{10,... | collective-permute-start | bytes 1081352 | tf_op jit(solution)/shard_map/ppermute | solution.py:470
  345.2 21.2 %collective-permute-start.25 = (bf16[1,64,2816]{2,1,0:T(8,128)(2,1)}, bf16[1,64,2816]{2,1,0:T(8,128)(2,1)}, u32[]{:S(2)}, u32[]{:S(2)}) collective-permute-start(bf16[1,64,2816]{2,1,0:T(8,128)(2,1)} %bitcast.83), channel_id=1, source_target_pairs={{0,2},{1,3},{2,0},{3,1},{4,6},{5,7},{6,4},{7,5},{8,10},{9,11},{10,... | collective-permute-start | bytes 1081352 | tf_op jit(solution)/shard_map/ppermute | solution.py:470
  383.0 20.8 %collective-permute-start.26 = (bf16[3,512,512]{2,1,0:T(8,128)(2,1)}, bf16[3,512,512]{2,1,0:T(8,128)(2,1)S(1)}, u32[]{:S(2)}, u32[]{:S(2)}) collective-permute-start(bf16[3,512,512]{2,1,0:T(8,128)(2,1)} %get-tuple-element.229), channel_id=1, source_target_pairs={{0,8},{1,9},{2,10},{3,11},{4,12},{5,13},{6,14},{7,15},{8,0},{9,1},... | collective-permute-start | bytes 4718600 | tf_op jit(solution)/shard_map/ppermute | solution.py:470
  383.1 20.8 %collective-permute-start.27 = (bf16[1,352,1024]{2,1,0:T(8,128)(2,1)}, bf16[1,352,1024]{2,1,0:T(8,128)(2,1)}, u32[]{:S(2)}, u32[]{:S(2)}) collective-permute-start(bf16[1,352,1024]{2,1,0:T(8,128)(2,1)} %bitcast.86), channel_id=1, source_target_pairs={{0,1},{1,0},{2,3},{3,2},{4,5},{5,4},{6,7},{7,6},{8,9},{9,8},{10,11... | collective-permute-start | bytes 2162696 | tf_op jit(solution)/shard_map/ppermute | solution.py:470
  383.9 19.9 %collective-permute-start.28 = (bf16[5,128,512]{2,1,0:T(8,128)(2,1)}, bf16[5,128,512]{2,1,0:T(8,128)(2,1)}, u32[]{:S(2)}, u32[]{:S(2)}) collective-permute-start(bf16[5,128,512]{2,1,0:T(8,128)(2,1)} %dynamic-slice_bitcast_fusion.3), channel_id=1, source_target_pairs={{0,16},{1,17},{2,18},{3,19},{4,20},{5,21},{6,22},{7,23},{8,24},{9,... | collective-permute-start | bytes 1966088 | tf_op jit(solution)/shard_map/ppermute | solution.py:470
  384.8 17.4 %collective-permute-start.29 = (bf16[1,32,2816]{2,1,0:T(8,128)(2,1)}, bf16[1,32,2816]{2,1,0:T(8,128)(2,1)S(1)}, u32[]{:S(2)}, u32[]{:S(2)}) collective-permute-start(bf16[1,32,2816]{2,1,0:T(8,128)(2,1)} %dynamic-slice_bitcast_fusion.6), channel_id=1, source_target_pairs={{0,4},{1,5},{2,6},{3,7},{4,0},{5,1},{6,2},{7,3},{8,12},{9,13},{10,... | collective-permute-start | bytes 540680 | tf_op jit(solution)/shard_map/ppermute | solution.py:470
  386.4 17.5 %collective-permute-start.30 = (bf16[1,32,2816]{2,1,0:T(8,128)(2,1)S(1)}, bf16[1,32,2816]{2,1,0:T(8,128)(2,1)S(1)}, u32[]{:S(2)}, u32[]{:S(2)}) collective-permute-start(bf16[1,32,2816]{2,1,0:T(8,128)(2,1)S(1)} %dynamic-slice_bitcast_fusion.5), channel_id=1, source_target_pairs={{0,4},{1,5},{2,6},{3,7},{4,0},{5,1},{6,2},{7,3},{8,12},{9,13},{10,... | collective-permute-start | bytes 540680 | tf_op jit(solution)/shard_map/ppermute | solution.py:470
  407.7 20.2 %collective-permute-start.31 = (bf16[3,128,512]{2,1,0:T(8,128)(2,1)S(1)}, bf16[3,128,512]{2,1,0:T(8,128)(2,1)S(1)}, u32[]{:S(2)}, u32[]{:S(2)}) collective-permute-start(bf16[3,128,512]{2,1,0:T(8,128)(2,1)S(1)} %bitcast.308), channel_id=1, source_target_pairs={{0,16},{1,17},{2,18},{3,19},{4,20},{5,21},{6,22},{7,23},{8,24},{9,... | collective-permute-start | bytes 1179656 | tf_op jit(solution)/shard_map/ppermute | solution.py:470
  409.0 18.9 %collective-permute-start.32 = (bf16[3,128,512]{2,1,0:T(8,128)(2,1)S(1)}, bf16[3,128,512]{2,1,0:T(8,128)(2,1)S(1)}, u32[]{:S(2)}, u32[]{:S(2)}) collective-permute-start(bf16[3,128,512]{2,1,0:T(8,128)(2,1)S(1)} %bitcast.307), channel_id=1, source_target_pairs={{0,1},{1,0},{2,3},{3,2},{4,5},{5,4},{6,7},{7,6},{8,9},{9,8},{10,11... | collective-permute-start | bytes 1179656 | tf_op jit(solution)/shard_map/ppermute | solution.py:470
  410.1 17.8 %collective-permute-start.33 = (bf16[3,128,512]{2,1,0:T(8,128)(2,1)S(1)}, bf16[3,128,512]{2,1,0:T(8,128)(2,1)S(1)}, u32[]{:S(2)}, u32[]{:S(2)}) collective-permute-start(bf16[3,128,512]{2,1,0:T(8,128)(2,1)S(1)} %bitcast.306), channel_id=1, source_target_pairs={{0,17},{1,16},{2,19},{3,18},{4,21},{5,20},{6,23},{7,22},{8,25},{9,... | collective-permute-start | bytes 1179656 | tf_op jit(solution)/shard_map/ppermute | solution.py:470
  428.6 22.2 %collective-permute-start.39 = (bf16[1,88,1024]{2,1,0:T(8,128)(2,1)S(1)}, bf16[1,88,1024]{2,1,0:T(8,128)(2,1)S(1)}, u32[]{:S(2)}, u32[]{:S(2)}) collective-permute-start(bf16[1,88,1024]{2,1,0:T(8,128)(2,1)S(1)} %dynamic-slice_bitcast_fusion.4), channel_id=1, source_target_pairs={{0,4},{1,5},{2,6},{3,7},{4,0},{5,1},{6,2},{7,3},{8,12},{9,13},{10,... | collective-permute-start | bytes 540680 | tf_op jit(solution)/shard_map/ppermute | solution.py:470
  428.9 21.8 %collective-permute-start.40 = (bf16[5,32,512]{2,1,0:T(8,128)(2,1)S(1)}, bf16[5,32,512]{2,1,0:T(8,128)(2,1)S(1)}, u32[]{:S(2)}, u32[]{:S(2)}) collective-permute-start(bf16[5,32,512]{2,1,0:T(8,128)(2,1)S(1)} %dynamic-slice_bitcast_fusion.7), channel_id=1, source_target_pairs={{0,4},{1,5},{2,6},{3,7},{4,0},{5,1},{6,2},{7,3},{8,12},{9,13},{10,... | collective-permute-start | bytes 491528 | tf_op jit(solution)/shard_map/ppermute | solution.py:470
  431.8 18.9 %collective-permute-start.37 = (bf16[3,32,512]{2,1,0:T(8,128)(2,1)S(1)}, bf16[3,32,512]{2,1,0:T(8,128)(2,1)S(1)}, u32[]{:S(2)}, u32[]{:S(2)}) collective-permute-start(bf16[3,32,512]{2,1,0:T(8,128)(2,1)S(1)} %get-tuple-element.253), channel_id=1, source_target_pairs={{0,4},{1,5},{2,6},{3,7},{4,0},{5,1},{6,2},{7,3},{8,12},{9,13},{10,... | collective-permute-start | bytes 294920 | tf_op jit(solution)/shard_map/ppermute | solution.py:470
  (76 other events, 839.2 us)
Sparse Core Ops, SparseCore 0:
  11.5 82.6 all-gather.2
  97.6 99.2 all-gather.4

commit v6 on v5

--- a/solution.py
+++ b/solution.py
@@ -660,8 +660,12 @@
     )
     scale_one = rms_scale(inputs)
 
-    scale_one = tick(scale_one, [], [out_rows, down_rows])
-    scale_one = tick(scale_one, [out_rows, down_rows], [out_rows])
+    scale_one, cosine, sine, bias = tick(
+        (scale_one, cosine, sine, bias), [], [out_rows, down_rows]
+    )
+    scale_one, cosine, sine, bias = tick(
+        (scale_one, cosine, sine, bias), [out_rows, down_rows], [out_rows]
+    )
     scale_one = tick(scale_one, [out_rows], [])
     gain_first_f = first_set[:, 3 * model_width].astype(jnp.float32)[None, :]
     gain_second_f = first_set[:, 3 * model_width + 1].astype(jnp.float32)[None, :]

time: 468 us -> 465 us (level)
  waiting for transfers between devices: 95.2 us -> 89.2 us
    all_gather x1, waiting for transfers between devices: 27.6 us -> 21.2 us  [shards(): lax.all_gather(jnp.concatenate([*projections, gain_columns], axis=1), AXE...]
    unnamed x130 -> x152, local copies, waits for them, and re-layouts: 17 us -> 18.1 us
  transfers between devices with their start and end apart: 43 -> 43, of which waited for: 15 -> 16; matrix products, arithmetic and copies ran while one was open for 25% -> 25% of each run, Pallas kernels for 20% -> 21%
where the time goes in v6:
time: 465 us; the launch traced here: 459 us
  Pallas kernels  135 us (29%)
  waiting for transfers between devices  89.2 us (19%)
  other arithmetic  68.5 us (15%)
  local copies, waits for them, and re-layouts  60.2 us (13%)
  starting transfers between devices  47.7 us (10%)
  matrix products  43.4 us (9%)
  between operations  15.5 us (3%)
    ppermute x41, waiting for transfers between devices, flip(): return lax.ppermute(value, AXES, pairs)  66 us
    ppermute x41, starting transfers between devices, flip(): return lax.ppermute(value, AXES, pairs)  47.6 us
    pallas_call x2, Pallas kernels, attend_back(): pl.pallas_call(partial(attend_back_kernel, slot_count, head_size), grid=(...  45.4 us
    pallas_call x1, Pallas kernels, feed(): pl.pallas_call(feed_kernel, grid=(steps,), in_specs=[pl.BlockSpec((token_...  40.1 us
    pallas_call x1, Pallas kernels, attend(): pl.pallas_call(partial(attend_kernel, slot_count, head_size), grid=(steps...  35.8 us
    dot_general x4, matrix products, contract_last(): lax.dot_general(left, right, (((1,), (1,)), ((), ())), preferred_element_...  31.5 us
    all_gather x1, waiting for transfers between devices, shards(): lax.all_gather(jnp.concatenate([*projections, gain_columns], axis=1), AXE...  21.2 us
    select_n x14, other arithmetic, settle(): jnp.where(mine, near.reshape(shape), far.reshape(shape))  20.7 us
  transfers between devices with their start and end apart: 43, of which 16 were waited for; matrix products, arithmetic and copies ran while one was open for 25% of the time, Pallas kernels for 21%

profile of v6, /device:TPU:0, one launch (start us, length us, event | category | flops | bytes accessed | tf_op | source)
XLA Modules:
  0.0 459.3 jit_solution(5578816245722470192)
XLA Ops:
  19.4 3.1 collective-permute-start.3
  22.5 2.6 collective-permute-start.4
  26.0 3.5 collective-permute-start.1
  30.8 9.7 %collective-permute-done = bf16[32,1024]{1,0:T(8,128)(2,1)S(1)} collective-permute-done((bf16[32,1024]{1,0:T(8,128)(2,1)S(1)}, bf16[32,1024]{1,0:T(8,128)(2,1)S(1)}, u32[]{:S(2)}, u32[]{:S(2)}) %collective-permute-start) | collective-permute-done | bytes 65568 | tf_op jit(solution)/shard_map/ppermute | solution.py:470
  40.5 3.3 collective-permute-start.2
  43.9 6.5 %collective-permute-done.1 = bf16[32,1024]{1,0:T(8,128)(2,1)S(1)} collective-permute-done((bf16[32,1024]{1,0:T(8,128)(2,1)S(1)}, bf16[32,1024]{1,0:T(8,128)(2,1)S(1)}, u32[]{:S(2)}, u32[]{:S(2)}) %collective-permute-start.1) | collective-permute-done | bytes 65568 | tf_op jit(solution)/shard_map/ppermute | solution.py:470
  63.9 4.2 collective-permute-done.8
  71.6 21.2 %all-gather.3.cloned.1.call-done.wq_ref.wk_ref.wv_ref = bf16[1024,3200]{1,0:T(8,128)(2,1)} async-done(((bf16[32,3200]{1,0:T(8,128)(2,1)}), bf16[1024,3200]{1,0:T(8,128)(2,1)}) %all-gather.3.cloned.1.call-update) | async-done | bytes 6553616 | tf_op jit(solution)/shard_map/all_gather | solution.py:639
  106.2 35.8 %attend.1 = (bf16[1024,1024]{1,0:T(8,128)(2,1)}, bf16[1024,1024]{1,0:T(8,128)(2,1)}, bf16[1024,1024]{1,0:T(8,128)(2,1)}, bf16[1024,1024]{1,0:T(8,128)(2,1)}, f32[2,4,4,512]{3,2,1,0:T(4,128)}) custom-call(bf16[1024,1024]{1,0:T(8,128)(2,1)} %fusion.9.normed_ref, bf16[1024,3200]{1,0:T(8,128)(2,1)} %all-gather.3.cloned.1.call-done.wq_ref.wk_ref.wv_ref, ...), custom_call_target="tpu_custom_call" | custom-call | tf_op jit(solution)/shard_map/attend/pallas_call | solution.py:154
  152.0 4.1 copy.131
  156.1 2.6 bitcast_select_fusion.2
  162.7 2.5 multiply_reduce_fusion.1
  167.8 5.7 %bitcast_select_fusion = bf16[2816,1024]{1,0:T(8,128)(2,1)} fusion(pred[2816]{0:T(1024)(128)(4,1)S(1)} %copy-done.58, bf16[2,704,1024]{2,1,0:T(8,128)(2,1)} %bitcast.52, bf16[2,704,1024]{2,1,0:T(8,128)(2,1)S(1)} %broadcast_select_fusion), kind=kLoop, calls=%fused_computation.13 | loop fusion | flops 2883584 | bytes 11537152 | tf_op jit(solution)/shard_map/jit(_where)/select_n | solution.py:550
  177.7 8.8 %fusion.48.grad_product_ref = f32[1024,2816]{1,0:T(8,128)} fusion(bf16[1024,1024]{1,0:T(8,128)(2,1)S(1)} %copy-done.12, bf16[2816,1024]{1,0:T(8,128)(2,1)S(1)} %copy-done.17), kind=kOutput, calls=%fused_computation.203 | convolution fusion | flops 5905580032 | bytes 19398656 | tf_op jit(solution)/shard_map/dot_general | solution.py:22
  186.5 4.1 copy.135.normed_t_ref
  190.6 2.6 copy.139.rest_0_
  195.2 40.1 %feed.1 = (bf16[1024,2816]{1,0:T(8,128)(2,1)}, bf16[1024,2816]{1,0:T(8,128)(2,1)}, bf16[1024,2816]{1,0:T(8,128)(2,1)}, bf16[512,2816]{1,0:T(8,128)(2,1)}, bf16[5...) custom-call(bf16[1024,1024]{1,0:T(8,128)(2,1)} %copy-done.5, ...), custom_call_target="tpu_custom_call" | custom-call | flops 1 | bytes 1 | tf_op jit(solution)/shard_map/feed/pallas_call | solution.py:389
  235.4 6.5 %constant_dynamic-slice_fusion.21 = (bf16[1,2,1,704,1024]{4,3,2,1,0:T(8,128)(2,1)}, bf16[1,2,1,704,1024]{4,3,2,1,0:T(8,128)(2,1)}) fusion(bf16[1,2,2,704,1024]{4,3,2,1,0:T(8,128)(2,1)} %bitcast.274, s32[]{:T(128)S(6)} %select_n.330, s32[]{:T(128)S(6)} %select_n.325), kind=kLoop, calls=%fused_computation.162 | loop fusion | bytes 11534344 | tf_op jit(solution)/shard_map/jit(dynamic_index_in_dim)/dynamic_slice | solution.py:498
  243.4 9.9 %fusion = f32[1024,1024]{1,0:T(8,128)} fusion(bf16[1024,2816]{1,0:T(8,128)(2,1)} %get-tuple-element.195, bf16[1024,5632]{1,0:T(8,128)(2,1)S(1)} %copy-done), kind=kOutput, calls=%fused_computation.3 | convolution fusion | flops 5905580032 | bytes 15728640 | tf_op jit(solution)/shard_map/dot_general | solution.py:22
  253.3 9.0 %fusion.15 = f32[1024,1024]{1,0:T(8,128)S(1)} fusion(f32[1024,1024]{1,0:T(8,128)} %fusion, bf16[1024,2816]{1,0:T(8,128)(2,1)} %get-tuple-element.194, bf16[1024,5632]{1,0:T(8,128)(2,1)S(1)} %copy-done), kind=kOutput, calls=%fused_computation.41 | convolution fusion | flops 5906628608 | bytes 19922944 | tf_op jit(solution)/shard_map/dot_general | solution.py:22
  273.9 3.0 fusion.47
  277.0 3.8 convolution_convert_fusion.grad_ref
  280.8 24.7 %attend_back.2 = (bf16[3,1024,512]{2,1,0:T(8,128)(2,1)}, f32[1024,1024]{1,0:T(8,128)}, bf16[5,512,512]{2,1,0:T(8,128)(2,1)}, bf16[5,512,512]{2,1,0:T(8,128)(2,1)}) custom-call(bf16[1024,1024]{1,0:T(8,128)(2,1)} %get-tuple-element.212.q_ref, bf16[1024,1024]{1,0:T(8,128)(2,1)} %get-tuple-element.213.k_ref, bf16[1024,1024]{1,0:T(8,128)(2,1)} %get-tuple-element.214.v_ref, ...), custom_call_target="tpu_custom_call" | custom-call | flops 1 | bytes 1 | tf_op jit(solution)/shard_map/attend_back/pallas_call | solution.py:300
  317.7 9.5 %add_convert_fusion.1 = bf16[1024,1024]{1,0:T(8,128)(2,1)} fusion(f32[1024,1024]{1,0:T(8,128)S(1)} %copy-done.2, bf16[1024,2816]{1,0:T(8,128)(2,1)} %get-tuple-element.220, bf16[2816,1024]{1,0:T(8,128)(2,1)S(1)} %bitcast.273), kind=kOutput, calls=%fused_computation.18 | convolution fusion | flops 5907677184 | bytes 17825792 | tf_op jit(solution)/shard_map/dot_general | solution.py:18
  327.2 5.7 %collective-permute-done.19 = bf16[1,128,2816]{2,1,0:T(8,128)(2,1)S(1)} collective-permute-done((bf16[1,128,2816]{2,1,0:T(8,128)(2,1)S(1)}, bf16[1,128,2816]{2,1,0:T(8,128)(2,1)S(1)}, u32[]{:S(2)}, u32[]{:S(2)}) %collective-permute-start.19) | collective-permute-done | bytes 720928 | tf_op jit(solution)/shard_map/ppermute | solution.py:470
  342.0 20.7 %attend_back.3 = (bf16[3,1024,512]{2,1,0:T(8,128)(2,1)}, f32[1024,1024]{1,0:T(8,128)}, bf16[3,512,512]{2,1,0:T(8,128)(2,1)}, bf16[3,512,512]{2,1,0:T(8,128)(2,1)}) custom-call(bf16[1024,1024]{1,0:T(8,128)(2,1)} %get-tuple-element.212.q_ref, bf16[1024,1024]{1,0:T(8,128)(2,1)} %get-tuple-element.213.k_ref, ...), custom_call_target="tpu_custom_call", output_to_operand_aliasing={{1}: (9, {})} | custom-call | flops 1 | bytes 1 | tf_op jit(solution)/shard_map/attend_back/pallas_call | solution.py:300
  362.8 5.3 %collective-permute-done.23 = bf16[5,256,512]{2,1,0:T(8,128)(2,1)} collective-permute-done((bf16[5,256,512]{2,1,0:T(8,128)(2,1)}, bf16[5,256,512]{2,1,0:T(8,128)(2,1)}, u32[]{:S(2)}, u32[]{:S(2)}) %collective-permute-start.23) | collective-permute-done | bytes 1310752 | tf_op jit(solution)/shard_map/ppermute | solution.py:470
  385.4 13.5 %finish.1 = f32[1024,1024]{1,0:T(8,128)} custom-call(bf16[3,1024,512]{2,1,0:T(8,128)(2,1)} %get-tuple-element.232.low_one_ref, bf16[3,1024,512]{2,1,0:T(8,128)(2,1)} %get-tuple-element.246.low_two_ref, bf16[1024,3200]{1,0:T(8,128)(2,1)} %all-gather.3.cloned.1.call-done.wq_ref.wk_ref.wv_ref, ...), custom_call_target="tpu_custom_call" | custom-call | flops 1 | bytes 1 | tf_op jit(solution)/shard_map/finish/pallas_call | solution.py:446
  412.0 12.8 %collective-permute-done.35 = bf16[5,64,512]{2,1,0:T(8,128)(2,1)S(1)} collective-permute-done((bf16[5,64,512]{2,1,0:T(8,128)(2,1)S(1)}, bf16[5,64,512]{2,1,0:T(8,128)(2,1)S(1)}, u32[]{:S(2)}, u32[]{:S(2)}) %collective-permute-start.35) | collective-permute-done | bytes 327712 | tf_op jit(solution)/shard_map/ppermute | solution.py:470
  426.2 2.2 collective-permute-start.40
  433.3 2.4 collective-permute-done.36
  435.7 12.0 %collective-permute-done.37 = bf16[3,32,512]{2,1,0:T(8,128)(2,1)S(1)} collective-permute-done((bf16[3,32,512]{2,1,0:T(8,128)(2,1)S(1)}, bf16[3,32,512]{2,1,0:T(8,128)(2,1)S(1)}, u32[]{:S(2)}, u32[]{:S(2)}) %collective-permute-start.37) | collective-permute-done | bytes 98336 | tf_op jit(solution)/shard_map/ppermute | solution.py:470
  (364 shorter events, 142.6 us)
Async XLA Ops:
  7.2 85.6 %all-gather.3.cloned.1.call-start = ((), (), s32[]{:S(2)}) async-start(), calls=%async_computation | async-start | bytes 6758400 | tf_op jit(solution)/shard_map/all_gather | solution.py:639
  9.6 185.6 %all-gather.5.cloned.1.call-start = ((), (), s32[]{:S(2)}) async-start(), calls=%async_computation.1 | async-start | bytes 11894784 | tf_op jit(solution)/shard_map/all_gather | solution.py:642
  19.4 31.0 %collective-permute-start.3 = (bf16[88,1024]{1,0:T(8,128)(2,1)S(1)}, bf16[88,1024]{1,0:T(8,128)(2,1)S(1)}, u32[]{:S(2)}, u32[]{:S(2)}) collective-permute-start(bf16[88,1024]{1,0:T(8,128)(2,1)S(1)} %copy-done.45), channel_id=1, source_target_pairs={{0,2},{1,3},{2,0},{3,1},{4,6},{5,7},{6,4},{7,5},{8,10},{9,11},{10,... | collective-permute-start | bytes 540680 | tf_op jit(solution)/shard_map/ppermute | solution.py:470
  22.5 27.9 %collective-permute-start.4 = (bf16[88,1024]{1,0:T(8,128)(2,1)S(1)}, bf16[88,1024]{1,0:T(8,128)(2,1)S(1)}, u32[]{:S(2)}, u32[]{:S(2)}) collective-permute-start(bf16[88,1024]{1,0:T(8,128)(2,1)S(1)} %copy-done.45), channel_id=1, source_target_pairs={{0,4},{1,5},{2,6},{3,7},{4,0},{5,1},{6,2},{7,3},{8,12},{9,13},{10,... | collective-permute-start | bytes 540680 | tf_op jit(solution)/shard_map/ppermute | solution.py:470
  25.1 25.9 %collective-permute-start.5 = (bf16[88,1024]{1,0:T(8,128)(2,1)S(1)}, bf16[88,1024]{1,0:T(8,128)(2,1)S(1)}, u32[]{:S(2)}, u32[]{:S(2)}) collective-permute-start(bf16[88,1024]{1,0:T(8,128)(2,1)S(1)} %copy-done.45), channel_id=1, source_target_pairs={{0,6},{1,7},{2,4},{3,5},{4,2},{5,3},{6,0},{7,1},{8,14},{9,15},{10,... | collective-permute-start | bytes 540680 | tf_op jit(solution)/shard_map/ppermute | solution.py:470
  26.0 24.3 %collective-permute-start.1 = (bf16[32,1024]{1,0:T(8,128)(2,1)S(1)}, bf16[32,1024]{1,0:T(8,128)(2,1)S(1)}, u32[]{:S(2)}, u32[]{:S(2)}) collective-permute-start(bf16[32,1024]{1,0:T(8,128)(2,1)S(1)} %copy-done.53), channel_id=1, source_target_pairs={{0,4},{1,5},{2,6},{3,7},{4,0},{5,1},{6,2},{7,3},{8,12},{9,13},{10,... | collective-permute-start | bytes 196616 | tf_op jit(solution)/shard_map/ppermute | solution.py:470
  96.1 45.9 %collective-permute-start.9 = (bf16[512,1024]{1,0:T(8,128)(2,1)}, bf16[512,1024]{1,0:T(8,128)(2,1)}, u32[]{:S(2)}, u32[]{:S(2)}) collective-permute-start(bf16[512,1024]{1,0:T(8,128)(2,1)} %bitcast_select_fusion.5), channel_id=1, source_target_pairs={{0,8},{1,9},{2,10},{3,11},{4,12},{5,13},{6,14},{7,15},{8,0},{9,1},... | collective-permute-start | bytes 3145736 | tf_op jit(solution)/shard_map/ppermute | solution.py:470
  96.4 45.6 %collective-permute-start.10 = (bf16[352,1024]{1,0:T(8,128)(2,1)}, bf16[352,1024]{1,0:T(8,128)(2,1)}, u32[]{:S(2)}, u32[]{:S(2)}) collective-permute-start(bf16[352,1024]{1,0:T(8,128)(2,1)} %bitcast_select_fusion.6), channel_id=1, source_target_pairs={{0,1},{1,0},{2,3},{3,2},{4,5},{5,4},{6,7},{7,6},{8,9},{9,8},{10,11... | collective-permute-start | bytes 2162696 | tf_op jit(solution)/shard_map/ppermute | solution.py:470
  97.9 44.1 %collective-permute-start.11 = (bf16[352,1024]{1,0:T(8,128)(2,1)}, bf16[352,1024]{1,0:T(8,128)(2,1)}, u32[]{:S(2)}, u32[]{:S(2)}) collective-permute-start(bf16[352,1024]{1,0:T(8,128)(2,1)} %bitcast_select_fusion.6), channel_id=1, source_target_pairs={{0,16},{1,17},{2,18},{3,19},{4,20},{5,21},{6,22},{7,23},{8,24},{9,... | collective-permute-start | bytes 2162696 | tf_op jit(solution)/shard_map/ppermute | solution.py:470
  98.4 43.6 %collective-permute-start.12 = (bf16[352,1024]{1,0:T(8,128)(2,1)}, bf16[352,1024]{1,0:T(8,128)(2,1)}, u32[]{:S(2)}, u32[]{:S(2)}) collective-permute-start(bf16[352,1024]{1,0:T(8,128)(2,1)} %bitcast_select_fusion.6), channel_id=1, source_target_pairs={{0,17},{1,16},{2,19},{3,18},{4,21},{5,20},{6,23},{7,22},{8,25},{9,... | collective-permute-start | bytes 2162696 | tf_op jit(solution)/shard_map/ppermute | solution.py:470
  146.1 21.5 %collective-permute-start.13 = (bf16[1408,1024]{1,0:T(8,128)(2,1)}, bf16[1408,1024]{1,0:T(8,128)(2,1)}, u32[]{:S(2)}, u32[]{:S(2)}) collective-permute-start(bf16[1408,1024]{1,0:T(8,128)(2,1)} %bitcast_select_fusion.1), channel_id=1, source_target_pairs={{0,8},{1,9},{2,10},{3,11},{4,12},{5,13},{6,14},{7,15},{8,0},{9,1},... | collective-permute-start | bytes 8650760 | tf_op jit(solution)/shard_map/ppermute | solution.py:470
  241.8 20.5 %collective-permute-start.14 = (bf16[1,512,2816]{2,1,0:T(8,128)(2,1)}, bf16[1,512,2816]{2,1,0:T(8,128)(2,1)S(1)}, u32[]{:S(2)}, u32[]{:S(2)}) collective-permute-start(bf16[1,512,2816]{2,1,0:T(8,128)(2,1)} %bitcast.318), channel_id=1, source_target_pairs={{0,8},{1,9},{2,10},{3,11},{4,12},{5,13},{6,14},{7,15},{8,0},{9,1},... | collective-permute-start | bytes 8650760 | tf_op jit(solution)/shard_map/ppermute | solution.py:470
  242.1 20.3 %collective-permute-start.15 = (bf16[1,512,2816]{2,1,0:T(8,128)(2,1)}, bf16[1,512,2816]{2,1,0:T(8,128)(2,1)S(1)}, u32[]{:S(2)}, u32[]{:S(2)}) collective-permute-start(bf16[1,512,2816]{2,1,0:T(8,128)(2,1)} %bitcast.317), channel_id=1, source_target_pairs={{0,8},{1,9},{2,10},{3,11},{4,12},{5,13},{6,14},{7,15},{8,0},{9,1},... | collective-permute-start | bytes 8650760 | tf_op jit(solution)/shard_map/ppermute | solution.py:470
  242.3 20.0 %collective-permute-start.16 = (bf16[1,1408,1024]{2,1,0:T(8,128)(2,1)}, bf16[1,1408,1024]{2,1,0:T(8,128)(2,1)S(1)}, u32[]{:S(2)}, u32[]{:S(2)}) collective-permute-start(bf16[1,1408,1024]{2,1,0:T(8,128)(2,1)} %bitcast.60), channel_id=1, source_target_pairs={{0,8},{1,9},{2,10},{3,11},{4,12},{5,13},{6,14},{7,15},{8,0},{9,1},... | collective-permute-start | bytes 8650760 | tf_op jit(solution)/shard_map/ppermute | solution.py:470
  271.8 34.1 %collective-permute-start.17 = (bf16[1,256,2816]{2,1,0:T(8,128)(2,1)}, bf16[1,256,2816]{2,1,0:T(8,128)(2,1)}, u32[]{:S(2)}, u32[]{:S(2)}) collective-permute-start(bf16[1,256,2816]{2,1,0:T(8,128)(2,1)} %bitcast.63), channel_id=1, source_target_pairs={{0,1},{1,0},{2,3},{3,2},{4,5},{5,4},{6,7},{7,6},{8,9},{9,8},{10,11... | collective-permute-start | bytes 4325384 | tf_op jit(solution)/shard_map/ppermute | solution.py:470
  273.4 33.8 %collective-permute-start.18 = (bf16[1,256,2816]{2,1,0:T(8,128)(2,1)}, bf16[1,256,2816]{2,1,0:T(8,128)(2,1)}, u32[]{:S(2)}, u32[]{:S(2)}) collective-permute-start(bf16[1,256,2816]{2,1,0:T(8,128)(2,1)} %dynamic-slice_bitcast_fusion.1), channel_id=1, source_target_pairs={{0,16},{1,17},{2,18},{3,19},{4,20},{5,21},{6,22},{7,23},{8,24},{9,... | collective-permute-start | bytes 4325384 | tf_op jit(solution)/shard_map/ppermute | solution.py:470
  311.1 22.0 %collective-permute-start.21 = (bf16[5,512,512]{2,1,0:T(8,128)(2,1)S(1)}, bf16[5,512,512]{2,1,0:T(8,128)(2,1)S(1)}, u32[]{:S(2)}, u32[]{:S(2)}) collective-permute-start(bf16[5,512,512]{2,1,0:T(8,128)(2,1)S(1)} %copy-done.71), channel_id=1, source_target_pairs={{0,8},{1,9},{2,10},{3,11},{4,12},{5,13},{6,14},{7,15},{8,0},{9,1},... | collective-permute-start | bytes 7864328 | tf_op jit(solution)/shard_map/ppermute | solution.py:470
  337.9 31.8 %collective-permute-start.22 = (bf16[1,704,1024]{2,1,0:T(8,128)(2,1)}, bf16[1,704,1024]{2,1,0:T(8,128)(2,1)}, u32[]{:S(2)}, u32[]{:S(2)}) collective-permute-start(bf16[1,704,1024]{2,1,0:T(8,128)(2,1)} %dynamic-slice_bitcast_fusion), channel_id=1, source_target_pairs={{0,16},{1,17},{2,18},{3,19},{4,20},{5,21},{6,22},{7,23},{8,24},{9,... | collective-permute-start | bytes 4325384 | tf_op jit(solution)/shard_map/ppermute | solution.py:470
  339.4 28.7 %collective-permute-start.23 = (bf16[5,256,512]{2,1,0:T(8,128)(2,1)}, bf16[5,256,512]{2,1,0:T(8,128)(2,1)}, u32[]{:S(2)}, u32[]{:S(2)}) collective-permute-start(bf16[5,256,512]{2,1,0:T(8,128)(2,1)} %bitcast.77), channel_id=1, source_target_pairs={{0,1},{1,0},{2,3},{3,2},{4,5},{5,4},{6,7},{7,6},{8,9},{9,8},{10,11... | collective-permute-start | bytes 3932168 | tf_op jit(solution)/shard_map/ppermute | solution.py:470
  340.0 22.8 %collective-permute-start.24 = (bf16[1,64,2816]{2,1,0:T(8,128)(2,1)}, bf16[1,64,2816]{2,1,0:T(8,128)(2,1)}, u32[]{:S(2)}, u32[]{:S(2)}) collective-permute-start(bf16[1,64,2816]{2,1,0:T(8,128)(2,1)} %bitcast.80), channel_id=1, source_target_pairs={{0,2},{1,3},{2,0},{3,1},{4,6},{5,7},{6,4},{7,5},{8,10},{9,11},{10,... | collective-permute-start | bytes 1081352 | tf_op jit(solution)/shard_map/ppermute | solution.py:470
  341.3 21.4 %collective-permute-start.25 = (bf16[1,64,2816]{2,1,0:T(8,128)(2,1)}, bf16[1,64,2816]{2,1,0:T(8,128)(2,1)}, u32[]{:S(2)}, u32[]{:S(2)}) collective-permute-start(bf16[1,64,2816]{2,1,0:T(8,128)(2,1)} %bitcast.83), channel_id=1, source_target_pairs={{0,2},{1,3},{2,0},{3,1},{4,6},{5,7},{6,4},{7,5},{8,10},{9,11},{10,... | collective-permute-start | bytes 1081352 | tf_op jit(solution)/shard_map/ppermute | solution.py:470
  379.4 21.2 %collective-permute-start.26 = (bf16[3,512,512]{2,1,0:T(8,128)(2,1)}, bf16[3,512,512]{2,1,0:T(8,128)(2,1)S(1)}, u32[]{:S(2)}, u32[]{:S(2)}) collective-permute-start(bf16[3,512,512]{2,1,0:T(8,128)(2,1)} %get-tuple-element.247), channel_id=1, source_target_pairs={{0,8},{1,9},{2,10},{3,11},{4,12},{5,13},{6,14},{7,15},{8,0},{9,1},... | collective-permute-start | bytes 4718600 | tf_op jit(solution)/shard_map/ppermute | solution.py:470
  379.4 21.2 %collective-permute-start.27 = (bf16[1,352,1024]{2,1,0:T(8,128)(2,1)}, bf16[1,352,1024]{2,1,0:T(8,128)(2,1)}, u32[]{:S(2)}, u32[]{:S(2)}) collective-permute-start(bf16[1,352,1024]{2,1,0:T(8,128)(2,1)} %bitcast.86), channel_id=1, source_target_pairs={{0,1},{1,0},{2,3},{3,2},{4,5},{5,4},{6,7},{7,6},{8,9},{9,8},{10,11... | collective-permute-start | bytes 2162696 | tf_op jit(solution)/shard_map/ppermute | solution.py:470
  380.8 19.8 %collective-permute-start.28 = (bf16[5,128,512]{2,1,0:T(8,128)(2,1)}, bf16[5,128,512]{2,1,0:T(8,128)(2,1)}, u32[]{:S(2)}, u32[]{:S(2)}) collective-permute-start(bf16[5,128,512]{2,1,0:T(8,128)(2,1)} %dynamic-slice_bitcast_fusion.3), channel_id=1, source_target_pairs={{0,16},{1,17},{2,18},{3,19},{4,20},{5,21},{6,22},{7,23},{8,24},{9,... | collective-permute-start | bytes 1966088 | tf_op jit(solution)/shard_map/ppermute | solution.py:470
  381.4 17.4 %collective-permute-start.29 = (bf16[1,32,2816]{2,1,0:T(8,128)(2,1)}, bf16[1,32,2816]{2,1,0:T(8,128)(2,1)S(1)}, u32[]{:S(2)}, u32[]{:S(2)}) collective-permute-start(bf16[1,32,2816]{2,1,0:T(8,128)(2,1)} %dynamic-slice_bitcast_fusion.6), channel_id=1, source_target_pairs={{0,4},{1,5},{2,6},{3,7},{4,0},{5,1},{6,2},{7,3},{8,12},{9,13},{10,... | collective-permute-start | bytes 540680 | tf_op jit(solution)/shard_map/ppermute | solution.py:470
  383.3 17.2 %collective-permute-start.30 = (bf16[1,32,2816]{2,1,0:T(8,128)(2,1)S(1)}, bf16[1,32,2816]{2,1,0:T(8,128)(2,1)S(1)}, u32[]{:S(2)}, u32[]{:S(2)}) collective-permute-start(bf16[1,32,2816]{2,1,0:T(8,128)(2,1)S(1)} %dynamic-slice_bitcast_fusion.5), channel_id=1, source_target_pairs={{0,4},{1,5},{2,6},{3,7},{4,0},{5,1},{6,2},{7,3},{8,12},{9,13},{10,... | collective-permute-start | bytes 540680 | tf_op jit(solution)/shard_map/ppermute | solution.py:470
  404.4 20.3 %collective-permute-start.31 = (bf16[3,128,512]{2,1,0:T(8,128)(2,1)S(1)}, bf16[3,128,512]{2,1,0:T(8,128)(2,1)S(1)}, u32[]{:S(2)}, u32[]{:S(2)}) collective-permute-start(bf16[3,128,512]{2,1,0:T(8,128)(2,1)S(1)} %bitcast.308), channel_id=1, source_target_pairs={{0,16},{1,17},{2,18},{3,19},{4,20},{5,21},{6,22},{7,23},{8,24},{9,... | collective-permute-start | bytes 1179656 | tf_op jit(solution)/shard_map/ppermute | solution.py:470
  405.9 18.9 %collective-permute-start.32 = (bf16[3,128,512]{2,1,0:T(8,128)(2,1)S(1)}, bf16[3,128,512]{2,1,0:T(8,128)(2,1)S(1)}, u32[]{:S(2)}, u32[]{:S(2)}) collective-permute-start(bf16[3,128,512]{2,1,0:T(8,128)(2,1)S(1)} %bitcast.307), channel_id=1, source_target_pairs={{0,1},{1,0},{2,3},{3,2},{4,5},{5,4},{6,7},{7,6},{8,9},{9,8},{10,11... | collective-permute-start | bytes 1179656 | tf_op jit(solution)/shard_map/ppermute | solution.py:470
  406.5 18.3 %collective-permute-start.33 = (bf16[3,128,512]{2,1,0:T(8,128)(2,1)S(1)}, bf16[3,128,512]{2,1,0:T(8,128)(2,1)S(1)}, u32[]{:S(2)}, u32[]{:S(2)}) collective-permute-start(bf16[3,128,512]{2,1,0:T(8,128)(2,1)S(1)} %bitcast.306), channel_id=1, source_target_pairs={{0,17},{1,16},{2,19},{3,18},{4,21},{5,20},{6,23},{7,22},{8,25},{9,... | collective-permute-start | bytes 1179656 | tf_op jit(solution)/shard_map/ppermute | solution.py:470
  425.4 22.3 %collective-permute-start.39 = (bf16[1,88,1024]{2,1,0:T(8,128)(2,1)S(1)}, bf16[1,88,1024]{2,1,0:T(8,128)(2,1)S(1)}, u32[]{:S(2)}, u32[]{:S(2)}) collective-permute-start(bf16[1,88,1024]{2,1,0:T(8,128)(2,1)S(1)} %dynamic-slice_bitcast_fusion.4), channel_id=1, source_target_pairs={{0,4},{1,5},{2,6},{3,7},{4,0},{5,1},{6,2},{7,3},{8,12},{9,13},{10,... | collective-permute-start | bytes 540680 | tf_op jit(solution)/shard_map/ppermute | solution.py:470
  426.2 21.5 %collective-permute-start.40 = (bf16[5,32,512]{2,1,0:T(8,128)(2,1)S(1)}, bf16[5,32,512]{2,1,0:T(8,128)(2,1)S(1)}, u32[]{:S(2)}, u32[]{:S(2)}) collective-permute-start(bf16[5,32,512]{2,1,0:T(8,128)(2,1)S(1)} %dynamic-slice_bitcast_fusion.7), channel_id=1, source_target_pairs={{0,4},{1,5},{2,6},{3,7},{4,0},{5,1},{6,2},{7,3},{8,12},{9,13},{10,... | collective-permute-start | bytes 491528 | tf_op jit(solution)/shard_map/ppermute | solution.py:470
  428.7 19.0 %collective-permute-start.37 = (bf16[3,32,512]{2,1,0:T(8,128)(2,1)S(1)}, bf16[3,32,512]{2,1,0:T(8,128)(2,1)S(1)}, u32[]{:S(2)}, u32[]{:S(2)}) collective-permute-start(bf16[3,32,512]{2,1,0:T(8,128)(2,1)S(1)} %get-tuple-element.271), channel_id=1, source_target_pairs={{0,4},{1,5},{2,6},{3,7},{4,0},{5,1},{6,2},{7,3},{8,12},{9,13},{10,... | collective-permute-start | bytes 294920 | tf_op jit(solution)/shard_map/ppermute | solution.py:470
  (87 other events, 727.9 us)
Sparse Core Ops, SparseCore 0:
  11.5 81.3 all-gather.2
  96.2 98.9 all-gather.4

commit v7 on v6

--- a/solution.py
+++ b/solution.py
@@ -598,6 +598,7 @@
     return {
         "high_first": [core, high, [0]] + singles,
         "low_first": [core, [0], high] + singles,
+        "tail": singles,
         "short": [core, high + [0]] + pairs,
         "gather": pairs[::-1] + [[0] + high, core],
     }
@@ -742,25 +743,27 @@
     one = exchange(None, plans["low_first"], first=parts_one)
     grad_context, product = tick((grad_context, product), [gate, up], [gate, up, one])
     out_tokens = (hidden + forward_dot(product, down_w)).astype(jnp.bfloat16)
-    grad_context, out_tokens = tick(
-        (grad_context, out_tokens), [gate, up, one], [down, one, gate, up]
-    )
+    grad_context, out_tokens = tick((grad_context, out_tokens), [gate, up, one], [])
+    gate_up = exchange(
+        jnp.concatenate([gate.current, up.current]), plans["tail"]
+    )
+    grad_context, out_tokens = tick((grad_context, out_tokens), [], [down, one, gate_up])
     low_two, grad_first, *parts_two = attend_back_half(1, grad_context, first_part, (None, None))
     two = exchange(None, plans["short"], first=parts_two)
-    low_two = tick(low_two, [down, one, gate, up], [two, down, one, gate, up])
+    low_two = tick(low_two, [down, one, gate_up], [two, down, one, gate_up])
     grad_tokens = finish(
         low_one, low_two, first_set, grad_hidden, tokens, scale_one, gain_first_f
     )
-    grad_tokens = tick(grad_tokens, [two, down, one, gate, up], [two, down, one])
-    pending = [two, down, one, gate, up]
+    grad_tokens = tick(grad_tokens, [two, down, one, gate_up], [two, down, one])
+    pending = [two, down, one, gate_up]
     while any(item.steps for item in pending):
         grad_tokens = tick(grad_tokens, pending, pending)
     projection_sums = [
         jnp.concatenate([one.current[index], two.current[index]], axis=1) for index in range(3)
     ]
     grad_out_sum = jnp.concatenate([one.current[3], one.current[4]], axis=1)
-    grad_gate_sum = gate.current[0]
-    grad_up_sum = up.current[0]
+    grad_gate_sum = gate_up.current[0]
+    grad_up_sum = gate_up.current[1]
     grad_down_sum = down.current[0]
 
     def gain_grad(gain, sums, weights):

time: 465 us -> 463 us (level)
    ppermute x41 -> x39, starting transfers between devices: 47.6 us -> 46 us  [flip(): return lax.ppermute(value, AXES, pairs)]
    ppermute x41 -> x39, waiting for transfers between devices: 66 us -> 67.1 us  [flip(): return lax.ppermute(value, AXES, pairs)]
    convert_element_type x18 -> x17, other arithmetic: 17.5 us -> 16.5 us  [settle(): self.current = total.astype(jnp.bfloat16) if self.steps else total]
    dynamic_slice x14 -> x13, local copies, waits for them, and re-layouts: 13.3 us -> 12.9 us  [part(): value = lax.dynamic_index_in_dim(view, chosen, 2, keepdims=False)]
    unnamed x152 -> x140, local copies, waits for them, and re-layouts: 18.1 us -> 18 us
  transfers between devices with their start and end apart: 43 -> 41, of which waited for: 16 -> 16; matrix products, arithmetic and copies ran while one was open for 25% -> 25% of each run, Pallas kernels for 21% -> 21%
where the time goes in v7:
time: 463 us; the launch traced here: 457 us
  Pallas kernels  135 us (29%)
  waiting for transfers between devices  90.4 us (20%)
  other arithmetic  67.7 us (15%)
  local copies, waits for them, and re-layouts  59.1 us (13%)
  starting transfers between devices  46.1 us (10%)
  matrix products  43.6 us (9%)
  between operations  15.4 us (3%)
    ppermute x39, waiting for transfers between devices, flip(): return lax.ppermute(value, AXES, pairs)  67.1 us
    ppermute x39, starting transfers between devices, flip(): return lax.ppermute(value, AXES, pairs)  46 us
    pallas_call x2, Pallas kernels, attend_back(): pl.pallas_call(partial(attend_back_kernel, slot_count, head_size), grid=(...  45.5 us
    pallas_call x1, Pallas kernels, feed(): pl.pallas_call(feed_kernel, grid=(steps,), in_specs=[pl.BlockSpec((token_...  40.1 us
    pallas_call x1, Pallas kernels, attend(): pl.pallas_call(partial(attend_kernel, slot_count, head_size), grid=(steps...  35.8 us
    dot_general x4, matrix products, contract_last(): lax.dot_general(left, right, (((1,), (1,)), ((), ())), preferred_element_...  31.5 us
    all_gather x1, waiting for transfers between devices, shards(): lax.all_gather(jnp.concatenate([*projections, gain_columns], axis=1), AXE...  21.2 us
    select_n x14, other arithmetic, settle(): jnp.where(mine, near.reshape(shape), far.reshape(shape))  20.7 us
  transfers between devices with their start and end apart: 41, of which 16 were waited for; matrix products, arithmetic and copies ran while one was open for 25% of the time, Pallas kernels for 21%

profile of v7, /device:TPU:0, one launch (start us, length us, event | category | flops | bytes accessed | tf_op | source)
XLA Modules:
  0.0 457.1 jit_solution(2405131838612771810)
XLA Ops:
  19.4 3.1 collective-permute-start.3
  22.5 2.6 collective-permute-start.4
  26.0 3.5 collective-permute-start.1
  30.8 9.7 %collective-permute-done = bf16[32,1024]{1,0:T(8,128)(2,1)S(1)} collective-permute-done((bf16[32,1024]{1,0:T(8,128)(2,1)S(1)}, bf16[32,1024]{1,0:T(8,128)(2,1)S(1)}, u32[]{:S(2)}, u32[]{:S(2)}) %collective-permute-start) | collective-permute-done | bytes 65568 | tf_op jit(solution)/shard_map/ppermute | solution.py:470
  40.5 3.3 collective-permute-start.2
  43.9 6.5 %collective-permute-done.1 = bf16[32,1024]{1,0:T(8,128)(2,1)S(1)} collective-permute-done((bf16[32,1024]{1,0:T(8,128)(2,1)S(1)}, bf16[32,1024]{1,0:T(8,128)(2,1)S(1)}, u32[]{:S(2)}, u32[]{:S(2)}) %collective-permute-start.1) | collective-permute-done | bytes 65568 | tf_op jit(solution)/shard_map/ppermute | solution.py:470
  63.9 4.2 collective-permute-done.8
  71.6 21.2 %all-gather.3.cloned.1.call-done.wq_ref.wk_ref.wv_ref = bf16[1024,3200]{1,0:T(8,128)(2,1)} async-done(((bf16[32,3200]{1,0:T(8,128)(2,1)}), bf16[1024,3200]{1,0:T(8,128)(2,1)}) %all-gather.3.cloned.1.call-update) | async-done | bytes 6553616 | tf_op jit(solution)/shard_map/all_gather | solution.py:640
  106.1 35.8 %attend.1 = (bf16[1024,1024]{1,0:T(8,128)(2,1)}, bf16[1024,1024]{1,0:T(8,128)(2,1)}, bf16[1024,1024]{1,0:T(8,128)(2,1)}, bf16[1024,1024]{1,0:T(8,128)(2,1)}, f32[2,4,4,512]{3,2,1,0:T(4,128)}) custom-call(bf16[1024,1024]{1,0:T(8,128)(2,1)} %fusion.9.normed_ref, bf16[1024,3200]{1,0:T(8,128)(2,1)} %all-gather.3.cloned.1.call-done.wq_ref.wk_ref.wv_ref, ...), custom_call_target="tpu_custom_call" | custom-call | tf_op jit(solution)/shard_map/attend/pallas_call | solution.py:154
  151.8 4.1 copy.129
  156.0 2.6 bitcast_select_fusion.2
  162.5 2.5 multiply_reduce_fusion.1
  167.7 5.7 %bitcast_select_fusion = bf16[2816,1024]{1,0:T(8,128)(2,1)} fusion(pred[2816]{0:T(1024)(128)(4,1)S(1)} %copy-done.52, bf16[2,704,1024]{2,1,0:T(8,128)(2,1)} %bitcast.52, bf16[2,704,1024]{2,1,0:T(8,128)(2,1)S(1)} %broadcast_select_fusion), kind=kLoop, calls=%fused_computation.13 | loop fusion | flops 2883584 | bytes 11537152 | tf_op jit(solution)/shard_map/jit(_where)/select_n | solution.py:550
  177.6 8.8 %fusion.43.grad_product_ref = f32[1024,2816]{1,0:T(8,128)} fusion(bf16[1024,1024]{1,0:T(8,128)(2,1)S(1)} %copy-done.12, bf16[2816,1024]{1,0:T(8,128)(2,1)S(1)} %copy-done.17), kind=kOutput, calls=%fused_computation.198 | convolution fusion | flops 5905580032 | bytes 19398656 | tf_op jit(solution)/shard_map/dot_general | solution.py:22
  186.4 4.1 copy.133.normed_t_ref
  190.5 2.7 copy.137.rest_0_
  195.1 40.1 %feed.1 = (bf16[1024,2816]{1,0:T(8,128)(2,1)}, bf16[1024,2816]{1,0:T(8,128)(2,1)}, bf16[1024,2816]{1,0:T(8,128)(2,1)}, bf16[512,2816]{1,0:T(8,128)(2,1)}, bf16[5...) custom-call(bf16[1024,1024]{1,0:T(8,128)(2,1)} %copy-done.5, ...), custom_call_target="tpu_custom_call" | custom-call | flops 1 | bytes 1 | tf_op jit(solution)/shard_map/feed/pallas_call | solution.py:389
  235.3 6.5 %constant_dynamic-slice_fusion.19 = (bf16[1,2,1,704,1024]{4,3,2,1,0:T(8,128)(2,1)}, bf16[1,2,1,704,1024]{4,3,2,1,0:T(8,128)(2,1)}) fusion(bf16[1,2,2,704,1024]{4,3,2,1,0:T(8,128)(2,1)} %bitcast.261, s32[]{:T(128)S(6)} %select_n.326, s32[]{:T(128)S(6)} %select_n.321), kind=kLoop, calls=%fused_computation.157 | loop fusion | bytes 11534344 | tf_op jit(solution)/shard_map/jit(dynamic_index_in_dim)/dynamic_slice | solution.py:498
  243.3 9.9 %fusion = f32[1024,1024]{1,0:T(8,128)} fusion(bf16[1024,2816]{1,0:T(8,128)(2,1)} %get-tuple-element.191, bf16[1024,5632]{1,0:T(8,128)(2,1)S(1)} %copy-done), kind=kOutput, calls=%fused_computation.3 | convolution fusion | flops 5905580032 | bytes 15728640 | tf_op jit(solution)/shard_map/dot_general | solution.py:22
  253.2 9.0 %fusion.15 = f32[1024,1024]{1,0:T(8,128)S(1)} fusion(f32[1024,1024]{1,0:T(8,128)} %fusion, bf16[1024,2816]{1,0:T(8,128)(2,1)} %get-tuple-element.190, bf16[1024,5632]{1,0:T(8,128)(2,1)S(1)} %copy-done), kind=kOutput, calls=%fused_computation.41 | convolution fusion | flops 5906628608 | bytes 19922944 | tf_op jit(solution)/shard_map/dot_general | solution.py:22
  273.9 3.0 fusion.42
  276.9 3.8 convolution_convert_fusion.grad_ref
  280.7 24.7 %attend_back.2 = (bf16[3,1024,512]{2,1,0:T(8,128)(2,1)}, f32[1024,1024]{1,0:T(8,128)}, bf16[5,512,512]{2,1,0:T(8,128)(2,1)}, bf16[5,512,512]{2,1,0:T(8,128)(2,1)}) custom-call(bf16[1024,1024]{1,0:T(8,128)(2,1)} %get-tuple-element.208.q_ref, bf16[1024,1024]{1,0:T(8,128)(2,1)} %get-tuple-element.209.k_ref, bf16[1024,1024]{1,0:T(8,128)(2,1)} %get-tuple-element.210.v_ref, ...), custom_call_target="tpu_custom_call" | custom-call | flops 1 | bytes 1 | tf_op jit(solution)/shard_map/attend_back/pallas_call | solution.py:300
  317.7 9.6 %add_convert_fusion.1 = bf16[1024,1024]{1,0:T(8,128)(2,1)} fusion(f32[1024,1024]{1,0:T(8,128)S(1)} %copy-done.2, bf16[1024,2816]{1,0:T(8,128)(2,1)} %get-tuple-element.216, bf16[2816,1024]{1,0:T(8,128)(2,1)S(1)} %bitcast.260), kind=kOutput, calls=%fused_computation.18 | convolution fusion | flops 5907677184 | bytes 17825792 | tf_op jit(solution)/shard_map/dot_general | solution.py:18
  327.3 5.5 %collective-permute-done.19 = bf16[1,128,2816]{2,1,0:T(8,128)(2,1)S(1)} collective-permute-done((bf16[1,128,2816]{2,1,0:T(8,128)(2,1)S(1)}, bf16[1,128,2816]{2,1,0:T(8,128)(2,1)S(1)}, u32[]{:S(2)}, u32[]{:S(2)}) %collective-permute-start.19) | collective-permute-done | bytes 720928 | tf_op jit(solution)/shard_map/ppermute | solution.py:470
  340.9 20.8 %attend_back.3 = (bf16[3,1024,512]{2,1,0:T(8,128)(2,1)}, f32[1024,1024]{1,0:T(8,128)}, bf16[3,512,512]{2,1,0:T(8,128)(2,1)}, bf16[3,512,512]{2,1,0:T(8,128)(2,1)}) custom-call(bf16[1024,1024]{1,0:T(8,128)(2,1)} %get-tuple-element.208.q_ref, bf16[1024,1024]{1,0:T(8,128)(2,1)} %get-tuple-element.209.k_ref, ...), custom_call_target="tpu_custom_call", output_to_operand_aliasing={{1}: (9, {})} | custom-call | flops 1 | bytes 1 | tf_op jit(solution)/shard_map/attend_back/pallas_call | solution.py:300
  361.7 6.0 %collective-permute-done.23 = bf16[5,256,512]{2,1,0:T(8,128)(2,1)} collective-permute-done((bf16[5,256,512]{2,1,0:T(8,128)(2,1)}, bf16[5,256,512]{2,1,0:T(8,128)(2,1)}, u32[]{:S(2)}, u32[]{:S(2)}) %collective-permute-start.23) | collective-permute-done | bytes 1310752 | tf_op jit(solution)/shard_map/ppermute | solution.py:470
  382.5 13.5 %finish.1 = f32[1024,1024]{1,0:T(8,128)} custom-call(bf16[3,1024,512]{2,1,0:T(8,128)(2,1)} %get-tuple-element.228.low_one_ref, bf16[3,1024,512]{2,1,0:T(8,128)(2,1)} %get-tuple-element.240.low_two_ref, bf16[1024,3200]{1,0:T(8,128)(2,1)} %all-gather.3.cloned.1.call-done.wq_ref.wk_ref.wv_ref, ...), custom_call_target="tpu_custom_call" | custom-call | flops 1 | bytes 1 | tf_op jit(solution)/shard_map/finish/pallas_call | solution.py:446
  395.9 2.5 collective-permute-done.28
  410.0 12.6 %collective-permute-done.33 = bf16[5,64,512]{2,1,0:T(8,128)(2,1)S(1)} collective-permute-done((bf16[5,64,512]{2,1,0:T(8,128)(2,1)S(1)}, bf16[5,64,512]{2,1,0:T(8,128)(2,1)S(1)}, u32[]{:S(2)}, u32[]{:S(2)}) %collective-permute-start.33) | collective-permute-done | bytes 327712 | tf_op jit(solution)/shard_map/ppermute | solution.py:470
  431.2 2.6 collective-permute-done.34
  433.8 11.8 %collective-permute-done.35 = bf16[3,32,512]{2,1,0:T(8,128)(2,1)S(1)} collective-permute-done((bf16[3,32,512]{2,1,0:T(8,128)(2,1)S(1)}, bf16[3,32,512]{2,1,0:T(8,128)(2,1)S(1)}, u32[]{:S(2)}, u32[]{:S(2)}) %collective-permute-start.35) | collective-permute-done | bytes 98336 | tf_op jit(solution)/shard_map/ppermute | solution.py:470
  (346 shorter events, 139.6 us)
Async XLA Ops:
  7.2 85.6 %all-gather.3.cloned.1.call-start = ((), (), s32[]{:S(2)}) async-start(), calls=%async_computation | async-start | bytes 6758400 | tf_op jit(solution)/shard_map/all_gather | solution.py:640
  9.6 185.5 %all-gather.5.cloned.1.call-start = ((), (), s32[]{:S(2)}) async-start(), calls=%async_computation.1 | async-start | bytes 11894784 | tf_op jit(solution)/shard_map/all_gather | solution.py:643
  19.4 31.0 %collective-permute-start.3 = (bf16[88,1024]{1,0:T(8,128)(2,1)S(1)}, bf16[88,1024]{1,0:T(8,128)(2,1)S(1)}, u32[]{:S(2)}, u32[]{:S(2)}) collective-permute-start(bf16[88,1024]{1,0:T(8,128)(2,1)S(1)} %copy-done.43), channel_id=1, source_target_pairs={{0,2},{1,3},{2,0},{3,1},{4,6},{5,7},{6,4},{7,5},{8,10},{9,11},{10,... | collective-permute-start | bytes 540680 | tf_op jit(solution)/shard_map/ppermute | solution.py:470
  22.5 27.9 %collective-permute-start.4 = (bf16[88,1024]{1,0:T(8,128)(2,1)S(1)}, bf16[88,1024]{1,0:T(8,128)(2,1)S(1)}, u32[]{:S(2)}, u32[]{:S(2)}) collective-permute-start(bf16[88,1024]{1,0:T(8,128)(2,1)S(1)} %copy-done.43), channel_id=1, source_target_pairs={{0,4},{1,5},{2,6},{3,7},{4,0},{5,1},{6,2},{7,3},{8,12},{9,13},{10,... | collective-permute-start | bytes 540680 | tf_op jit(solution)/shard_map/ppermute | solution.py:470
  25.1 25.9 %collective-permute-start.5 = (bf16[88,1024]{1,0:T(8,128)(2,1)S(1)}, bf16[88,1024]{1,0:T(8,128)(2,1)S(1)}, u32[]{:S(2)}, u32[]{:S(2)}) collective-permute-start(bf16[88,1024]{1,0:T(8,128)(2,1)S(1)} %copy-done.43), channel_id=1, source_target_pairs={{0,6},{1,7},{2,4},{3,5},{4,2},{5,3},{6,0},{7,1},{8,14},{9,15},{10,... | collective-permute-start | bytes 540680 | tf_op jit(solution)/shard_map/ppermute | solution.py:470
  26.0 24.3 %collective-permute-start.1 = (bf16[32,1024]{1,0:T(8,128)(2,1)S(1)}, bf16[32,1024]{1,0:T(8,128)(2,1)S(1)}, u32[]{:S(2)}, u32[]{:S(2)}) collective-permute-start(bf16[32,1024]{1,0:T(8,128)(2,1)S(1)} %copy-done.47), channel_id=1, source_target_pairs={{0,4},{1,5},{2,6},{3,7},{4,0},{5,1},{6,2},{7,3},{8,12},{9,13},{10,... | collective-permute-start | bytes 196616 | tf_op jit(solution)/shard_map/ppermute | solution.py:470
  96.0 45.8 %collective-permute-start.9 = (bf16[512,1024]{1,0:T(8,128)(2,1)}, bf16[512,1024]{1,0:T(8,128)(2,1)}, u32[]{:S(2)}, u32[]{:S(2)}) collective-permute-start(bf16[512,1024]{1,0:T(8,128)(2,1)} %bitcast_select_fusion.5), channel_id=1, source_target_pairs={{0,8},{1,9},{2,10},{3,11},{4,12},{5,13},{6,14},{7,15},{8,0},{9,1},... | collective-permute-start | bytes 3145736 | tf_op jit(solution)/shard_map/ppermute | solution.py:470
  96.3 45.6 %collective-permute-start.10 = (bf16[352,1024]{1,0:T(8,128)(2,1)}, bf16[352,1024]{1,0:T(8,128)(2,1)}, u32[]{:S(2)}, u32[]{:S(2)}) collective-permute-start(bf16[352,1024]{1,0:T(8,128)(2,1)} %bitcast_select_fusion.6), channel_id=1, source_target_pairs={{0,1},{1,0},{2,3},{3,2},{4,5},{5,4},{6,7},{7,6},{8,9},{9,8},{10,11... | collective-permute-start | bytes 2162696 | tf_op jit(solution)/shard_map/ppermute | solution.py:470
  97.8 44.1 %collective-permute-start.11 = (bf16[352,1024]{1,0:T(8,128)(2,1)}, bf16[352,1024]{1,0:T(8,128)(2,1)}, u32[]{:S(2)}, u32[]{:S(2)}) collective-permute-start(bf16[352,1024]{1,0:T(8,128)(2,1)} %bitcast_select_fusion.6), channel_id=1, source_target_pairs={{0,16},{1,17},{2,18},{3,19},{4,20},{5,21},{6,22},{7,23},{8,24},{9,... | collective-permute-start | bytes 2162696 | tf_op jit(solution)/shard_map/ppermute | solution.py:470
  98.3 43.6 %collective-permute-start.12 = (bf16[352,1024]{1,0:T(8,128)(2,1)}, bf16[352,1024]{1,0:T(8,128)(2,1)}, u32[]{:S(2)}, u32[]{:S(2)}) collective-permute-start(bf16[352,1024]{1,0:T(8,128)(2,1)} %bitcast_select_fusion.6), channel_id=1, source_target_pairs={{0,17},{1,16},{2,19},{3,18},{4,21},{5,20},{6,23},{7,22},{8,25},{9,... | collective-permute-start | bytes 2162696 | tf_op jit(solution)/shard_map/ppermute | solution.py:470
  146.0 21.4 %collective-permute-start.13 = (bf16[1408,1024]{1,0:T(8,128)(2,1)}, bf16[1408,1024]{1,0:T(8,128)(2,1)}, u32[]{:S(2)}, u32[]{:S(2)}) collective-permute-start(bf16[1408,1024]{1,0:T(8,128)(2,1)} %bitcast_select_fusion.1), channel_id=1, source_target_pairs={{0,8},{1,9},{2,10},{3,11},{4,12},{5,13},{6,14},{7,15},{8,0},{9,1},... | collective-permute-start | bytes 8650760 | tf_op jit(solution)/shard_map/ppermute | solution.py:470
  241.7 20.5 %collective-permute-start.14 = (bf16[1,512,2816]{2,1,0:T(8,128)(2,1)}, bf16[1,512,2816]{2,1,0:T(8,128)(2,1)S(1)}, u32[]{:S(2)}, u32[]{:S(2)}) collective-permute-start(bf16[1,512,2816]{2,1,0:T(8,128)(2,1)} %bitcast.302), channel_id=1, source_target_pairs={{0,8},{1,9},{2,10},{3,11},{4,12},{5,13},{6,14},{7,15},{8,0},{9,1},... | collective-permute-start | bytes 8650760 | tf_op jit(solution)/shard_map/ppermute | solution.py:470
  242.0 20.2 %collective-permute-start.15 = (bf16[1,512,2816]{2,1,0:T(8,128)(2,1)}, bf16[1,512,2816]{2,1,0:T(8,128)(2,1)S(1)}, u32[]{:S(2)}, u32[]{:S(2)}) collective-permute-start(bf16[1,512,2816]{2,1,0:T(8,128)(2,1)} %bitcast.301), channel_id=1, source_target_pairs={{0,8},{1,9},{2,10},{3,11},{4,12},{5,13},{6,14},{7,15},{8,0},{9,1},... | collective-permute-start | bytes 8650760 | tf_op jit(solution)/shard_map/ppermute | solution.py:470
  242.2 20.0 %collective-permute-start.16 = (bf16[1,1408,1024]{2,1,0:T(8,128)(2,1)}, bf16[1,1408,1024]{2,1,0:T(8,128)(2,1)S(1)}, u32[]{:S(2)}, u32[]{:S(2)}) collective-permute-start(bf16[1,1408,1024]{2,1,0:T(8,128)(2,1)} %bitcast.60), channel_id=1, source_target_pairs={{0,8},{1,9},{2,10},{3,11},{4,12},{5,13},{6,14},{7,15},{8,0},{9,1},... | collective-permute-start | bytes 8650760 | tf_op jit(solution)/shard_map/ppermute | solution.py:470
  271.7 34.1 %collective-permute-start.17 = (bf16[1,256,2816]{2,1,0:T(8,128)(2,1)}, bf16[1,256,2816]{2,1,0:T(8,128)(2,1)}, u32[]{:S(2)}, u32[]{:S(2)}) collective-permute-start(bf16[1,256,2816]{2,1,0:T(8,128)(2,1)} %bitcast.63), channel_id=1, source_target_pairs={{0,1},{1,0},{2,3},{3,2},{4,5},{5,4},{6,7},{7,6},{8,9},{9,8},{10,11... | collective-permute-start | bytes 4325384 | tf_op jit(solution)/shard_map/ppermute | solution.py:470
  273.3 33.8 %collective-permute-start.18 = (bf16[1,256,2816]{2,1,0:T(8,128)(2,1)}, bf16[1,256,2816]{2,1,0:T(8,128)(2,1)}, u32[]{:S(2)}, u32[]{:S(2)}) collective-permute-start(bf16[1,256,2816]{2,1,0:T(8,128)(2,1)} %dynamic-slice_bitcast_fusion.1), channel_id=1, source_target_pairs={{0,16},{1,17},{2,18},{3,19},{4,20},{5,21},{6,22},{7,23},{8,24},{9,... | collective-permute-start | bytes 4325384 | tf_op jit(solution)/shard_map/ppermute | solution.py:470
  311.0 22.0 %collective-permute-start.21 = (bf16[5,512,512]{2,1,0:T(8,128)(2,1)S(1)}, bf16[5,512,512]{2,1,0:T(8,128)(2,1)S(1)}, u32[]{:S(2)}, u32[]{:S(2)}) collective-permute-start(bf16[5,512,512]{2,1,0:T(8,128)(2,1)S(1)} %copy-done.65), channel_id=1, source_target_pairs={{0,8},{1,9},{2,10},{3,11},{4,12},{5,13},{6,14},{7,15},{8,0},{9,1},... | collective-permute-start | bytes 7864328 | tf_op jit(solution)/shard_map/ppermute | solution.py:470
  315.7 17.1 %collective-permute-start.19 = (bf16[1,128,2816]{2,1,0:T(8,128)(2,1)S(1)}, bf16[1,128,2816]{2,1,0:T(8,128)(2,1)S(1)}, u32[]{:S(2)}, u32[]{:S(2)}) collective-permute-start(bf16[1,128,2816]{2,1,0:T(8,128)(2,1)S(1)} %dynamic-slice_bitcast_fusion.2), channel_id=1, source_target_pairs={{0,16},{1,17},{2,18},{3,19},{4,20},{5,21},{6,22},{7,23},{8,24},{9,... | collective-permute-start | bytes 2162696 | tf_op jit(solution)/shard_map/ppermute | solution.py:470
  316.2 16.9 %collective-permute-start.20 = (bf16[1,128,2816]{2,1,0:T(8,128)(2,1)S(1)}, bf16[1,128,2816]{2,1,0:T(8,128)(2,1)S(1)}, u32[]{:S(2)}, u32[]{:S(2)}) collective-permute-start(bf16[1,128,2816]{2,1,0:T(8,128)(2,1)S(1)} %bitcast.289), channel_id=1, source_target_pairs={{0,1},{1,0},{2,3},{3,2},{4,5},{5,4},{6,7},{7,6},{8,9},{9,8},{10,11... | collective-permute-start | bytes 2162696 | tf_op jit(solution)/shard_map/ppermute | solution.py:470
  337.5 31.8 %collective-permute-start.22 = (bf16[1,704,1024]{2,1,0:T(8,128)(2,1)}, bf16[1,704,1024]{2,1,0:T(8,128)(2,1)}, u32[]{:S(2)}, u32[]{:S(2)}) collective-permute-start(bf16[1,704,1024]{2,1,0:T(8,128)(2,1)} %dynamic-slice_bitcast_fusion), channel_id=1, source_target_pairs={{0,16},{1,17},{2,18},{3,19},{4,20},{5,21},{6,22},{7,23},{8,24},{9,... | collective-permute-start | bytes 4325384 | tf_op jit(solution)/shard_map/ppermute | solution.py:470
  339.0 28.7 %collective-permute-start.23 = (bf16[5,256,512]{2,1,0:T(8,128)(2,1)}, bf16[5,256,512]{2,1,0:T(8,128)(2,1)}, u32[]{:S(2)}, u32[]{:S(2)}) collective-permute-start(bf16[5,256,512]{2,1,0:T(8,128)(2,1)} %bitcast.77), channel_id=1, source_target_pairs={{0,1},{1,0},{2,3},{3,2},{4,5},{5,4},{6,7},{7,6},{8,9},{9,8},{10,11... | collective-permute-start | bytes 3932168 | tf_op jit(solution)/shard_map/ppermute | solution.py:470
  339.5 22.1 %collective-permute-start.24 = (bf16[2,64,2816]{2,1,0:T(8,128)(2,1)}, bf16[2,64,2816]{2,1,0:T(8,128)(2,1)}, u32[]{:S(2)}, u32[]{:S(2)}) collective-permute-start(bf16[2,64,2816]{2,1,0:T(8,128)(2,1)} %bitcast.81), channel_id=1, source_target_pairs={{0,2},{1,3},{2,0},{3,1},{4,6},{5,7},{6,4},{7,5},{8,10},{9,11},{10,... | collective-permute-start | bytes 2162696 | tf_op jit(solution)/shard_map/ppermute | solution.py:470
  377.4 21.1 %collective-permute-start.25 = (bf16[3,512,512]{2,1,0:T(8,128)(2,1)}, bf16[3,512,512]{2,1,0:T(8,128)(2,1)S(1)}, u32[]{:S(2)}, u32[]{:S(2)}) collective-permute-start(bf16[3,512,512]{2,1,0:T(8,128)(2,1)} %get-tuple-element.241), channel_id=1, source_target_pairs={{0,8},{1,9},{2,10},{3,11},{4,12},{5,13},{6,14},{7,15},{8,0},{9,1},... | collective-permute-start | bytes 4718600 | tf_op jit(solution)/shard_map/ppermute | solution.py:470
  377.4 21.0 %collective-permute-start.26 = (bf16[1,352,1024]{2,1,0:T(8,128)(2,1)}, bf16[1,352,1024]{2,1,0:T(8,128)(2,1)}, u32[]{:S(2)}, u32[]{:S(2)}) collective-permute-start(bf16[1,352,1024]{2,1,0:T(8,128)(2,1)} %bitcast.84), channel_id=1, source_target_pairs={{0,1},{1,0},{2,3},{3,2},{4,5},{5,4},{6,7},{7,6},{8,9},{9,8},{10,11... | collective-permute-start | bytes 2162696 | tf_op jit(solution)/shard_map/ppermute | solution.py:470
  378.9 19.5 %collective-permute-start.27 = (bf16[5,128,512]{2,1,0:T(8,128)(2,1)}, bf16[5,128,512]{2,1,0:T(8,128)(2,1)}, u32[]{:S(2)}, u32[]{:S(2)}) collective-permute-start(bf16[5,128,512]{2,1,0:T(8,128)(2,1)} %dynamic-slice_bitcast_fusion.3), channel_id=1, source_target_pairs={{0,16},{1,17},{2,18},{3,19},{4,20},{5,21},{6,22},{7,23},{8,24},{9,... | collective-permute-start | bytes 1966088 | tf_op jit(solution)/shard_map/ppermute | solution.py:470
  379.6 18.9 %collective-permute-start.28 = (bf16[2,32,2816]{2,1,0:T(8,128)(2,1)S(1)}, bf16[2,32,2816]{2,1,0:T(8,128)(2,1)}, u32[]{:S(2)}, u32[]{:S(2)}) collective-permute-start(bf16[2,32,2816]{2,1,0:T(8,128)(2,1)S(1)} %dynamic-slice_bitcast_fusion.4), channel_id=1, source_target_pairs={{0,4},{1,5},{2,6},{3,7},{4,0},{5,1},{6,2},{7,3},{8,12},{9,13},{10,... | collective-permute-start | bytes 1081352 | tf_op jit(solution)/shard_map/ppermute | solution.py:470
  402.2 20.4 %collective-permute-start.29 = (bf16[3,128,512]{2,1,0:T(8,128)(2,1)S(1)}, bf16[3,128,512]{2,1,0:T(8,128)(2,1)S(1)}, u32[]{:S(2)}, u32[]{:S(2)}) collective-permute-start(bf16[3,128,512]{2,1,0:T(8,128)(2,1)S(1)} %bitcast.292), channel_id=1, source_target_pairs={{0,16},{1,17},{2,18},{3,19},{4,20},{5,21},{6,22},{7,23},{8,24},{9,... | collective-permute-start | bytes 1179656 | tf_op jit(solution)/shard_map/ppermute | solution.py:470
  403.7 18.9 %collective-permute-start.30 = (bf16[3,128,512]{2,1,0:T(8,128)(2,1)S(1)}, bf16[3,128,512]{2,1,0:T(8,128)(2,1)S(1)}, u32[]{:S(2)}, u32[]{:S(2)}) collective-permute-start(bf16[3,128,512]{2,1,0:T(8,128)(2,1)S(1)} %bitcast.291), channel_id=1, source_target_pairs={{0,1},{1,0},{2,3},{3,2},{4,5},{5,4},{6,7},{7,6},{8,9},{9,8},{10,11... | collective-permute-start | bytes 1179656 | tf_op jit(solution)/shard_map/ppermute | solution.py:470
  404.3 18.3 %collective-permute-start.31 = (bf16[3,128,512]{2,1,0:T(8,128)(2,1)S(1)}, bf16[3,128,512]{2,1,0:T(8,128)(2,1)S(1)}, u32[]{:S(2)}, u32[]{:S(2)}) collective-permute-start(bf16[3,128,512]{2,1,0:T(8,128)(2,1)S(1)} %bitcast.290), channel_id=1, source_target_pairs={{0,17},{1,16},{2,19},{3,18},{4,21},{5,20},{6,23},{7,22},{8,25},{9,... | collective-permute-start | bytes 1179656 | tf_op jit(solution)/shard_map/ppermute | solution.py:470
  423.3 22.2 %collective-permute-start.37 = (bf16[1,88,1024]{2,1,0:T(8,128)(2,1)S(1)}, bf16[1,88,1024]{2,1,0:T(8,128)(2,1)S(1)}, u32[]{:S(2)}, u32[]{:S(2)}) collective-permute-start(bf16[1,88,1024]{2,1,0:T(8,128)(2,1)S(1)} %dynamic-slice_bitcast_fusion.5), channel_id=1, source_target_pairs={{0,4},{1,5},{2,6},{3,7},{4,0},{5,1},{6,2},{7,3},{8,12},{9,13},{10,... | collective-permute-start | bytes 540680 | tf_op jit(solution)/shard_map/ppermute | solution.py:470
  424.2 21.3 %collective-permute-start.38 = (bf16[5,32,512]{2,1,0:T(8,128)(2,1)S(1)}, bf16[5,32,512]{2,1,0:T(8,128)(2,1)S(1)}, u32[]{:S(2)}, u32[]{:S(2)}) collective-permute-start(bf16[5,32,512]{2,1,0:T(8,128)(2,1)S(1)} %dynamic-slice_bitcast_fusion.6), channel_id=1, source_target_pairs={{0,4},{1,5},{2,6},{3,7},{4,0},{5,1},{6,2},{7,3},{8,12},{9,13},{10,... | collective-permute-start | bytes 491528 | tf_op jit(solution)/shard_map/ppermute | solution.py:470
  426.6 19.0 %collective-permute-start.35 = (bf16[3,32,512]{2,1,0:T(8,128)(2,1)S(1)}, bf16[3,32,512]{2,1,0:T(8,128)(2,1)S(1)}, u32[]{:S(2)}, u32[]{:S(2)}) collective-permute-start(bf16[3,32,512]{2,1,0:T(8,128)(2,1)S(1)} %get-tuple-element.264), channel_id=1, source_target_pairs={{0,4},{1,5},{2,6},{3,7},{4,0},{5,1},{6,2},{7,3},{8,12},{9,13},{10,... | collective-permute-start | bytes 294920 | tf_op jit(solution)/shard_map/ppermute | solution.py:470
  (79 other events, 679.1 us)
Sparse Core Ops, SparseCore 0:
  11.5 81.3 all-gather.2
  96.2 98.8 all-gather.4
